TPU v7x, 256 devices: a whole 4x4x8 slice. The times are simulated.
256 devices in a mesh: sx: 32 (over x_hi, z, core), sy: 8 (over y, x_lo).
Axes of the slice: x: 4 (x_hi: 2, x_lo: 2; x = x_hi * 2 + x_lo), y: 4, z: 8, core: 2. Of those that a mesh axis runs over, the one named last changes fastest.
Arguments:
- object_field: float32 [2, 4096, 4096], P(None, 'sx', 'sy'), may hold values from -6 to 6
- probe_field: float32 [2, 256, 256], replicated, may hold values from -4.2 to 4.2
- amplitudes: float32 [32, 8, 2, 256, 256], P('sx', 'sy'), may hold values from 0 to 2
- centres: int32 [32, 8, 2, 2], P('sx', 'sy'), may hold values from 0 to 511, as said below
- counts: int32 [32, 8], P(None, 'sy'), may hold values from 1 to 2, as said below
Outputs:
- object_next: float32 [2, 4096, 4096], P(None, 'sx', 'sy')
Inputs may be any that keep to these rules, and one draw needn't show every extreme that they name: centres[s, t, k, 0] is below 128 and centres[s, t, k, 1] below 512; slots from counts[s, t] on are unused. A device's live positions are its first counts[s, t] slots; 2 is reached in every draw.
All inputs are finite; a program needn't handle non-finite values.
Results may differ from a plain program's by a relative error of at most 0.0003.
Values sent between devices are 32-bit elements; how exact they have to be, the bound alone decides.
A program may use at most 128 MiB of HBM per device.

v0:
```python
import math

import jax
import jax.numpy as jnp
from jax import lax
from jax.sharding import PartitionSpec as P

ITERS = 2


SMOOTH = 1.0
DAMPING = 1.0


def with_halo(cells, sides, width):
    for axis, dim in sides:
        count = lax.axis_size(axis)
        ends = count - 1
        head = lax.slice_in_dim(cells, 0, width, axis=dim)
        tail = lax.slice_in_dim(cells, cells.shape[dim] - width, cells.shape[dim], axis=dim)
        cells = jnp.concatenate(
            [
                lax.ppermute(tail, axis, [(i, (i + 1) % count) for i in range(ends)]),
                cells,
                lax.ppermute(head, axis, [((i + 1) % count, i) for i in range(ends)]),
            ],
            axis=dim,
        )
    return cells


def dft_tables(length):
    index_values = jnp.arange(length, dtype=jnp.int32)
    product_mod = index_values[:, None] * index_values[None, :] % length
    angles = product_mod.astype(jnp.float32) * (2.0 * math.pi / length)
    scaling = 1.0 / math.sqrt(length)
    return (jnp.cos(angles) * scaling, -jnp.sin(angles) * scaling)


def matmul_exact(left_side, right_side):
    return jnp.dot(left_side, right_side, precision=lax.Precision.HIGHEST)


def complex_left(table_real, table_imag, field_real, field_imag):
    out_real = matmul_exact(table_real, field_real) - matmul_exact(table_imag, field_imag)
    out_imag = matmul_exact(table_real, field_imag) + matmul_exact(table_imag, field_real)
    return (out_real, out_imag)


def complex_right(field_real, field_imag, table_real, table_imag):
    out_real = matmul_exact(field_real, table_real) - matmul_exact(field_imag, table_imag)
    out_imag = matmul_exact(field_real, table_imag) + matmul_exact(field_imag, table_real)
    return (out_real, out_imag)


def position_gradient(object_patch, probe_field, amplitude, table_real, table_imag):
    probe_real = probe_field[0]
    probe_imag = probe_field[1]
    exit_real = probe_real * object_patch[0] - probe_imag * object_patch[1]
    exit_imag = probe_real * object_patch[1] + probe_imag * object_patch[0]
    half_real, half_imag = complex_left(table_real, table_imag, exit_real, exit_imag)
    far_real, far_imag = complex_right(half_real, half_imag, table_real, table_imag)
    factor = 1.0 - amplitude / jnp.sqrt(far_real * far_real + far_imag * far_imag + SMOOTH)
    miss_real = far_real * factor
    miss_imag = far_imag * factor
    back_real, back_imag = complex_left(table_real, -table_imag, miss_real, miss_imag)
    near_real, near_imag = complex_right(back_real, back_imag, table_real, -table_imag)
    return jnp.stack(
        [
            probe_real * near_real + probe_imag * near_imag,
            probe_real * near_imag - probe_imag * near_real,
        ]
    )


def add_patch(canvas, patch_values, corner_row, corner_col):
    zero_index = jnp.zeros((), jnp.int32)
    starts = (zero_index, corner_row, corner_col)
    present = lax.dynamic_slice(canvas, starts, patch_values.shape)
    return lax.dynamic_update_slice(canvas, present + patch_values, starts)


def fold_rows(extended, margin, length):
    middle_part = extended[:, 2 * margin : 2 * margin + length]
    upper_rim = extended[:, :margin]
    lower_rim = extended[:, extended.shape[1] - margin :]
    middle_part = middle_part.at[:, :margin].add(upper_rim)
    return middle_part.at[:, length - margin :].add(lower_rim)


def fold_cols(extended, margin, length):
    middle_part = extended[:, :, 2 * margin : 2 * margin + length]
    left_rim = extended[:, :, :margin]
    right_rim = extended[:, :, extended.shape[2] - margin :]
    middle_part = middle_part.at[:, :, :margin].add(left_rim)
    return middle_part.at[:, :, length - margin :].add(right_rim)


def settle(stacked, margin, block_rows, block_cols):
    full_ext = with_halo(stacked, (("sx", 1), ("sy", 2)), margin)
    return fold_cols(fold_rows(full_ext, margin, block_rows), margin, block_cols)


def local_pass(canvas, extended, spots, own_amps, probe_field, table_real, table_imag, upper_bound):
    size_probe = probe_field.shape[1]

    def local_step(slot_index, canvas_state):
        row_start = spots[slot_index, 0]
        col_start = spots[slot_index, 1]
        zero_index = jnp.zeros((), jnp.int32)
        object_patch = lax.dynamic_slice(
            extended, (zero_index, row_start, col_start), (2, size_probe, size_probe)
        )
        update = position_gradient(
            object_patch, probe_field, own_amps[slot_index], table_real, table_imag
        )
        return add_patch(canvas_state, update, row_start, col_start)

    return lax.fori_loop(0, upper_bound, local_step, canvas)


def on_device(object_field, probe_field, amplitudes, centres, counts):
    size_probe = probe_field.shape[1]
    margin = size_probe // 2
    block_rows = object_field.shape[1]
    block_cols = object_field.shape[2]
    table_real, table_imag = dft_tables(size_probe)
    spots = centres[0, 0]
    own_amps = amplitudes[0, 0]
    sx_size = lax.axis_size("sx")
    sx_index = lax.axis_index("sx")
    column_counts = counts[:, 0]
    sx_positions = jnp.arange(sx_size, dtype=jnp.int32)
    own_count = jnp.sum(jnp.where(sx_positions == sx_index, column_counts, 0))
    ext_shape = (block_rows + size_probe, block_cols + size_probe)
    spot_power = (probe_field[0] * probe_field[0] + probe_field[1] * probe_field[1])[None]

    def add_power(slot_index, canvas_state):
        return add_patch(canvas_state, spot_power, spots[slot_index, 0], spots[slot_index, 1])

    power_ext = lax.fori_loop(0, own_count, add_power, jnp.zeros((1,) + ext_shape, jnp.float32))
    current = object_field
    for sweep_index in range(ITERS):
        extended = with_halo(current, (("sx", 1), ("sy", 2)), margin)
        canvas = jnp.zeros((2,) + ext_shape, jnp.float32)
        canvas = local_pass(
            canvas, extended, spots, own_amps, probe_field, table_real, table_imag, own_count
        )
        if sweep_index == 0:
            settled = settle(
                jnp.concatenate([canvas, power_ext], axis=0), margin, block_rows, block_cols
            )
            illumination = settled[2]
            gradient = settled[0:2]
        else:
            gradient = settle(canvas, margin, block_rows, block_cols)
        current = current - gradient / (illumination + DAMPING)
    return current


def solution(mesh):
    return jax.shard_map(
        on_device,
        mesh=mesh,
        in_specs=(
            P(None, "sx", "sy"),
            P(),
            P("sx", "sy", None, None, None),
            P("sx", "sy", None, None),
            P(None, "sy"),
        ),
        out_specs=P(None, "sx", "sy"),
        check_vma=False,
    )
```

profile of v0, /device:TPU:4, one launch (start us, length us, event | category | flops | bytes accessed | tf_op | source)
XLA Modules:
  0.0 367.6 jit_solution(16354226319147389080)
XLA Ops:
  2.1 7.3 %collective-permute-start.1 = (f32[2,128,512]{2,1,0:T(8,128)}, f32[2,128,512]{2,1,0:T(8,128)S(1)}, u32[]{:S(2)}, u32[]{:S(2)}) collective-permute-start(f32[2,128,512]{2,1,0:T(8,128)} %param.35), channel_id=1, source_target_pairs={{8,0},{16,8},{24,16},{32,24},{40,32},{48,40},{56,48},{64,56},{72,6... | collective-permute-start | bytes 1572872 | tf_op jit(solution)/shard_map/ppermute | solution.py:25
  17.3 4.6 %collective-permute-start.2 = (f32[2,384,128]{2,1,0:T(8,128)}, f32[2,384,128]{2,1,0:T(8,128)}, u32[]{:S(2)}, u32[]{:S(2)}) collective-permute-start(f32[2,384,128]{2,1,0:T(8,128)} %get-tuple-element.608), channel_id=1, source_target_pairs={{0,1},{1,2},{2,3},{3,4},{4,5},{5,6},{6,7},{8,9},{9,10},{10,11},{11... | collective-permute-start | bytes 1179656 | tf_op jit(solution)/shard_map/ppermute | solution.py:23
  23.3 19.9 %while.48 = (s32[]{:T(128)}, f32[1,384,768]{2,1,0:T(8,128)S(1)}, s32[]{:T(128)}, s32[2,2]{1,0:T(2,128)S(1)}, f32[1,256,256]{2,1,0:T(8,128)S(1)}, /*index=5*/s32[...) while((s32[]{:T(128)}, f32[1,384,768]{2,1,0:T(8,128)S(1)}, s32[]{:T(128)}, s32[2,2]{1,0:T(2,128)S(1)}, ...), condition=%wide.region_4.5_spmd, body=%wide.region_3.4_spmd.sunk | while | flops 65547 | bytes 1310955 | solution.py:141
  28.5 4.4 %dynamic_update_slice.18 = f32[1,384,768]{2,1,0:T(8,128)S(1)} dynamic-update-slice(f32[1,384,768]{2,1,0:T(8,128)S(1)} %get-tuple-element.816, f32[1,256,256]{2,1,0:T(8,128)S(1)} %dynamic-slice_add_fusion.2, s32[]{:T(128)} %constant.291.clone.1..sunk, s32[]{:T(128)S(6)} %select_n.278, s32[]{:T(128)S(6)} %select_n.279) | dynamic-update-slice | bytes 524292 | tf_op jit(solution)/shard_map/while/body/dynamic_update_slice | solution.py:80
  38.0 4.6 %dynamic_update_slice.18 = f32[1,384,768]{2,1,0:T(8,128)S(1)} dynamic-update-slice(f32[1,384,768]{2,1,0:T(8,128)S(1)} %get-tuple-element.816, f32[1,256,256]{2,1,0:T(8,128)S(1)} %dynamic-slice_add_fusion.2, s32[]{:T(128)} %constant.291.clone.1..sunk, s32[]{:T(128)S(6)} %select_n.278, s32[]{:T(128)S(6)} %select_n.279) | dynamic-update-slice | bytes 524292 | tf_op jit(solution)/shard_map/while/body/dynamic_update_slice | solution.py:80
  48.0 81.9 %while.49 = (s32[]{:T(128)}, f32[2,384,768]{2,1,0:T(8,128)S(1)}, s32[]{:T(128)}, s32[2,2]{1,0:T(2,128)S(1)}, f32[2,256,256]{2,1,0:T(8,128)S(1)}, /*index=5*/f32[...) while((s32[]{:T(128)}, f32[2,384,768]{2,1,0:T(8,128)S(1)}, ...), condition=%wide.region_2.3_spmd.clone.clone, body=%wide.region_1.2_spmd.clone.clone.sunk | while | flops 3239837696 | bytes 16515359 | solution.py:119
  79.4 8.9 %dynamic_update_slice.19 = f32[2,384,768]{2,1,0:T(8,128)S(1)} dynamic-update-slice(f32[2,384,768]{2,1,0:T(8,128)S(1)} %get-tuple-element.780, f32[2,256,256]{2,1,0:T(8,128)S(1)} %maximum_add_fusion.6, s32[]{:T(128)} %constant.291.clone.1..sunk.1, s32[]{:T(128)S(6)} %select_n.297, s32[]{:T(128)S(6)} %select_n.298) | dynamic-update-slice | bytes 1048580 | tf_op jit(solution)/shard_map/while/body/dynamic_update_slice | solution.py:80
  119.7 9.3 %dynamic_update_slice.19 = f32[2,384,768]{2,1,0:T(8,128)S(1)} dynamic-update-slice(f32[2,384,768]{2,1,0:T(8,128)S(1)} %get-tuple-element.780, f32[2,256,256]{2,1,0:T(8,128)S(1)} %maximum_add_fusion.6, s32[]{:T(128)} %constant.291.clone.1..sunk.1, s32[]{:T(128)S(6)} %select_n.297, s32[]{:T(128)S(6)} %select_n.298) | dynamic-update-slice | bytes 1048580 | tf_op jit(solution)/shard_map/while/body/dynamic_update_slice | solution.py:80
  133.5 7.3 %collective-permute-start.5 = (f32[3,128,768]{2,1,0:T(8,128)S(1)}, f32[3,128,768]{2,1,0:T(8,128)S(1)}, u32[]{:S(2)}, u32[]{:S(2)}) collective-permute-start(f32[3,128,768]{2,1,0:T(8,128)S(1)} %get-tuple-element.603), channel_id=1, source_target_pairs={{8,0},{16,8},{24,16},{32,24},{40,32},{48,40},{56,48},{64,56},{72,6... | collective-permute-start | bytes 3538952 | tf_op jit(solution)/shard_map/ppermute | solution.py:25
  140.7 12.0 %collective-permute-done.4 = f32[3,128,768]{2,1,0:T(8,128)S(1)} collective-permute-done((f32[3,128,768]{2,1,0:T(8,128)S(1)}, f32[3,128,768]{2,1,0:T(8,128)S(1)}, u32[]{:S(2)}, u32[]{:S(2)}) %collective-permute-start.4) | collective-permute-done | bytes 1179680 | tf_op jit(solution)/shard_map/ppermute | solution.py:23
  154.6 4.5 %collective-permute-start.6 = (f32[3,640,128]{2,1,0:T(8,128)S(1)}, f32[3,640,128]{2,1,0:T(8,128)S(1)}, u32[]{:S(2)}, u32[]{:S(2)}) collective-permute-start(f32[3,640,128]{2,1,0:T(8,128)S(1)} %get-tuple-element.598), channel_id=1, source_target_pairs={{0,1},{1,2},{2,3},{3,4},{4,5},{5,6},{6,7},{8,9},{9,10},{10,11},{11... | collective-permute-start | bytes 2949128 | tf_op jit(solution)/shard_map/ppermute | solution.py:23
  160.4 11.7 %collective-permute-done.6 = f32[3,640,128]{2,1,0:T(8,128)S(1)} collective-permute-done((f32[3,640,128]{2,1,0:T(8,128)S(1)}, f32[3,640,128]{2,1,0:T(8,128)S(1)}, u32[]{:S(2)}, u32[]{:S(2)}) %collective-permute-start.6) | collective-permute-done | bytes 983072 | tf_op jit(solution)/shard_map/ppermute | solution.py:23
  172.2 25.8 %collective-permute-done.7 = f32[3,640,128]{2,1,0:T(8,128)S(1)} collective-permute-done((f32[3,640,128]{2,1,0:T(8,128)S(1)}, f32[3,640,128]{2,1,0:T(8,128)S(1)}, u32[]{:S(2)}, u32[]{:S(2)}) %collective-permute-start.7) | collective-permute-done | bytes 983072 | tf_op jit(solution)/shard_map/ppermute | solution.py:25
  202.7 7.3 %collective-permute-start.9 = (f32[2,128,512]{2,1,0:T(8,128)S(1)}, f32[2,128,512]{2,1,0:T(8,128)S(1)}, u32[]{:S(2)}, u32[]{:S(2)}) collective-permute-start(f32[2,128,512]{2,1,0:T(8,128)S(1)} %fusion.228), channel_id=1, source_target_pairs={{8,0},{16,8},{24,16},{32,24},{40,32},{48,40},{56,48},{64,56},{72,6... | collective-permute-start | bytes 1572872 | tf_op jit(solution)/shard_map/ppermute | solution.py:25
  209.9 5.0 %collective-permute-done.8 = f32[2,128,512]{2,1,0:T(8,128)S(1)} collective-permute-done((f32[2,128,512]{2,1,0:T(8,128)S(1)}, f32[2,128,512]{2,1,0:T(8,128)S(1)}, u32[]{:S(2)}, u32[]{:S(2)}) %collective-permute-start.8) | collective-permute-done | bytes 524320 | tf_op jit(solution)/shard_map/ppermute | solution.py:23
  221.0 4.3 %collective-permute-done.10 = f32[2,384,128]{2,1,0:T(8,128)S(1)} collective-permute-done((f32[2,384,128]{2,1,0:T(8,128)}, f32[2,384,128]{2,1,0:T(8,128)S(1)}, u32[]{:S(2)}, u32[]{:S(2)}) %collective-permute-start.10) | collective-permute-done | bytes 393248 | tf_op jit(solution)/shard_map/ppermute | solution.py:23
  225.2 9.1 %collective-permute-done.11 = f32[2,384,128]{2,1,0:T(8,128)S(1)} collective-permute-done((f32[2,384,128]{2,1,0:T(8,128)S(1)}, f32[2,384,128]{2,1,0:T(8,128)S(1)}, u32[]{:S(2)}, u32[]{:S(2)}) %collective-permute-start.11) | collective-permute-done | bytes 393248 | tf_op jit(solution)/shard_map/ppermute | solution.py:25
  236.1 81.0 %while.50 = (s32[]{:T(128)}, f32[2,384,768]{2,1,0:T(8,128)S(1)}, s32[]{:T(128)}, s32[2,2]{1,0:T(2,128)S(1)}, f32[2,256,256]{2,1,0:T(8,128)S(1)}, /*index=5*/f32[...) while((s32[]{:T(128)}, f32[2,384,768]{2,1,0:T(8,128)S(1)}, ...), condition=%wide.region_6.7_spmd.clone.clone, body=%wide.region_5.6_spmd.clone.clone.sunk | while | flops 3239837696 | bytes 16515359 | solution.py:119
  267.3 8.9 %dynamic_update_slice.20 = f32[2,384,768]{2,1,0:T(8,128)S(1)} dynamic-update-slice(f32[2,384,768]{2,1,0:T(8,128)S(1)} %get-tuple-element.849, f32[2,256,256]{2,1,0:T(8,128)S(1)} %maximum_add_fusion.7, s32[]{:T(128)} %constant.291.clone.1..sunk.2, s32[]{:T(128)S(6)} %select_n.316, s32[]{:T(128)S(6)} %select_n.317) | dynamic-update-slice | bytes 1048580 | tf_op jit(solution)/shard_map/while/body/dynamic_update_slice | solution.py:80
  307.1 9.3 %dynamic_update_slice.20 = f32[2,384,768]{2,1,0:T(8,128)S(1)} dynamic-update-slice(f32[2,384,768]{2,1,0:T(8,128)S(1)} %get-tuple-element.849, f32[2,256,256]{2,1,0:T(8,128)S(1)} %maximum_add_fusion.7, s32[]{:T(128)} %constant.291.clone.1..sunk.2, s32[]{:T(128)S(6)} %select_n.316, s32[]{:T(128)S(6)} %select_n.317) | dynamic-update-slice | bytes 1048580 | tf_op jit(solution)/shard_map/while/body/dynamic_update_slice | solution.py:80
  319.2 7.3 %collective-permute-start.13 = (f32[2,128,768]{2,1,0:T(8,128)S(1)}, f32[2,128,768]{2,1,0:T(8,128)S(1)}, u32[]{:S(2)}, u32[]{:S(2)}) collective-permute-start(f32[2,128,768]{2,1,0:T(8,128)S(1)} %get-tuple-element.604), channel_id=1, source_target_pairs={{8,0},{16,8},{24,16},{32,24},{40,32},{48,40},{56,48},{64,56},{72,6... | collective-permute-start | bytes 2359304 | tf_op jit(solution)/shard_map/ppermute | solution.py:25
  326.5 7.8 %collective-permute-done.12 = f32[2,128,768]{2,1,0:T(8,128)S(1)} collective-permute-done((f32[2,128,768]{2,1,0:T(8,128)S(1)}, f32[2,128,768]{2,1,0:T(8,128)S(1)}, u32[]{:S(2)}, u32[]{:S(2)}) %collective-permute-start.12) | collective-permute-done | bytes 786464 | tf_op jit(solution)/shard_map/ppermute | solution.py:23
  339.4 6.7 %collective-permute-done.14 = f32[2,640,128]{2,1,0:T(8,128)S(1)} collective-permute-done((f32[2,640,128]{2,1,0:T(8,128)S(1)}, f32[2,640,128]{2,1,0:T(8,128)S(1)}, u32[]{:S(2)}, u32[]{:S(2)}) %collective-permute-start.14) | collective-permute-done | bytes 655392 | tf_op jit(solution)/shard_map/ppermute | solution.py:23
  346.1 18.9 %collective-permute-done.15 = f32[2,640,128]{2,1,0:T(8,128)S(1)} collective-permute-done((f32[2,640,128]{2,1,0:T(8,128)S(1)}, f32[2,640,128]{2,1,0:T(8,128)S(1)}, u32[]{:S(2)}, u32[]{:S(2)}) %collective-permute-start.15) | collective-permute-done | bytes 655392 | tf_op jit(solution)/shard_map/ppermute | solution.py:25
  (149 shorter events, 152.6 us)
Async XLA Ops:
  0.0 15.7 %copy-start.7 = (f32[2,128,512]{2,1,0:T(8,128)S(1)}, f32[2,128,512]{2,1,0:T(8,128)}, u32[]{:S(2)}) copy-start(f32[2,128,512]{2,1,0:T(8,128)} %param.35) | copy-start | bytes 1572868
  0.0 14.6 %collective-permute-start = (f32[2,128,512]{2,1,0:T(8,128)}, f32[2,128,512]{2,1,0:T(8,128)}, u32[]{:S(2)}, u32[]{:S(2)}) collective-permute-start(f32[2,128,512]{2,1,0:T(8,128)} %param.35), channel_id=1, source_target_pairs={{0,8},{8,16},{16,24},{24,32},{32,40},{40,48},{48,56},{56,64},{64,7... | collective-permute-start | bytes 1572872 | tf_op jit(solution)/shard_map/ppermute | solution.py:23
  2.1 14.3 %collective-permute-start.1 = (f32[2,128,512]{2,1,0:T(8,128)}, f32[2,128,512]{2,1,0:T(8,128)S(1)}, u32[]{:S(2)}, u32[]{:S(2)}) collective-permute-start(f32[2,128,512]{2,1,0:T(8,128)} %param.35), channel_id=1, source_target_pairs={{8,0},{16,8},{24,16},{32,24},{40,32},{48,40},{56,48},{64,56},{72,6... | collective-permute-start | bytes 1572872 | tf_op jit(solution)/shard_map/ppermute | solution.py:25
  16.4 7.0 %copy-start.9 = (s32[1,1,2,2]{3,2,1,0:T(2,128)S(1)}, s32[1,1,2,2]{3,2,1,0:T(2,128)}, u32[]{:S(2)}) copy-start(s32[1,1,2,2]{3,2,1,0:T(2,128)} %param.38) | copy-start | bytes 52
  17.3 26.0 %collective-permute-start.2 = (f32[2,384,128]{2,1,0:T(8,128)}, f32[2,384,128]{2,1,0:T(8,128)}, u32[]{:S(2)}, u32[]{:S(2)}) collective-permute-start(f32[2,384,128]{2,1,0:T(8,128)} %get-tuple-element.608), channel_id=1, source_target_pairs={{0,1},{1,2},{2,3},{3,4},{4,5},{5,6},{6,7},{8,9},{9,10},{10,11},{11... | collective-permute-start | bytes 1179656 | tf_op jit(solution)/shard_map/ppermute | solution.py:23
  21.9 21.3 %collective-permute-start.3 = (f32[2,384,128]{2,1,0:T(8,128)}, f32[2,384,128]{2,1,0:T(8,128)}, u32[]{:S(2)}, u32[]{:S(2)}) collective-permute-start(f32[2,384,128]{2,1,0:T(8,128)} %get-tuple-element.609), channel_id=1, source_target_pairs={{1,0},{2,1},{3,2},{4,3},{5,4},{6,5},{7,6},{9,8},{10,9},{11,10},{12... | collective-permute-start | bytes 1179656 | tf_op jit(solution)/shard_map/ppermute | solution.py:25
  129.9 1.3 copy-start.2
  131.5 21.2 %collective-permute-start.4 = (f32[3,128,768]{2,1,0:T(8,128)S(1)}, f32[3,128,768]{2,1,0:T(8,128)S(1)}, u32[]{:S(2)}, u32[]{:S(2)}) collective-permute-start(f32[3,128,768]{2,1,0:T(8,128)S(1)} %get-tuple-element.602), channel_id=1, source_target_pairs={{0,8},{8,16},{16,24},{24,32},{32,40},{40,48},{48,56},{56,64},{64,7... | collective-permute-start | bytes 3538952 | tf_op jit(solution)/shard_map/ppermute | solution.py:23
  133.5 21.0 %collective-permute-start.5 = (f32[3,128,768]{2,1,0:T(8,128)S(1)}, f32[3,128,768]{2,1,0:T(8,128)S(1)}, u32[]{:S(2)}, u32[]{:S(2)}) collective-permute-start(f32[3,128,768]{2,1,0:T(8,128)S(1)} %get-tuple-element.603), channel_id=1, source_target_pairs={{8,0},{16,8},{24,16},{32,24},{40,32},{48,40},{56,48},{64,56},{72,6... | collective-permute-start | bytes 3538952 | tf_op jit(solution)/shard_map/ppermute | solution.py:25
  154.6 17.6 %collective-permute-start.6 = (f32[3,640,128]{2,1,0:T(8,128)S(1)}, f32[3,640,128]{2,1,0:T(8,128)S(1)}, u32[]{:S(2)}, u32[]{:S(2)}) collective-permute-start(f32[3,640,128]{2,1,0:T(8,128)S(1)} %get-tuple-element.598), channel_id=1, source_target_pairs={{0,1},{1,2},{2,3},{3,4},{4,5},{5,6},{6,7},{8,9},{9,10},{10,11},{11... | collective-permute-start | bytes 2949128 | tf_op jit(solution)/shard_map/ppermute | solution.py:23
  159.1 38.9 %collective-permute-start.7 = (f32[3,640,128]{2,1,0:T(8,128)S(1)}, f32[3,640,128]{2,1,0:T(8,128)S(1)}, u32[]{:S(2)}, u32[]{:S(2)}) collective-permute-start(f32[3,640,128]{2,1,0:T(8,128)S(1)} %get-tuple-element.599), channel_id=1, source_target_pairs={{1,0},{2,1},{3,2},{4,3},{5,4},{6,5},{7,6},{9,8},{10,9},{11,10},{12... | collective-permute-start | bytes 2949128 | tf_op jit(solution)/shard_map/ppermute | solution.py:25
  199.6 1.0 copy-start.8
  200.6 16.9 %copy-start.5 = (f32[128,512]{1,0:T(8,128)}, f32[128,512]{1,0:T(8,128)S(1)}, u32[]{:S(2)}) copy-start(f32[128,512]{1,0:T(8,128)S(1)} %fusion.229) | copy-start | bytes 786436
  200.7 33.6 %copy-start.3 = (f32[2,128,512]{2,1,0:T(8,128)}, f32[2,128,512]{2,1,0:T(8,128)S(1)}, u32[]{:S(2)}) copy-start(f32[2,128,512]{2,1,0:T(8,128)S(1)} %fusion.228) | copy-start | bytes 1572868
  200.7 14.2 %collective-permute-start.8 = (f32[2,128,512]{2,1,0:T(8,128)S(1)}, f32[2,128,512]{2,1,0:T(8,128)S(1)}, u32[]{:S(2)}, u32[]{:S(2)}) collective-permute-start(f32[2,128,512]{2,1,0:T(8,128)S(1)} %fusion.228), channel_id=1, source_target_pairs={{0,8},{8,16},{16,24},{24,32},{32,40},{40,48},{48,56},{56,64},{64,7... | collective-permute-start | bytes 1572872 | tf_op jit(solution)/shard_map/ppermute | solution.py:23
  202.7 14.0 %collective-permute-start.9 = (f32[2,128,512]{2,1,0:T(8,128)S(1)}, f32[2,128,512]{2,1,0:T(8,128)S(1)}, u32[]{:S(2)}, u32[]{:S(2)}) collective-permute-start(f32[2,128,512]{2,1,0:T(8,128)S(1)} %fusion.228), channel_id=1, source_target_pairs={{8,0},{16,8},{24,16},{32,24},{40,32},{48,40},{56,48},{64,56},{72,6... | collective-permute-start | bytes 1572872 | tf_op jit(solution)/shard_map/ppermute | solution.py:25
  217.5 7.8 %collective-permute-start.10 = (f32[2,384,128]{2,1,0:T(8,128)}, f32[2,384,128]{2,1,0:T(8,128)S(1)}, u32[]{:S(2)}, u32[]{:S(2)}) collective-permute-start(f32[2,384,128]{2,1,0:T(8,128)} %get-tuple-element.606), channel_id=1, source_target_pairs={{0,1},{1,2},{2,3},{3,4},{4,5},{5,6},{6,7},{8,9},{9,10},{10,11},{11... | collective-permute-start | bytes 1179656 | tf_op jit(solution)/shard_map/ppermute | solution.py:23
  219.7 14.7 %collective-permute-start.11 = (f32[2,384,128]{2,1,0:T(8,128)S(1)}, f32[2,384,128]{2,1,0:T(8,128)S(1)}, u32[]{:S(2)}, u32[]{:S(2)}) collective-permute-start(f32[2,384,128]{2,1,0:T(8,128)S(1)} %get-tuple-element.607), channel_id=1, source_target_pairs={{1,0},{2,1},{3,2},{4,3},{5,4},{6,5},{7,6},{9,8},{10,9},{11,10},{12... | collective-permute-start | bytes 1179656 | tf_op jit(solution)/shard_map/ppermute | solution.py:25
  317.3 17.0 %collective-permute-start.12 = (f32[2,128,768]{2,1,0:T(8,128)S(1)}, f32[2,128,768]{2,1,0:T(8,128)S(1)}, u32[]{:S(2)}, u32[]{:S(2)}) collective-permute-start(f32[2,128,768]{2,1,0:T(8,128)S(1)} %get-tuple-element.605), channel_id=1, source_target_pairs={{0,8},{8,16},{16,24},{24,32},{32,40},{40,48},{48,56},{56,64},{64,7... | collective-permute-start | bytes 2359304 | tf_op jit(solution)/shard_map/ppermute | solution.py:23
  319.2 16.8 %collective-permute-start.13 = (f32[2,128,768]{2,1,0:T(8,128)S(1)}, f32[2,128,768]{2,1,0:T(8,128)S(1)}, u32[]{:S(2)}, u32[]{:S(2)}) collective-permute-start(f32[2,128,768]{2,1,0:T(8,128)S(1)} %get-tuple-element.604), channel_id=1, source_target_pairs={{8,0},{16,8},{24,16},{32,24},{40,32},{48,40},{56,48},{64,56},{72,6... | collective-permute-start | bytes 2359304 | tf_op jit(solution)/shard_map/ppermute | solution.py:25
  336.2 10.0 %collective-permute-start.14 = (f32[2,640,128]{2,1,0:T(8,128)S(1)}, f32[2,640,128]{2,1,0:T(8,128)S(1)}, u32[]{:S(2)}, u32[]{:S(2)}) collective-permute-start(f32[2,640,128]{2,1,0:T(8,128)S(1)} %get-tuple-element.600), channel_id=1, source_target_pairs={{0,1},{1,2},{2,3},{3,4},{4,5},{5,6},{6,7},{8,9},{9,10},{10,11},{11... | collective-permute-start | bytes 1966088 | tf_op jit(solution)/shard_map/ppermute | solution.py:23
  338.1 27.0 %collective-permute-start.15 = (f32[2,640,128]{2,1,0:T(8,128)S(1)}, f32[2,640,128]{2,1,0:T(8,128)S(1)}, u32[]{:S(2)}, u32[]{:S(2)}) collective-permute-start(f32[2,640,128]{2,1,0:T(8,128)S(1)} %get-tuple-element.601), channel_id=1, source_target_pairs={{1,0},{2,1},{3,2},{4,3},{5,4},{6,5},{7,6},{9,8},{10,9},{11,10},{12... | collective-permute-start | bytes 1966088 | tf_op jit(solution)/shard_map/ppermute | solution.py:25
  365.3 1.0 copy-start.4
  365.3 1.1 copy-start.6
  (2 other events, 2.1 us)
where the time goes:
time: 369 us; the launch traced here: 368 us
  waiting for transfers between devices  110 us (30%)
  matrix products  98.1 us (27%)
  local copies, waits for them, and re-layouts  57.4 us (16%)
  starting transfers between devices  55.3 us (15%)
  loops' own time  29.3 us (8%)
  other arithmetic  17 us (5%)
    dot_general x64, matrix products, matmul_exact(): return jnp.dot(left_side, right_side, precision=lax.Precision.HIGHEST)  98.1 us
    ppermute x8, waiting for transfers between devices, with_halo(): lax.ppermute(head, axis, [((i + 1) % count, i) for i in range(ends)])  59.4 us
    ppermute x8, waiting for transfers between devices, with_halo(): lax.ppermute(tail, axis, [(i, (i + 1) % count) for i in range(ends)])  50.5 us
    dynamic_update_slice x6, local copies, waits for them, and re-layouts, add_patch(): return lax.dynamic_update_slice(canvas, present + patch_values, starts)  45.4 us
    ppermute x8, starting transfers between devices, with_halo(): lax.ppermute(head, axis, [((i + 1) % count, i) for i in range(ends)])  34.2 us
    ppermute x8, starting transfers between devices, with_halo(): lax.ppermute(tail, axis, [(i, (i + 1) % count) for i in range(ends)])  21.1 us
    another operation x2, loops' own time, local_pass(): return lax.fori_loop(0, upper_bound, local_step, canvas)  19.9 us
    another operation x1, loops' own time, on_device(): lax.fori_loop(0, own_count, add_power, jnp.zeros((1,) + ext_shape, jnp.fl...  9.35 us
  transfers between devices with their start and end apart: 16, of which 14 were waited for; matrix products, arithmetic and copies ran while one was open for 4% of the time, Pallas kernels for 0%

commit v1 on v0

--- a/solution.py
+++ b/solution.py
@@ -4,6 +4,8 @@
 import jax.numpy as jnp
 from jax import lax
 from jax.sharding import PartitionSpec as P
+from jax.experimental import pallas as pl
+from jax.experimental.pallas import tpu as pltpu
 
 ITERS = 2
 
@@ -119,12 +121,87 @@
     return lax.fori_loop(0, upper_bound, local_step, canvas)
 
 
+def dot_exact(left_side, right_side):
+    return jnp.dot(
+        left_side, right_side, precision=lax.Precision.HIGHEST, preferred_element_type=jnp.float32
+    )
+
+
+def gradient_kernel(spots_ref, count_ref, ext_ref, probe_ref, amps_ref, fr_ref, fi_ref, out_ref):
+    size = probe_ref.shape[1]
+    lanes = 128
+    sublanes = 8
+    wide = size + lanes
+    tall = size + sublanes
+    out_ref[...] = jnp.zeros(out_ref.shape, jnp.float32)
+    with_power = out_ref.shape[0] > 2
+    for slot in range(amps_ref.shape[0]):
+
+        @pl.when(slot < count_ref[0])
+        def _():
+            row = spots_ref[slot, 0]
+            col = spots_ref[slot, 1]
+            row_base = pl.multiple_of((row // sublanes) * sublanes, sublanes)
+            col_base = pl.multiple_of((col // lanes) * lanes, lanes)
+            row_shift = row % sublanes
+            col_shift = col % lanes
+            rows = pl.ds(row_base, tall)
+            cols = pl.ds(col_base, wide)
+
+            def take(channel):
+                block = ext_ref[channel, rows, cols]
+                block = pltpu.roll(block, (tall - row_shift) % tall, 0)
+                return pltpu.roll(block, (wide - col_shift) % wide, 1)[:size, :size]
+
+            def put(channel, values):
+                block = jnp.concatenate([values, jnp.zeros((size, lanes), jnp.float32)], axis=1)
+                block = jnp.concatenate([block, jnp.zeros((sublanes, wide), jnp.float32)], axis=0)
+                block = pltpu.roll(pltpu.roll(block, col_shift, 1), row_shift, 0)
+                out_ref[channel, rows, cols] += block
+
+            probe_real = probe_ref[0]
+            probe_imag = probe_ref[1]
+            table_real = fr_ref[...]
+            table_imag = fi_ref[...]
+            obj_real = take(0)
+            obj_imag = take(1)
+            exit_real = probe_real * obj_real - probe_imag * obj_imag
+            exit_imag = probe_real * obj_imag + probe_imag * obj_real
+            half_real = dot_exact(table_real, exit_real) - dot_exact(table_imag, exit_imag)
+            half_imag = dot_exact(table_real, exit_imag) + dot_exact(table_imag, exit_real)
+            far_real = dot_exact(half_real, table_real) - dot_exact(half_imag, table_imag)
+            far_imag = dot_exact(half_real, table_imag) + dot_exact(half_imag, table_real)
+            factor = 1.0 - amps_ref[slot] / jnp.sqrt(far_real * far_real + far_imag * far_imag + SMOOTH)
+            miss_real = far_real * factor
+            miss_imag = far_imag * factor
+            back_real = dot_exact(table_real, miss_real) + dot_exact(table_imag, miss_imag)
+            back_imag = dot_exact(table_real, miss_imag) - dot_exact(table_imag, miss_real)
+            near_real = dot_exact(back_real, table_real) + dot_exact(back_imag, table_imag)
+            near_imag = dot_exact(back_imag, table_real) - dot_exact(back_real, table_imag)
+            put(0, probe_real * near_real + probe_imag * near_imag)
+            put(1, probe_real * near_imag - probe_imag * near_real)
+            if with_power:
+                put(2, probe_real * probe_real + probe_imag * probe_imag)
+
+
+def gradient_canvas(channels, ext_shape, spots, count, extended, probe_field, own_amps, tables):
+    vmem = pl.BlockSpec(memory_space=pltpu.VMEM)
+    smem = pl.BlockSpec(memory_space=pltpu.SMEM)
+    return pl.pallas_call(
+        gradient_kernel,
+        out_shape=jax.ShapeDtypeStruct((channels,) + ext_shape, jnp.float32),
+        in_specs=[smem, smem, vmem, vmem, vmem, vmem, vmem],
+        out_specs=vmem,
+        compiler_params=pltpu.CompilerParams(vmem_limit_bytes=60 * 1024 * 1024),
+    )(spots, count.reshape(1), extended, probe_field, own_amps, tables[0], tables[1])
+
+
 def on_device(object_field, probe_field, amplitudes, centres, counts):
     size_probe = probe_field.shape[1]
     margin = size_probe // 2
     block_rows = object_field.shape[1]
     block_cols = object_field.shape[2]
-    table_real, table_imag = dft_tables(size_probe)
+    tables = dft_tables(size_probe)
     spots = centres[0, 0]
     own_amps = amplitudes[0, 0]
     sx_size = lax.axis_size("sx")
@@ -133,27 +210,17 @@
     sx_positions = jnp.arange(sx_size, dtype=jnp.int32)
     own_count = jnp.sum(jnp.where(sx_positions == sx_index, column_counts, 0))
     ext_shape = (block_rows + size_probe, block_cols + size_probe)
-    spot_power = (probe_field[0] * probe_field[0] + probe_field[1] * probe_field[1])[None]
-
-    def add_power(slot_index, canvas_state):
-        return add_patch(canvas_state, spot_power, spots[slot_index, 0], spots[slot_index, 1])
-
-    power_ext = lax.fori_loop(0, own_count, add_power, jnp.zeros((1,) + ext_shape, jnp.float32))
     current = object_field
     for sweep_index in range(ITERS):
         extended = with_halo(current, (("sx", 1), ("sy", 2)), margin)
-        canvas = jnp.zeros((2,) + ext_shape, jnp.float32)
-        canvas = local_pass(
-            canvas, extended, spots, own_amps, probe_field, table_real, table_imag, own_count
-        )
+        channels = 3 if sweep_index == 0 else 2
+        canvas = gradient_canvas(
+            channels, ext_shape, spots, own_count, extended, probe_field, own_amps, tables
+        )
+        settled = settle(canvas, margin, block_rows, block_cols)
         if sweep_index == 0:
-            settled = settle(
-                jnp.concatenate([canvas, power_ext], axis=0), margin, block_rows, block_cols
-            )
             illumination = settled[2]
-            gradient = settled[0:2]
-        else:
-            gradient = settle(canvas, margin, block_rows, block_cols)
+        gradient = settled[0:2]
         current = current - gradient / (illumination + DAMPING)
     return current
 

time: 369 us -> 230 us (0.62)
  the two profiles are of different devices: /device:TPU:4 before, /device:TPU:225 now
where the time goes in v1:
time: 230 us; the launch traced here: 229 us
  waiting for transfers between devices  145 us (63%)
  starting transfers between devices  49.2 us (21%)
  Pallas kernels  20.7 us (9%)
  other arithmetic  8.84 us (4%)
  local copies, waits for them, and re-layouts  5.81 us (3%)
    ppermute x8, waiting for transfers between devices, with_halo(): lax.ppermute(head, axis, [((i + 1) % count, i) for i in range(ends)])  89.9 us
    ppermute x8, waiting for transfers between devices, with_halo(): lax.ppermute(tail, axis, [(i, (i + 1) % count) for i in range(ends)])  54.8 us
    ppermute x8, starting transfers between devices, with_halo(): lax.ppermute(tail, axis, [(i, (i + 1) % count) for i in range(ends)])  35.8 us
    pallas_call x2, Pallas kernels, gradient_canvas(): pl.pallas_call(gradient_kernel, out_shape=jax.ShapeDtypeStruct((channels,...  20.7 us
    ppermute x8, starting transfers between devices, with_halo(): lax.ppermute(head, axis, [((i + 1) % count, i) for i in range(ends)])  13.4 us
  transfers between devices with their start and end apart: 16, of which 16 were waited for; matrix products, arithmetic and copies ran while one was open for 2% of the time, Pallas kernels for 0%

profile of v1, /device:TPU:225, one launch (start us, length us, event | category | flops | bytes accessed | tf_op | source)
XLA Modules:
  0.0 229.4 jit_solution(17944934322685184643)
XLA Ops:
  0.0 2.0 collective-permute-start
  2.0 2.5 %collective-permute-start.1 = (f32[2,128,512]{2,1,0:T(8,128)}, f32[2,128,512]{2,1,0:T(8,128)S(1)}, u32[]{:S(2)}, u32[]{:S(2)}) collective-permute-start(f32[2,128,512]{2,1,0:T(8,128)} %param.29), channel_id=1, source_target_pairs={{8,0},{16,8},{24,16},{32,24},{40,32},{48,40},{56,48},{64,56},{72,6... | collective-permute-start | bytes 1572872 | tf_op jit(solution)/shard_map/ppermute | solution.py:27
  4.5 3.9 %collective-permute-done = f32[2,128,512]{2,1,0:T(8,128)S(1)} collective-permute-done((f32[2,128,512]{2,1,0:T(8,128)}, f32[2,128,512]{2,1,0:T(8,128)S(1)}, u32[]{:S(2)}, u32[]{:S(2)}) %collective-permute-start) | collective-permute-done | bytes 524320 | tf_op jit(solution)/shard_map/ppermute | solution.py:25
  9.6 6.9 %collective-permute-done.1 = f32[2,128,512]{2,1,0:T(8,128)S(1)} collective-permute-done((f32[2,128,512]{2,1,0:T(8,128)}, f32[2,128,512]{2,1,0:T(8,128)S(1)}, u32[]{:S(2)}, u32[]{:S(2)}) %collective-permute-start.1) | collective-permute-done | bytes 524320 | tf_op jit(solution)/shard_map/ppermute | solution.py:27
  16.6 3.0 %collective-permute-start.2 = (f32[2,384,128]{2,1,0:T(8,128)S(1)}, f32[2,384,128]{2,1,0:T(8,128)S(1)}, u32[]{:S(2)}, u32[]{:S(2)}) collective-permute-start(f32[2,384,128]{2,1,0:T(8,128)S(1)} %get-tuple-element.143), channel_id=1, source_target_pairs={{0,1},{1,2},{2,3},{3,4},{4,5},{5,6},{6,7},{8,9},{9,10},{10,11},{11... | collective-permute-start | bytes 1179656 | tf_op jit(solution)/shard_map/ppermute | solution.py:25
  23.4 2.5 %collective-permute-done.2 = f32[2,384,128]{2,1,0:T(8,128)S(1)} collective-permute-done((f32[2,384,128]{2,1,0:T(8,128)S(1)}, f32[2,384,128]{2,1,0:T(8,128)S(1)}, u32[]{:S(2)}, u32[]{:S(2)}) %collective-permute-start.2) | collective-permute-done | bytes 393248 | tf_op jit(solution)/shard_map/ppermute | solution.py:25
  25.8 10.1 %collective-permute-done.3 = f32[2,384,128]{2,1,0:T(8,128)S(1)} collective-permute-done((f32[2,384,128]{2,1,0:T(8,128)S(1)}, f32[2,384,128]{2,1,0:T(8,128)S(1)}, u32[]{:S(2)}, u32[]{:S(2)}) %collective-permute-start.3) | collective-permute-done | bytes 393248 | tf_op jit(solution)/shard_map/ppermute | solution.py:27
  37.6 10.5 %shard_map.75 = f32[3,384,768]{2,1,0:T(8,128)} custom-call(s32[2,2]{1,0:T(2,128)} %bitcast.9, s32[1]{0:T(128)} %bitcast.2.count_ref, f32[2,384,768]{2,1,0:T(8,128)} %pad_maximum_fusion.ext_ref, f32[2,256,256]{2,1,0:T(8,128)} %probe_ref.3, f32[2,256,256]{2,1,0:T(8,128)} %bitcast.7, f32[256,256]{1,0:T(8,128)} %get-tuple-element.146.fr_ref, ...), custom_call_target="tpu_custom_call" | custom-call | tf_op jit(solution)/shard_map/pallas_call | solution.py:190
  50.0 9.2 %collective-permute-start.4 = (f32[3,128,768]{2,1,0:T(8,128)S(1)}, f32[3,128,768]{2,1,0:T(8,128)S(1)}, u32[]{:S(2)}, u32[]{:S(2)}) collective-permute-start(f32[3,128,768]{2,1,0:T(8,128)S(1)} %get-tuple-element.137), channel_id=1, source_target_pairs={{0,8},{8,16},{16,24},{24,32},{32,40},{40,48},{48,56},{56,64},{64,7... | collective-permute-start | bytes 3538952 | tf_op jit(solution)/shard_map/ppermute | solution.py:25
  61.1 11.1 %collective-permute-done.4 = f32[3,128,768]{2,1,0:T(8,128)S(1)} collective-permute-done((f32[3,128,768]{2,1,0:T(8,128)S(1)}, f32[3,128,768]{2,1,0:T(8,128)S(1)}, u32[]{:S(2)}, u32[]{:S(2)}) %collective-permute-start.4) | collective-permute-done | bytes 1179680 | tf_op jit(solution)/shard_map/ppermute | solution.py:25
  72.2 8.3 %collective-permute-done.5 = f32[3,128,768]{2,1,0:T(8,128)S(1)} collective-permute-done((f32[3,128,768]{2,1,0:T(8,128)S(1)}, f32[3,128,768]{2,1,0:T(8,128)S(1)}, u32[]{:S(2)}, u32[]{:S(2)}) %collective-permute-start.5) | collective-permute-done | bytes 1179680 | tf_op jit(solution)/shard_map/ppermute | solution.py:27
  83.3 16.8 %collective-permute-done.6 = f32[3,640,128]{2,1,0:T(8,128)S(1)} collective-permute-done((f32[3,640,128]{2,1,0:T(8,128)S(1)}, f32[3,640,128]{2,1,0:T(8,128)S(1)}, u32[]{:S(2)}, u32[]{:S(2)}) %collective-permute-start.6) | collective-permute-done | bytes 983072 | tf_op jit(solution)/shard_map/ppermute | solution.py:25
  100.0 22.8 %collective-permute-done.7 = f32[3,640,128]{2,1,0:T(8,128)S(1)} collective-permute-done((f32[3,640,128]{2,1,0:T(8,128)S(1)}, f32[3,640,128]{2,1,0:T(8,128)S(1)}, u32[]{:S(2)}, u32[]{:S(2)}) %collective-permute-start.7) | collective-permute-done | bytes 983072 | tf_op jit(solution)/shard_map/ppermute | solution.py:27
  127.5 7.3 %collective-permute-start.8 = (f32[2,128,512]{2,1,0:T(8,128)S(1)}, f32[2,128,512]{2,1,0:T(8,128)S(1)}, u32[]{:S(2)}, u32[]{:S(2)}) collective-permute-start(f32[2,128,512]{2,1,0:T(8,128)S(1)} %fusion.2), channel_id=1, source_target_pairs={{0,8},{8,16},{16,24},{24,32},{32,40},{40,48},{48,56},{56,64},{64,7... | collective-permute-start | bytes 1572872 | tf_op jit(solution)/shard_map/ppermute | solution.py:25
  134.8 5.0 %collective-permute-done.9 = f32[2,128,512]{2,1,0:T(8,128)S(1)} collective-permute-done((f32[2,128,512]{2,1,0:T(8,128)S(1)}, f32[2,128,512]{2,1,0:T(8,128)S(1)}, u32[]{:S(2)}, u32[]{:S(2)}) %collective-permute-start.9) | collective-permute-done | bytes 524320 | tf_op jit(solution)/shard_map/ppermute | solution.py:27
  141.0 3.1 %collective-permute-start.10 = (f32[2,384,128]{2,1,0:T(8,128)S(1)}, f32[2,384,128]{2,1,0:T(8,128)S(1)}, u32[]{:S(2)}, u32[]{:S(2)}) collective-permute-start(f32[2,384,128]{2,1,0:T(8,128)S(1)} %get-tuple-element.141), channel_id=1, source_target_pairs={{0,1},{1,2},{2,3},{3,4},{4,5},{5,6},{6,7},{8,9},{9,10},{10,11},{11... | collective-permute-start | bytes 1179656 | tf_op jit(solution)/shard_map/ppermute | solution.py:25
  145.4 6.2 %collective-permute-done.10 = f32[2,384,128]{2,1,0:T(8,128)S(1)} collective-permute-done((f32[2,384,128]{2,1,0:T(8,128)S(1)}, f32[2,384,128]{2,1,0:T(8,128)S(1)}, u32[]{:S(2)}, u32[]{:S(2)}) %collective-permute-start.10) | collective-permute-done | bytes 393248 | tf_op jit(solution)/shard_map/ppermute | solution.py:25
  151.6 8.6 %collective-permute-done.11 = f32[2,384,128]{2,1,0:T(8,128)S(1)} collective-permute-done((f32[2,384,128]{2,1,0:T(8,128)S(1)}, f32[2,384,128]{2,1,0:T(8,128)S(1)}, u32[]{:S(2)}, u32[]{:S(2)}) %collective-permute-start.11) | collective-permute-done | bytes 393248 | tf_op jit(solution)/shard_map/ppermute | solution.py:27
  161.9 10.2 %shard_map.76 = f32[2,384,768]{2,1,0:T(8,128)} custom-call(s32[2,2]{1,0:T(2,128)} %bitcast.10, s32[1]{0:T(128)} %bitcast.2.count_ref, f32[2,384,768]{2,1,0:T(8,128)} %pad_maximum_fusion.1.ext_ref, f32[2,256,256]{2,1,0:T(8,128)} %probe_ref.3, f32[2,256,256]{2,1,0:T(8,128)} %bitcast.8, f32[256,256]{1,0:T(8,128)} %get-tuple-element.146.fr_ref, ...), custom_call_target="tpu_custom_call" | custom-call | tf_op jit(solution)/shard_map/pallas_call | solution.py:190
  173.7 8.4 %collective-permute-start.12 = (f32[2,128,768]{2,1,0:T(8,128)S(1)}, f32[2,128,768]{2,1,0:T(8,128)S(1)}, u32[]{:S(2)}, u32[]{:S(2)}) collective-permute-start(f32[2,128,768]{2,1,0:T(8,128)S(1)} %get-tuple-element.139), channel_id=1, source_target_pairs={{0,8},{8,16},{16,24},{24,32},{32,40},{40,48},{48,56},{56,64},{64,7... | collective-permute-start | bytes 2359304 | tf_op jit(solution)/shard_map/ppermute | solution.py:25
  184.0 7.0 %collective-permute-done.12 = f32[2,128,768]{2,1,0:T(8,128)S(1)} collective-permute-done((f32[2,128,768]{2,1,0:T(8,128)S(1)}, f32[2,128,768]{2,1,0:T(8,128)S(1)}, u32[]{:S(2)}, u32[]{:S(2)}) %collective-permute-start.12) | collective-permute-done | bytes 786464 | tf_op jit(solution)/shard_map/ppermute | solution.py:25
  191.1 8.1 %collective-permute-done.13 = f32[2,128,768]{2,1,0:T(8,128)S(1)} collective-permute-done((f32[2,128,768]{2,1,0:T(8,128)S(1)}, f32[2,128,768]{2,1,0:T(8,128)S(1)}, u32[]{:S(2)}, u32[]{:S(2)}) %collective-permute-start.13) | collective-permute-done | bytes 786464 | tf_op jit(solution)/shard_map/ppermute | solution.py:27
  201.9 6.2 %collective-permute-done.14 = f32[2,640,128]{2,1,0:T(8,128)S(1)} collective-permute-done((f32[2,640,128]{2,1,0:T(8,128)S(1)}, f32[2,640,128]{2,1,0:T(8,128)S(1)}, u32[]{:S(2)}, u32[]{:S(2)}) %collective-permute-start.14) | collective-permute-done | bytes 655392 | tf_op jit(solution)/shard_map/ppermute | solution.py:25
  208.0 20.1 %collective-permute-done.15 = f32[2,640,128]{2,1,0:T(8,128)S(1)} collective-permute-done((f32[2,640,128]{2,1,0:T(8,128)S(1)}, f32[2,640,128]{2,1,0:T(8,128)S(1)}, u32[]{:S(2)}, u32[]{:S(2)}) %collective-permute-start.15) | collective-permute-done | bytes 655392 | tf_op jit(solution)/shard_map/ppermute | solution.py:27
  (42 shorter events, 29.4 us)
Async XLA Ops:
  0.0 8.4 %collective-permute-start = (f32[2,128,512]{2,1,0:T(8,128)}, f32[2,128,512]{2,1,0:T(8,128)S(1)}, u32[]{:S(2)}, u32[]{:S(2)}) collective-permute-start(f32[2,128,512]{2,1,0:T(8,128)} %param.29), channel_id=1, source_target_pairs={{0,8},{8,16},{16,24},{24,32},{32,40},{40,48},{48,56},{56,64},{64,7... | collective-permute-start | bytes 1572872 | tf_op jit(solution)/shard_map/ppermute | solution.py:25
  2.0 14.4 %collective-permute-start.1 = (f32[2,128,512]{2,1,0:T(8,128)}, f32[2,128,512]{2,1,0:T(8,128)S(1)}, u32[]{:S(2)}, u32[]{:S(2)}) collective-permute-start(f32[2,128,512]{2,1,0:T(8,128)} %param.29), channel_id=1, source_target_pairs={{8,0},{16,8},{24,16},{32,24},{40,32},{48,40},{56,48},{64,56},{72,6... | collective-permute-start | bytes 1572872 | tf_op jit(solution)/shard_map/ppermute | solution.py:27
  9.6 11.3 %copy-start.3 = (s32[32,1]{0,1:T(1,128)S(1)}, s32[32,1]{0,1:T(1,128)}, u32[]{:S(2)}) copy-start(s32[32,1]{0,1:T(1,128)} %param.33) | copy-start | bytes 388
  16.6 9.3 %collective-permute-start.2 = (f32[2,384,128]{2,1,0:T(8,128)S(1)}, f32[2,384,128]{2,1,0:T(8,128)S(1)}, u32[]{:S(2)}, u32[]{:S(2)}) collective-permute-start(f32[2,384,128]{2,1,0:T(8,128)S(1)} %get-tuple-element.143), channel_id=1, source_target_pairs={{0,1},{1,2},{2,3},{3,4},{4,5},{5,6},{6,7},{8,9},{9,10},{10,11},{11... | collective-permute-start | bytes 1179656 | tf_op jit(solution)/shard_map/ppermute | solution.py:25
  19.6 16.4 %collective-permute-start.3 = (f32[2,384,128]{2,1,0:T(8,128)S(1)}, f32[2,384,128]{2,1,0:T(8,128)S(1)}, u32[]{:S(2)}, u32[]{:S(2)}) collective-permute-start(f32[2,384,128]{2,1,0:T(8,128)S(1)} %get-tuple-element.144), channel_id=1, source_target_pairs={{1,0},{2,1},{3,2},{4,3},{5,4},{6,5},{7,6},{9,8},{10,9},{11,10},{12... | collective-permute-start | bytes 1179656 | tf_op jit(solution)/shard_map/ppermute | solution.py:27
  48.1 32.4 %copy-start = (f32[3,384,768]{2,1,0:T(8,128)S(1)}, f32[3,384,768]{2,1,0:T(8,128)}, u32[]{:S(2)}) copy-start(f32[3,384,768]{2,1,0:T(8,128)} %shard_map.75) | copy-start | bytes 10616836
  50.0 22.2 %collective-permute-start.4 = (f32[3,128,768]{2,1,0:T(8,128)S(1)}, f32[3,128,768]{2,1,0:T(8,128)S(1)}, u32[]{:S(2)}, u32[]{:S(2)}) collective-permute-start(f32[3,128,768]{2,1,0:T(8,128)S(1)} %get-tuple-element.137), channel_id=1, source_target_pairs={{0,8},{8,16},{16,24},{24,32},{32,40},{40,48},{48,56},{56,64},{64,7... | collective-permute-start | bytes 3538952 | tf_op jit(solution)/shard_map/ppermute | solution.py:25
  59.2 21.2 %collective-permute-start.5 = (f32[3,128,768]{2,1,0:T(8,128)S(1)}, f32[3,128,768]{2,1,0:T(8,128)S(1)}, u32[]{:S(2)}, u32[]{:S(2)}) collective-permute-start(f32[3,128,768]{2,1,0:T(8,128)S(1)} %get-tuple-element.138), channel_id=1, source_target_pairs={{8,0},{16,8},{24,16},{32,24},{40,32},{48,40},{56,48},{64,56},{72,6... | collective-permute-start | bytes 3538952 | tf_op jit(solution)/shard_map/ppermute | solution.py:27
  80.6 19.4 %collective-permute-start.6 = (f32[3,640,128]{2,1,0:T(8,128)S(1)}, f32[3,640,128]{2,1,0:T(8,128)S(1)}, u32[]{:S(2)}, u32[]{:S(2)}) collective-permute-start(f32[3,640,128]{2,1,0:T(8,128)S(1)} %get-tuple-element.133), channel_id=1, source_target_pairs={{0,1},{1,2},{2,3},{3,4},{4,5},{5,6},{6,7},{8,9},{9,10},{10,11},{11... | collective-permute-start | bytes 2949128 | tf_op jit(solution)/shard_map/ppermute | solution.py:25
  82.0 40.9 %collective-permute-start.7 = (f32[3,640,128]{2,1,0:T(8,128)S(1)}, f32[3,640,128]{2,1,0:T(8,128)S(1)}, u32[]{:S(2)}, u32[]{:S(2)}) collective-permute-start(f32[3,640,128]{2,1,0:T(8,128)S(1)} %get-tuple-element.134), channel_id=1, source_target_pairs={{1,0},{2,1},{3,2},{4,3},{5,4},{6,5},{7,6},{9,8},{10,9},{11,10},{12... | collective-permute-start | bytes 2949128 | tf_op jit(solution)/shard_map/ppermute | solution.py:27
  124.4 1.0 copy-start.2
  125.6 14.2 %collective-permute-start.9 = (f32[2,128,512]{2,1,0:T(8,128)S(1)}, f32[2,128,512]{2,1,0:T(8,128)S(1)}, u32[]{:S(2)}, u32[]{:S(2)}) collective-permute-start(f32[2,128,512]{2,1,0:T(8,128)S(1)} %fusion.2), channel_id=1, source_target_pairs={{8,0},{16,8},{24,16},{32,24},{40,32},{48,40},{56,48},{64,56},{72,6... | collective-permute-start | bytes 1572872 | tf_op jit(solution)/shard_map/ppermute | solution.py:27
  127.5 13.4 %collective-permute-start.8 = (f32[2,128,512]{2,1,0:T(8,128)S(1)}, f32[2,128,512]{2,1,0:T(8,128)S(1)}, u32[]{:S(2)}, u32[]{:S(2)}) collective-permute-start(f32[2,128,512]{2,1,0:T(8,128)S(1)} %fusion.2), channel_id=1, source_target_pairs={{0,8},{8,16},{16,24},{24,32},{32,40},{40,48},{48,56},{56,64},{64,7... | collective-permute-start | bytes 1572872 | tf_op jit(solution)/shard_map/ppermute | solution.py:25
  141.0 10.7 %collective-permute-start.10 = (f32[2,384,128]{2,1,0:T(8,128)S(1)}, f32[2,384,128]{2,1,0:T(8,128)S(1)}, u32[]{:S(2)}, u32[]{:S(2)}) collective-permute-start(f32[2,384,128]{2,1,0:T(8,128)S(1)} %get-tuple-element.141), channel_id=1, source_target_pairs={{0,1},{1,2},{2,3},{3,4},{4,5},{5,6},{6,7},{8,9},{9,10},{10,11},{11... | collective-permute-start | bytes 1179656 | tf_op jit(solution)/shard_map/ppermute | solution.py:25
  144.1 16.1 %collective-permute-start.11 = (f32[2,384,128]{2,1,0:T(8,128)S(1)}, f32[2,384,128]{2,1,0:T(8,128)S(1)}, u32[]{:S(2)}, u32[]{:S(2)}) collective-permute-start(f32[2,384,128]{2,1,0:T(8,128)S(1)} %get-tuple-element.142), channel_id=1, source_target_pairs={{1,0},{2,1},{3,2},{4,3},{5,4},{6,5},{7,6},{9,8},{10,9},{11,10},{12... | collective-permute-start | bytes 1179656 | tf_op jit(solution)/shard_map/ppermute | solution.py:27
  172.0 27.1 %copy-start.1 = (f32[2,384,768]{2,1,0:T(8,128)S(1)}, f32[2,384,768]{2,1,0:T(8,128)}, u32[]{:S(2)}) copy-start(f32[2,384,768]{2,1,0:T(8,128)} %shard_map.76) | copy-start | bytes 7077892
  173.7 17.4 %collective-permute-start.12 = (f32[2,128,768]{2,1,0:T(8,128)S(1)}, f32[2,128,768]{2,1,0:T(8,128)S(1)}, u32[]{:S(2)}, u32[]{:S(2)}) collective-permute-start(f32[2,128,768]{2,1,0:T(8,128)S(1)} %get-tuple-element.139), channel_id=1, source_target_pairs={{0,8},{8,16},{16,24},{24,32},{32,40},{40,48},{48,56},{56,64},{64,7... | collective-permute-start | bytes 2359304 | tf_op jit(solution)/shard_map/ppermute | solution.py:25
  182.1 17.0 %collective-permute-start.13 = (f32[2,128,768]{2,1,0:T(8,128)S(1)}, f32[2,128,768]{2,1,0:T(8,128)S(1)}, u32[]{:S(2)}, u32[]{:S(2)}) collective-permute-start(f32[2,128,768]{2,1,0:T(8,128)S(1)} %get-tuple-element.140), channel_id=1, source_target_pairs={{8,0},{16,8},{24,16},{32,24},{40,32},{48,40},{56,48},{64,56},{72,6... | collective-permute-start | bytes 2359304 | tf_op jit(solution)/shard_map/ppermute | solution.py:27
  199.2 8.8 %collective-permute-start.14 = (f32[2,640,128]{2,1,0:T(8,128)S(1)}, f32[2,640,128]{2,1,0:T(8,128)S(1)}, u32[]{:S(2)}, u32[]{:S(2)}) collective-permute-start(f32[2,640,128]{2,1,0:T(8,128)S(1)} %get-tuple-element.135), channel_id=1, source_target_pairs={{0,1},{1,2},{2,3},{3,4},{4,5},{5,6},{6,7},{8,9},{9,10},{10,11},{11... | collective-permute-start | bytes 1966088 | tf_op jit(solution)/shard_map/ppermute | solution.py:25
  200.6 27.6 %collective-permute-start.15 = (f32[2,640,128]{2,1,0:T(8,128)S(1)}, f32[2,640,128]{2,1,0:T(8,128)S(1)}, u32[]{:S(2)}, u32[]{:S(2)}) collective-permute-start(f32[2,640,128]{2,1,0:T(8,128)S(1)} %get-tuple-element.136), channel_id=1, source_target_pairs={{1,0},{2,1},{3,2},{4,3},{5,4},{6,5},{7,6},{9,8},{10,9},{11,10},{12... | collective-permute-start | bytes 1966088 | tf_op jit(solution)/shard_map/ppermute | solution.py:27

commit v2 on v1

--- a/solution.py
+++ b/solution.py
@@ -127,44 +127,46 @@
     )
 
 
-def gradient_kernel(spots_ref, count_ref, ext_ref, probe_ref, amps_ref, fr_ref, fi_ref, out_ref):
-    size = probe_ref.shape[1]
+def window_tools(size, row, col):
     lanes = 128
     sublanes = 8
     wide = size + lanes
     tall = size + sublanes
+    row_base = pl.multiple_of((row // sublanes) * sublanes, sublanes)
+    col_base = pl.multiple_of((col // lanes) * lanes, lanes)
+    row_shift = row % sublanes
+    col_shift = col % lanes
+    rows = pl.ds(row_base, tall)
+    cols = pl.ds(col_base, wide)
+
+    def take(ref, channel):
+        block = ref[channel, rows, cols]
+        block = pltpu.roll(block, (tall - row_shift) % tall, 0)
+        return pltpu.roll(block, (wide - col_shift) % wide, 1)[:size, :size]
+
+    def put(ref, channel, values):
+        block = jnp.concatenate([values, jnp.zeros((size, lanes), jnp.float32)], axis=1)
+        block = jnp.concatenate([block, jnp.zeros((sublanes, wide), jnp.float32)], axis=0)
+        block = pltpu.roll(pltpu.roll(block, col_shift, 1), row_shift, 0)
+        ref[channel, rows, cols] += block
+
+    return take, put
+
+
+def gradient_kernel(spots_ref, count_ref, ext_ref, probe_ref, amps_ref, fr_ref, fi_ref, out_ref):
+    size = probe_ref.shape[1]
     out_ref[...] = jnp.zeros(out_ref.shape, jnp.float32)
-    with_power = out_ref.shape[0] > 2
     for slot in range(amps_ref.shape[0]):
 
         @pl.when(slot < count_ref[0])
         def _():
-            row = spots_ref[slot, 0]
-            col = spots_ref[slot, 1]
-            row_base = pl.multiple_of((row // sublanes) * sublanes, sublanes)
-            col_base = pl.multiple_of((col // lanes) * lanes, lanes)
-            row_shift = row % sublanes
-            col_shift = col % lanes
-            rows = pl.ds(row_base, tall)
-            cols = pl.ds(col_base, wide)
-
-            def take(channel):
-                block = ext_ref[channel, rows, cols]
-                block = pltpu.roll(block, (tall - row_shift) % tall, 0)
-                return pltpu.roll(block, (wide - col_shift) % wide, 1)[:size, :size]
-
-            def put(channel, values):
-                block = jnp.concatenate([values, jnp.zeros((size, lanes), jnp.float32)], axis=1)
-                block = jnp.concatenate([block, jnp.zeros((sublanes, wide), jnp.float32)], axis=0)
-                block = pltpu.roll(pltpu.roll(block, col_shift, 1), row_shift, 0)
-                out_ref[channel, rows, cols] += block
-
+            take, put = window_tools(size, spots_ref[slot, 0], spots_ref[slot, 1])
             probe_real = probe_ref[0]
             probe_imag = probe_ref[1]
             table_real = fr_ref[...]
             table_imag = fi_ref[...]
-            obj_real = take(0)
-            obj_imag = take(1)
+            obj_real = take(ext_ref, 0)
+            obj_imag = take(ext_ref, 1)
             exit_real = probe_real * obj_real - probe_imag * obj_imag
             exit_imag = probe_real * obj_imag + probe_imag * obj_real
             half_real = dot_exact(table_real, exit_real) - dot_exact(table_imag, exit_imag)
@@ -178,22 +180,86 @@
             back_imag = dot_exact(table_real, miss_imag) - dot_exact(table_imag, miss_real)
             near_real = dot_exact(back_real, table_real) + dot_exact(back_imag, table_imag)
             near_imag = dot_exact(back_imag, table_real) - dot_exact(back_real, table_imag)
-            put(0, probe_real * near_real + probe_imag * near_imag)
-            put(1, probe_real * near_imag - probe_imag * near_real)
-            if with_power:
-                put(2, probe_real * probe_real + probe_imag * probe_imag)
-
-
-def gradient_canvas(channels, ext_shape, spots, count, extended, probe_field, own_amps, tables):
-    vmem = pl.BlockSpec(memory_space=pltpu.VMEM)
-    smem = pl.BlockSpec(memory_space=pltpu.SMEM)
+            put(out_ref, 0, probe_real * near_real + probe_imag * near_imag)
+            put(out_ref, 1, probe_real * near_imag - probe_imag * near_real)
+
+
+def power_kernel(spots_ref, count_ref, probe_ref, out_ref):
+    size = probe_ref.shape[1]
+    out_ref[...] = jnp.zeros(out_ref.shape, jnp.float32)
+    power = probe_ref[0] * probe_ref[0] + probe_ref[1] * probe_ref[1]
+    for slot in range(spots_ref.shape[0]):
+
+        @pl.when(slot < count_ref[0])
+        def _():
+            _, put = window_tools(size, spots_ref[slot, 0], spots_ref[slot, 1])
+            put(out_ref, 0, power)
+
+
+VMEM_SPEC = pl.BlockSpec(memory_space=pltpu.VMEM)
+SMEM_SPEC = pl.BlockSpec(memory_space=pltpu.SMEM)
+KERNEL_PARAMS = pltpu.CompilerParams(vmem_limit_bytes=60 * 1024 * 1024)
+
+
+def gradient_canvas(ext_shape, spots, count, extended, probe_field, own_amps, tables):
     return pl.pallas_call(
         gradient_kernel,
-        out_shape=jax.ShapeDtypeStruct((channels,) + ext_shape, jnp.float32),
-        in_specs=[smem, smem, vmem, vmem, vmem, vmem, vmem],
-        out_specs=vmem,
-        compiler_params=pltpu.CompilerParams(vmem_limit_bytes=60 * 1024 * 1024),
+        out_shape=jax.ShapeDtypeStruct((2,) + ext_shape, jnp.float32),
+        in_specs=[SMEM_SPEC, SMEM_SPEC] + [VMEM_SPEC] * 5,
+        out_specs=VMEM_SPEC,
+        compiler_params=KERNEL_PARAMS,
     )(spots, count.reshape(1), extended, probe_field, own_amps, tables[0], tables[1])
+
+
+def power_canvas(ext_shape, spots, count, probe_field):
+    return pl.pallas_call(
+        power_kernel,
+        out_shape=jax.ShapeDtypeStruct((1,) + ext_shape, jnp.float32),
+        in_specs=[SMEM_SPEC, SMEM_SPEC, VMEM_SPEC],
+        out_specs=VMEM_SPEC,
+        compiler_params=KERNEL_PARAMS,
+    )(spots, count.reshape(1), probe_field)
+
+
+def from_prev(cells, axis):
+    count = lax.axis_size(axis)
+    return lax.ppermute(cells, axis, [(i, i + 1) for i in range(count - 1)])
+
+
+def from_next(cells, axis):
+    count = lax.axis_size(axis)
+    return lax.ppermute(cells, axis, [(i + 1, i) for i in range(count - 1)])
+
+
+def fold_canvas(canvas, margin, with_halo_cols):
+    rows = canvas.shape[1]
+    cols = canvas.shape[2]
+    upper = canvas[:, :margin]
+    lower = canvas[:, rows - margin :]
+    folded = canvas[:, margin : rows - margin] + from_prev(lower, "sx") + from_next(upper, "sx")
+    left_rim = folded[..., :margin]
+    left_edge = folded[..., margin : 2 * margin]
+    right_edge = folded[..., cols - 2 * margin : cols - margin]
+    right_rim = folded[..., cols - margin :]
+    inner = folded[..., 2 * margin : cols - 2 * margin]
+    if with_halo_cols:
+        got_prev = from_prev(jnp.concatenate([right_rim, right_edge], axis=0), "sy")
+        got_next = from_next(jnp.concatenate([left_rim, left_edge], axis=0), "sy")
+        depth = canvas.shape[0]
+        return jnp.concatenate(
+            [
+                left_rim + got_prev[depth:],
+                left_edge + got_prev[:depth],
+                inner,
+                right_edge + got_next[:depth],
+                right_rim + got_next[depth:],
+            ],
+            axis=2,
+        )
+    return jnp.concatenate(
+        [left_edge + from_prev(right_rim, "sy"), inner, right_edge + from_next(left_rim, "sy")],
+        axis=2,
+    )
 
 
 def on_device(object_field, probe_field, amplitudes, centres, counts):
@@ -206,22 +272,38 @@
     own_amps = amplitudes[0, 0]
     sx_size = lax.axis_size("sx")
     sx_index = lax.axis_index("sx")
+    sy_size = lax.axis_size("sy")
+    sy_index = lax.axis_index("sy")
     column_counts = counts[:, 0]
     sx_positions = jnp.arange(sx_size, dtype=jnp.int32)
     own_count = jnp.sum(jnp.where(sx_positions == sx_index, column_counts, 0))
     ext_shape = (block_rows + size_probe, block_cols + size_probe)
+
+    illumination = fold_canvas(power_canvas(ext_shape, spots, own_count, probe_field), margin, True)[0]
     current = object_field
+    wide = jnp.concatenate(
+        [
+            from_prev(current[..., block_cols - margin :], "sy"),
+            current,
+            from_next(current[..., :margin], "sy"),
+        ],
+        axis=2,
+    )
+    col_index = jnp.arange(block_cols + size_probe, dtype=jnp.int32)
+    inside = ((col_index >= margin) | (sy_index > 0)) & (
+        (col_index < block_cols + margin) | (sy_index < sy_size - 1)
+    )
     for sweep_index in range(ITERS):
-        extended = with_halo(current, (("sx", 1), ("sy", 2)), margin)
-        channels = 3 if sweep_index == 0 else 2
-        canvas = gradient_canvas(
-            channels, ext_shape, spots, own_count, extended, probe_field, own_amps, tables
-        )
-        settled = settle(canvas, margin, block_rows, block_cols)
-        if sweep_index == 0:
-            illumination = settled[2]
-        gradient = settled[0:2]
-        current = current - gradient / (illumination + DAMPING)
+        extended = jnp.concatenate([from_prev(wide, "sx"), wide, from_next(wide, "sx")], axis=1)
+        canvas = gradient_canvas(ext_shape, spots, own_count, extended, probe_field, own_amps, tables)
+        last = sweep_index == ITERS - 1
+        gradient = fold_canvas(canvas, margin, not last)
+        if last:
+            current = wide[..., margin : margin + block_cols] - gradient / (
+                illumination[:, margin : margin + block_cols] + DAMPING
+            )
+        else:
+            wide = jnp.where(inside, wide - gradient / (illumination + DAMPING), 0.0)
     return current
 
 

time: 230 us -> 181 us (0.79)
  the two profiles are of different devices: /device:TPU:225 before, /device:TPU:28 now
where the time goes in v2:
time: 181 us; the launch traced here: 180 us
  starting transfers between devices  67.4 us (37%)
  waiting for transfers between devices  60.7 us (34%)
  Pallas kernels  35.3 us (20%)
  other arithmetic  11.3 us (6%)
  local copies, waits for them, and re-layouts  5.35 us (3%)
    ppermute x9, starting transfers between devices, from_next(): return lax.ppermute(cells, axis, [(i + 1, i) for i in range(count - 1)])  48.9 us
    ppermute x9, waiting for transfers between devices, from_prev(): return lax.ppermute(cells, axis, [(i, i + 1) for i in range(count - 1)])  42.1 us
    pallas_call x2, Pallas kernels, gradient_canvas(): pl.pallas_call(gradient_kernel, out_shape=jax.ShapeDtypeStruct((2,) + ext...  31.8 us
    ppermute x9, waiting for transfers between devices, from_next(): return lax.ppermute(cells, axis, [(i + 1, i) for i in range(count - 1)])  18.6 us
    ppermute x9, starting transfers between devices, from_prev(): return lax.ppermute(cells, axis, [(i, i + 1) for i in range(count - 1)])  18.5 us
    slice x3, local copies, waits for them, and re-layouts, fold_canvas(): lower = canvas[:, rows - margin:]  4.14 us
  transfers between devices with their start and end apart: 18, of which 12 were waited for; matrix products, arithmetic and copies ran while one was open for 5% of the time, Pallas kernels for 11%

profile of v2, /device:TPU:28, one launch (start us, length us, event | category | flops | bytes accessed | tf_op | source)
XLA Modules:
  0.0 180.5 jit_solution(15744393232010240027)
XLA Ops:
  1.1 3.1 %collective-permute-start = (f32[2,128,128]{2,1,0:T(8,128)S(1)}, f32[2,128,128]{2,1,0:T(8,128)S(1)}, u32[]{:S(2)}, u32[]{:S(2)}) collective-permute-start(f32[2,128,128]{2,1,0:T(8,128)S(1)} %get-tuple-element.19), channel_id=1, source_target_pairs={{0,1},{1,2},{2,3},{3,4},{4,5},{5,6},{6,7},{8,9},{9,10},{10,11},{11... | collective-permute-start | bytes 393224 | tf_op jit(solution)/shard_map/ppermute | solution.py:226
  5.5 3.5 %shard_map.56 = f32[1,384,768]{2,1,0:T(8,128)} custom-call(s32[2,2]{1,0:T(2,128)} %bitcast.19, s32[1]{0:T(128)} %bitcast.2.count_ref, f32[2,256,256]{2,1,0:T(8,128)} %probe_ref.5), custom_call_target="tpu_custom_call" | custom-call | tf_op jit(solution)/shard_map/pallas_call | solution.py:215
  10.2 1.9 %collective-permute-start.8 = (f32[1,128,768]{2,1,0:T(8,128)S(1)}, f32[1,128,768]{2,1,0:T(8,128)S(1)}, u32[]{:S(2)}, u32[]{:S(2)}) collective-permute-start(f32[1,128,768]{2,1,0:T(8,128)S(1)} %get-tuple-element.9), channel_id=1, source_target_pairs={{0,8},{8,16},{16,24},{24,32},{32,40},{40,48},{48,56},{56,64},{64,7... | collective-permute-start | bytes 1179656 | tf_op jit(solution)/shard_map/ppermute | solution.py:226
  12.2 7.3 %collective-permute-start.9 = (f32[1,128,768]{2,1,0:T(8,128)S(1)}, f32[1,128,768]{2,1,0:T(8,128)S(1)}, u32[]{:S(2)}, u32[]{:S(2)}) collective-permute-start(f32[1,128,768]{2,1,0:T(8,128)S(1)} %get-tuple-element.10), channel_id=1, source_target_pairs={{8,0},{16,8},{24,16},{32,24},{40,32},{48,40},{56,48},{64,56},{72,6... | collective-permute-start | bytes 1179656 | tf_op jit(solution)/shard_map/ppermute | solution.py:231
  19.4 3.9 %collective-permute-start.1 = (f32[2,128,128]{2,1,0:T(8,128)S(1)}, f32[2,128,128]{2,1,0:T(8,128)S(1)}, u32[]{:S(2)}, u32[]{:S(2)}) collective-permute-start(f32[2,128,128]{2,1,0:T(8,128)S(1)} %get-tuple-element.18), channel_id=1, source_target_pairs={{1,0},{2,1},{3,2},{4,3},{5,4},{6,5},{7,6},{9,8},{10,9},{11,10},{12... | collective-permute-start | bytes 393224 | tf_op jit(solution)/shard_map/ppermute | solution.py:231
  23.4 2.9 %collective-permute-done.1 = f32[2,128,128]{2,1,0:T(8,128)S(1)} collective-permute-done((f32[2,128,128]{2,1,0:T(8,128)S(1)}, f32[2,128,128]{2,1,0:T(8,128)S(1)}, u32[]{:S(2)}, u32[]{:S(2)}) %collective-permute-start.1) | collective-permute-done | bytes 131104 | tf_op jit(solution)/shard_map/ppermute | solution.py:231
  28.2 7.3 %collective-permute-start.3 = (f32[2,128,768]{2,1,0:T(8,128)S(1)}, f32[2,128,768]{2,1,0:T(8,128)S(1)}, u32[]{:S(2)}, u32[]{:S(2)}) collective-permute-start(f32[2,128,768]{2,1,0:T(8,128)S(1)} %constant_dynamic-update-slice_fusion), channel_id=1, source_target_pairs={{8,0},{16,8},{24,16},{32,24},{40,32},{48,40},{56,48},{64,56},{72,6... | collective-permute-start | bytes 2359304 | tf_op jit(solution)/shard_map/ppermute | solution.py:231
  40.3 4.8 %collective-permute-done.10 = f32[2,128,128]{2,1,0:T(8,128)S(1)} collective-permute-done((f32[2,128,128]{2,1,0:T(8,128)S(1)}, f32[2,128,128]{2,1,0:T(8,128)S(1)}, u32[]{:S(2)}, u32[]{:S(2)}) %collective-permute-start.10) | collective-permute-done | bytes 131104 | tf_op jit(solution)/shard_map/ppermute | solution.py:226
  45.2 4.1 %collective-permute-start.11 = (f32[2,128,128]{2,1,0:T(8,128)S(1)}, f32[2,128,128]{2,1,0:T(8,128)S(1)}, u32[]{:S(2)}, u32[]{:S(2)}) collective-permute-start(f32[2,128,128]{2,1,0:T(8,128)S(1)} %pad_maximum_fusion.5), channel_id=1, source_target_pairs={{1,0},{2,1},{3,2},{4,3},{5,4},{6,5},{7,6},{9,8},{10,9},{11,10},{12... | collective-permute-start | bytes 393224 | tf_op jit(solution)/shard_map/ppermute | solution.py:231
  51.0 15.9 %shard_map.55 = f32[2,384,768]{2,1,0:T(8,128)} custom-call(s32[2,2]{1,0:T(2,128)} %bitcast.20, s32[1]{0:T(128)} %bitcast.2.count_ref, f32[2,384,768]{2,1,0:T(8,128)} %pad_maximum_fusion.ext_ref, f32[2,256,256]{2,1,0:T(8,128)} %probe_ref.5, f32[2,256,256]{2,1,0:T(8,128)} %bitcast.16, f32[256,256]{1,0:T(8,128)} %get-tuple-element.26.fr_ref, ...), custom_call_target="tpu_custom_call" | custom-call | tf_op jit(solution)/shard_map/pallas_call | solution.py:205
  70.2 7.3 %collective-permute-start.5 = (f32[2,128,768]{2,1,0:T(8,128)S(1)}, f32[2,128,768]{2,1,0:T(8,128)S(1)}, u32[]{:S(2)}, u32[]{:S(2)}) collective-permute-start(f32[2,128,768]{2,1,0:T(8,128)S(1)} %get-tuple-element.8), channel_id=1, source_target_pairs={{8,0},{16,8},{24,16},{32,24},{40,32},{48,40},{56,48},{64,56},{72,6... | collective-permute-start | bytes 2359304 | tf_op jit(solution)/shard_map/ppermute | solution.py:231
  77.6 7.8 %collective-permute-done.4 = f32[2,128,768]{2,1,0:T(8,128)S(1)} collective-permute-done((f32[2,128,768]{2,1,0:T(8,128)S(1)}, f32[2,128,768]{2,1,0:T(8,128)S(1)}, u32[]{:S(2)}, u32[]{:S(2)}) %collective-permute-start.4) | collective-permute-done | bytes 786464 | tf_op jit(solution)/shard_map/ppermute | solution.py:226
  90.3 8.2 %collective-permute-done.6 = f32[4,128,128]{2,1,0:T(8,128)S(1)} collective-permute-done((f32[4,128,128]{2,1,0:T(8,128)S(1)}, f32[4,128,128]{2,1,0:T(8,128)S(1)}, u32[]{:S(2)}, u32[]{:S(2)}) %collective-permute-start.6) | collective-permute-done | bytes 262176 | tf_op jit(solution)/shard_map/ppermute | solution.py:226
  98.6 2.2 %collective-permute-start.7 = (f32[4,128,128]{2,1,0:T(8,128)S(1)}, f32[4,128,128]{2,1,0:T(8,128)S(1)}, u32[]{:S(2)}, u32[]{:S(2)}) collective-permute-start(f32[4,128,128]{2,1,0:T(8,128)S(1)} %pad_maximum_fusion.3), channel_id=1, source_target_pairs={{1,0},{2,1},{3,2},{4,3},{5,4},{6,5},{7,6},{9,8},{10,9},{11,10},{12... | collective-permute-start | bytes 786440 | tf_op jit(solution)/shard_map/ppermute | solution.py:231
  100.9 6.0 %collective-permute-done.7 = f32[4,128,128]{2,1,0:T(8,128)S(1)} collective-permute-done((f32[4,128,128]{2,1,0:T(8,128)S(1)}, f32[4,128,128]{2,1,0:T(8,128)S(1)}, u32[]{:S(2)}, u32[]{:S(2)}) %collective-permute-start.7) | collective-permute-done | bytes 262176 | tf_op jit(solution)/shard_map/ppermute | solution.py:231
  109.0 7.3 %collective-permute-start.13 = (f32[2,128,768]{2,1,0:T(8,128)S(1)}, f32[2,128,768]{2,1,0:T(8,128)S(1)}, u32[]{:S(2)}, u32[]{:S(2)}) collective-permute-start(f32[2,128,768]{2,1,0:T(8,128)S(1)} %subtract_select_fusion), channel_id=1, source_target_pairs={{8,0},{16,8},{24,16},{32,24},{40,32},{48,40},{56,48},{64,56},{72,6... | collective-permute-start | bytes 2359304 | tf_op jit(solution)/shard_map/ppermute | solution.py:231
  116.2 7.7 %collective-permute-done.12 = f32[2,128,768]{2,1,0:T(8,128)S(1)} collective-permute-done((f32[2,128,768]{2,1,0:T(8,128)S(1)}, f32[2,128,768]{2,1,0:T(8,128)S(1)}, u32[]{:S(2)}, u32[]{:S(2)}) %collective-permute-start.12) | collective-permute-done | bytes 786464 | tf_op jit(solution)/shard_map/ppermute | solution.py:226
  127.3 15.9 %shard_map.57 = f32[2,384,768]{2,1,0:T(8,128)} custom-call(s32[2,2]{1,0:T(2,128)} %bitcast.21, s32[1]{0:T(128)} %bitcast.2.count_ref, f32[2,384,768]{2,1,0:T(8,128)} %pad_maximum_fusion.1.ext_ref, f32[2,256,256]{2,1,0:T(8,128)} %probe_ref.5, f32[2,256,256]{2,1,0:T(8,128)} %bitcast.17, f32[256,256]{1,0:T(8,128)} %get-tuple-element.26.fr_ref, ...), custom_call_target="tpu_custom_call" | custom-call | tf_op jit(solution)/shard_map/pallas_call | solution.py:205
  144.7 1.9 %collective-permute-start.14 = (f32[2,128,768]{2,1,0:T(8,128)S(1)}, f32[2,128,768]{2,1,0:T(8,128)S(1)}, u32[]{:S(2)}, u32[]{:S(2)}) collective-permute-start(f32[2,128,768]{2,1,0:T(8,128)S(1)} %get-tuple-element.5), channel_id=1, source_target_pairs={{0,8},{8,16},{16,24},{24,32},{32,40},{40,48},{48,56},{56,64},{64,7... | collective-permute-start | bytes 2359304 | tf_op jit(solution)/shard_map/ppermute | solution.py:226
  146.6 7.4 %collective-permute-start.15 = (f32[2,128,768]{2,1,0:T(8,128)S(1)}, f32[2,128,768]{2,1,0:T(8,128)S(1)}, u32[]{:S(2)}, u32[]{:S(2)}) collective-permute-start(f32[2,128,768]{2,1,0:T(8,128)S(1)} %get-tuple-element.6), channel_id=1, source_target_pairs={{8,0},{16,8},{24,16},{32,24},{40,32},{48,40},{56,48},{64,56},{72,6... | collective-permute-start | bytes 2359304 | tf_op jit(solution)/shard_map/ppermute | solution.py:231
  154.1 7.8 %collective-permute-done.14 = f32[2,128,768]{2,1,0:T(8,128)S(1)} collective-permute-done((f32[2,128,768]{2,1,0:T(8,128)S(1)}, f32[2,128,768]{2,1,0:T(8,128)S(1)}, u32[]{:S(2)}, u32[]{:S(2)}) %collective-permute-start.14) | collective-permute-done | bytes 786464 | tf_op jit(solution)/shard_map/ppermute | solution.py:226
  166.8 5.8 %collective-permute-done.16 = f32[2,128,128]{2,1,0:T(8,128)S(1)} collective-permute-done((f32[2,128,128]{2,1,0:T(8,128)S(1)}, f32[2,128,128]{2,1,0:T(8,128)S(1)}, u32[]{:S(2)}, u32[]{:S(2)}) %collective-permute-start.16) | collective-permute-done | bytes 131104 | tf_op jit(solution)/shard_map/ppermute | solution.py:226
  172.7 2.3 %collective-permute-start.17 = (f32[2,128,128]{2,1,0:T(8,128)S(1)}, f32[2,128,128]{2,1,0:T(8,128)S(1)}, u32[]{:S(2)}, u32[]{:S(2)}) collective-permute-start(f32[2,128,128]{2,1,0:T(8,128)S(1)} %get-tuple-element.12), channel_id=1, source_target_pairs={{1,0},{2,1},{3,2},{4,3},{5,4},{6,5},{7,6},{9,8},{10,9},{11,10},{12... | collective-permute-start | bytes 393224 | tf_op jit(solution)/shard_map/ppermute | solution.py:231
  175.1 4.5 %collective-permute-done.17 = f32[2,128,128]{2,1,0:T(8,128)S(1)} collective-permute-done((f32[2,128,128]{2,1,0:T(8,128)S(1)}, f32[2,128,128]{2,1,0:T(8,128)S(1)}, u32[]{:S(2)}, u32[]{:S(2)}) %collective-permute-start.17) | collective-permute-done | bytes 131104 | tf_op jit(solution)/shard_map/ppermute | solution.py:231
  (61 shorter events, 33.3 us)
Async XLA Ops:
  0.0 23.3 %copy-start = (f32[2,128,512]{2,1,0:T(8,128)S(1)}, f32[2,128,512]{2,1,0:T(8,128)}, u32[]{:S(2)}) copy-start(f32[2,128,512]{2,1,0:T(8,128)} %param.5) | copy-start | bytes 1572868
  1.1 22.3 %collective-permute-start = (f32[2,128,128]{2,1,0:T(8,128)S(1)}, f32[2,128,128]{2,1,0:T(8,128)S(1)}, u32[]{:S(2)}, u32[]{:S(2)}) collective-permute-start(f32[2,128,128]{2,1,0:T(8,128)S(1)} %get-tuple-element.19), channel_id=1, source_target_pairs={{0,1},{1,2},{2,3},{3,4},{4,5},{5,6},{6,7},{8,9},{9,10},{10,11},{11... | collective-permute-start | bytes 393224 | tf_op jit(solution)/shard_map/ppermute | solution.py:226
  10.2 25.3 %collective-permute-start.8 = (f32[1,128,768]{2,1,0:T(8,128)S(1)}, f32[1,128,768]{2,1,0:T(8,128)S(1)}, u32[]{:S(2)}, u32[]{:S(2)}) collective-permute-start(f32[1,128,768]{2,1,0:T(8,128)S(1)} %get-tuple-element.9), channel_id=1, source_target_pairs={{0,8},{8,16},{16,24},{24,32},{32,40},{40,48},{48,56},{56,64},{64,7... | collective-permute-start | bytes 1179656 | tf_op jit(solution)/shard_map/ppermute | solution.py:226
  12.2 23.3 %collective-permute-start.9 = (f32[1,128,768]{2,1,0:T(8,128)S(1)}, f32[1,128,768]{2,1,0:T(8,128)S(1)}, u32[]{:S(2)}, u32[]{:S(2)}) collective-permute-start(f32[1,128,768]{2,1,0:T(8,128)S(1)} %get-tuple-element.10), channel_id=1, source_target_pairs={{8,0},{16,8},{24,16},{32,24},{40,32},{48,40},{56,48},{64,56},{72,6... | collective-permute-start | bytes 1179656 | tf_op jit(solution)/shard_map/ppermute | solution.py:231
  19.4 6.9 %collective-permute-start.1 = (f32[2,128,128]{2,1,0:T(8,128)S(1)}, f32[2,128,128]{2,1,0:T(8,128)S(1)}, u32[]{:S(2)}, u32[]{:S(2)}) collective-permute-start(f32[2,128,128]{2,1,0:T(8,128)S(1)} %get-tuple-element.18), channel_id=1, source_target_pairs={{1,0},{2,1},{3,2},{4,3},{5,4},{6,5},{7,6},{9,8},{10,9},{11,10},{12... | collective-permute-start | bytes 393224 | tf_op jit(solution)/shard_map/ppermute | solution.py:231
  26.3 23.0 %collective-permute-start.2 = (f32[2,128,768]{2,1,0:T(8,128)S(1)}, f32[2,128,768]{2,1,0:T(8,128)S(1)}, u32[]{:S(2)}, u32[]{:S(2)}) collective-permute-start(f32[2,128,768]{2,1,0:T(8,128)S(1)} %constant_dynamic-update-slice_fusion), channel_id=1, source_target_pairs={{0,8},{8,16},{16,24},{24,32},{32,40},{40,48},{48,56},{56,64},{64,7... | collective-permute-start | bytes 2359304 | tf_op jit(solution)/shard_map/ppermute | solution.py:226
  28.2 21.1 %collective-permute-start.3 = (f32[2,128,768]{2,1,0:T(8,128)S(1)}, f32[2,128,768]{2,1,0:T(8,128)S(1)}, u32[]{:S(2)}, u32[]{:S(2)}) collective-permute-start(f32[2,128,768]{2,1,0:T(8,128)S(1)} %constant_dynamic-update-slice_fusion), channel_id=1, source_target_pairs={{8,0},{16,8},{24,16},{32,24},{40,32},{48,40},{56,48},{64,56},{72,6... | collective-permute-start | bytes 2359304 | tf_op jit(solution)/shard_map/ppermute | solution.py:231
  36.6 8.6 %collective-permute-start.10 = (f32[2,128,128]{2,1,0:T(8,128)S(1)}, f32[2,128,128]{2,1,0:T(8,128)S(1)}, u32[]{:S(2)}, u32[]{:S(2)}) collective-permute-start(f32[2,128,128]{2,1,0:T(8,128)S(1)} %pad_maximum_fusion.4), channel_id=1, source_target_pairs={{0,1},{1,2},{2,3},{3,4},{4,5},{5,6},{6,7},{8,9},{9,10},{10,11},{11... | collective-permute-start | bytes 393224 | tf_op jit(solution)/shard_map/ppermute | solution.py:226
  45.2 32.3 %collective-permute-start.11 = (f32[2,128,128]{2,1,0:T(8,128)S(1)}, f32[2,128,128]{2,1,0:T(8,128)S(1)}, u32[]{:S(2)}, u32[]{:S(2)}) collective-permute-start(f32[2,128,128]{2,1,0:T(8,128)S(1)} %pad_maximum_fusion.5), channel_id=1, source_target_pairs={{1,0},{2,1},{3,2},{4,3},{5,4},{6,5},{7,6},{9,8},{10,9},{11,10},{12... | collective-permute-start | bytes 393224 | tf_op jit(solution)/shard_map/ppermute | solution.py:231
  68.3 17.0 %collective-permute-start.4 = (f32[2,128,768]{2,1,0:T(8,128)S(1)}, f32[2,128,768]{2,1,0:T(8,128)S(1)}, u32[]{:S(2)}, u32[]{:S(2)}) collective-permute-start(f32[2,128,768]{2,1,0:T(8,128)S(1)} %get-tuple-element.7), channel_id=1, source_target_pairs={{0,8},{8,16},{16,24},{24,32},{32,40},{40,48},{48,56},{56,64},{64,7... | collective-permute-start | bytes 2359304 | tf_op jit(solution)/shard_map/ppermute | solution.py:226
  70.2 16.8 %collective-permute-start.5 = (f32[2,128,768]{2,1,0:T(8,128)S(1)}, f32[2,128,768]{2,1,0:T(8,128)S(1)}, u32[]{:S(2)}, u32[]{:S(2)}) collective-permute-start(f32[2,128,768]{2,1,0:T(8,128)S(1)} %get-tuple-element.8), channel_id=1, source_target_pairs={{8,0},{16,8},{24,16},{32,24},{40,32},{48,40},{56,48},{64,56},{72,6... | collective-permute-start | bytes 2359304 | tf_op jit(solution)/shard_map/ppermute | solution.py:231
  88.4 10.2 %collective-permute-start.6 = (f32[4,128,128]{2,1,0:T(8,128)S(1)}, f32[4,128,128]{2,1,0:T(8,128)S(1)}, u32[]{:S(2)}, u32[]{:S(2)}) collective-permute-start(f32[4,128,128]{2,1,0:T(8,128)S(1)} %pad_maximum_fusion.2), channel_id=1, source_target_pairs={{0,1},{1,2},{2,3},{3,4},{4,5},{5,6},{6,7},{8,9},{9,10},{10,11},{11... | collective-permute-start | bytes 786440 | tf_op jit(solution)/shard_map/ppermute | solution.py:226
  98.6 8.3 %collective-permute-start.7 = (f32[4,128,128]{2,1,0:T(8,128)S(1)}, f32[4,128,128]{2,1,0:T(8,128)S(1)}, u32[]{:S(2)}, u32[]{:S(2)}) collective-permute-start(f32[4,128,128]{2,1,0:T(8,128)S(1)} %pad_maximum_fusion.3), channel_id=1, source_target_pairs={{1,0},{2,1},{3,2},{4,3},{5,4},{6,5},{7,6},{9,8},{10,9},{11,10},{12... | collective-permute-start | bytes 786440 | tf_op jit(solution)/shard_map/ppermute | solution.py:231
  107.0 16.9 %collective-permute-start.12 = (f32[2,128,768]{2,1,0:T(8,128)S(1)}, f32[2,128,768]{2,1,0:T(8,128)S(1)}, u32[]{:S(2)}, u32[]{:S(2)}) collective-permute-start(f32[2,128,768]{2,1,0:T(8,128)S(1)} %subtract_select_fusion), channel_id=1, source_target_pairs={{0,8},{8,16},{16,24},{24,32},{32,40},{40,48},{48,56},{56,64},{64,7... | collective-permute-start | bytes 2359304 | tf_op jit(solution)/shard_map/ppermute | solution.py:226
  109.0 16.8 %collective-permute-start.13 = (f32[2,128,768]{2,1,0:T(8,128)S(1)}, f32[2,128,768]{2,1,0:T(8,128)S(1)}, u32[]{:S(2)}, u32[]{:S(2)}) collective-permute-start(f32[2,128,768]{2,1,0:T(8,128)S(1)} %subtract_select_fusion), channel_id=1, source_target_pairs={{8,0},{16,8},{24,16},{32,24},{40,32},{48,40},{56,48},{64,56},{72,6... | collective-permute-start | bytes 2359304 | tf_op jit(solution)/shard_map/ppermute | solution.py:231
  144.7 17.2 %collective-permute-start.14 = (f32[2,128,768]{2,1,0:T(8,128)S(1)}, f32[2,128,768]{2,1,0:T(8,128)S(1)}, u32[]{:S(2)}, u32[]{:S(2)}) collective-permute-start(f32[2,128,768]{2,1,0:T(8,128)S(1)} %get-tuple-element.5), channel_id=1, source_target_pairs={{0,8},{8,16},{16,24},{24,32},{32,40},{40,48},{48,56},{56,64},{64,7... | collective-permute-start | bytes 2359304 | tf_op jit(solution)/shard_map/ppermute | solution.py:226
  146.6 17.0 %collective-permute-start.15 = (f32[2,128,768]{2,1,0:T(8,128)S(1)}, f32[2,128,768]{2,1,0:T(8,128)S(1)}, u32[]{:S(2)}, u32[]{:S(2)}) collective-permute-start(f32[2,128,768]{2,1,0:T(8,128)S(1)} %get-tuple-element.6), channel_id=1, source_target_pairs={{8,0},{16,8},{24,16},{32,24},{40,32},{48,40},{56,48},{64,56},{72,6... | collective-permute-start | bytes 2359304 | tf_op jit(solution)/shard_map/ppermute | solution.py:231
  164.9 7.8 %collective-permute-start.16 = (f32[2,128,128]{2,1,0:T(8,128)S(1)}, f32[2,128,128]{2,1,0:T(8,128)S(1)}, u32[]{:S(2)}, u32[]{:S(2)}) collective-permute-start(f32[2,128,128]{2,1,0:T(8,128)S(1)} %slice.173), channel_id=1, source_target_pairs={{0,1},{1,2},{2,3},{3,4},{4,5},{5,6},{6,7},{8,9},{9,10},{10,11},{11... | collective-permute-start | bytes 393224 | tf_op jit(solution)/shard_map/ppermute | solution.py:226
  172.7 6.9 %collective-permute-start.17 = (f32[2,128,128]{2,1,0:T(8,128)S(1)}, f32[2,128,128]{2,1,0:T(8,128)S(1)}, u32[]{:S(2)}, u32[]{:S(2)}) collective-permute-start(f32[2,128,128]{2,1,0:T(8,128)S(1)} %get-tuple-element.12), channel_id=1, source_target_pairs={{1,0},{2,1},{3,2},{4,3},{5,4},{6,5},{7,6},{9,8},{10,9},{11,10},{12... | collective-permute-start | bytes 393224 | tf_op jit(solution)/shard_map/ppermute | solution.py:231

commit v3 on v2

--- a/solution.py
+++ b/solution.py
@@ -221,45 +221,139 @@
     )(spots, count.reshape(1), probe_field)
 
 
-def from_prev(cells, axis):
-    count = lax.axis_size(axis)
-    return lax.ppermute(cells, axis, [(i, i + 1) for i in range(count - 1)])
-
-
-def from_next(cells, axis):
-    count = lax.axis_size(axis)
-    return lax.ppermute(cells, axis, [(i + 1, i) for i in range(count - 1)])
-
-
-def fold_canvas(canvas, margin, with_halo_cols):
-    rows = canvas.shape[1]
-    cols = canvas.shape[2]
-    upper = canvas[:, :margin]
-    lower = canvas[:, rows - margin :]
-    folded = canvas[:, margin : rows - margin] + from_prev(lower, "sx") + from_next(upper, "sx")
-    left_rim = folded[..., :margin]
-    left_edge = folded[..., margin : 2 * margin]
-    right_edge = folded[..., cols - 2 * margin : cols - margin]
-    right_rim = folded[..., cols - margin :]
-    inner = folded[..., 2 * margin : cols - 2 * margin]
-    if with_halo_cols:
-        got_prev = from_prev(jnp.concatenate([right_rim, right_edge], axis=0), "sy")
-        got_next = from_next(jnp.concatenate([left_rim, left_edge], axis=0), "sy")
-        depth = canvas.shape[0]
-        return jnp.concatenate(
-            [
-                left_rim + got_prev[depth:],
-                left_edge + got_prev[:depth],
-                inner,
-                right_edge + got_next[:depth],
-                right_rim + got_next[depth:],
-            ],
-            axis=2,
+NEIGHBOURS = [(-1, -1), (-1, 0), (-1, 1), (0, -1), (0, 1), (1, -1), (1, 0), (1, 1)]
+
+
+def mesh_place():
+    return (
+        lax.axis_index("sx"),
+        lax.axis_index("sy"),
+        lax.axis_size("sx"),
+        lax.axis_size("sy"),
+    )
+
+
+def exists(row_dev, col_dev, row_count, col_count):
+    return (row_dev >= 0) & (row_dev < row_count) & (col_dev >= 0) & (col_dev < col_count)
+
+
+def halo_kernel(cur_ref, ext_ref, send_sems, recv_sems):
+    rows = cur_ref.shape[1]
+    cols = cur_ref.shape[2]
+    margin = (ext_ref.shape[2] - cols) // 2
+    me_r, me_c, n_r, n_c = mesh_place()
+    ext_ref[:, margin : margin + rows, margin : margin + cols] = cur_ref[...]
+    src_cols = {-1: slice(0, margin), 0: slice(0, cols), 1: slice(cols - margin, cols)}
+    dst_rows = {-1: slice(margin + rows, 2 * margin + rows), 0: slice(margin, margin + rows), 1: slice(0, margin)}
+    dst_cols = {-1: slice(margin + cols, 2 * margin + cols), 0: slice(margin, margin + cols), 1: slice(0, margin)}
+    copies = []
+    for index, (dr, dc) in enumerate(NEIGHBOURS):
+        copy = pltpu.make_async_remote_copy(
+            src_ref=cur_ref.at[:, :, src_cols[dc]],
+            dst_ref=ext_ref.at[:, dst_rows[dr], dst_cols[dc]],
+            send_sem=send_sems.at[index],
+            recv_sem=recv_sems.at[index],
+            device_id=(me_r + dr, me_c + dc),
+            device_id_type=pl.DeviceIdType.MESH,
         )
-    return jnp.concatenate(
-        [left_edge + from_prev(right_rim, "sy"), inner, right_edge + from_next(left_rim, "sy")],
-        axis=2,
-    )
+        copies.append(copy)
+
+        @pl.when(exists(me_r + dr, me_c + dc, n_r, n_c))
+        def _():
+            copy.start()
+
+        @pl.when(jnp.logical_not(exists(me_r - dr, me_c - dc, n_r, n_c)))
+        def _():
+            region = (slice(None), dst_rows[dr], dst_cols[dc])
+            ext_ref[region] = jnp.zeros(ext_ref[region].shape, jnp.float32)
+
+    for index, (dr, dc) in enumerate(NEIGHBOURS):
+        copy = copies[index]
+
+        @pl.when(exists(me_r + dr, me_c + dc, n_r, n_c))
+        def _():
+            copy.wait_send()
+
+        @pl.when(exists(me_r - dr, me_c - dc, n_r, n_c))
+        def _():
+            copy.wait_recv()
+
+
+def fold_kernel(canvas_ref, out_ref, wide_bufs, narrow_bufs, send_sems, recv_sems):
+    rows = out_ref.shape[1]
+    cols = out_ref.shape[2]
+    margin = (canvas_ref.shape[2] - cols) // 2
+    me_r, me_c, n_r, n_c = mesh_place()
+    src_rows = {-1: slice(0, margin), 0: slice(margin, margin + rows), 1: slice(margin + rows, 2 * margin + rows)}
+    src_cols = {-1: slice(0, margin), 0: slice(margin, margin + cols), 1: slice(margin + cols, 2 * margin + cols)}
+    dst_cols = {-1: slice(cols - margin, cols), 0: slice(0, cols), 1: slice(0, margin)}
+    copies = []
+    wide_index = 0
+    narrow_index = 0
+    for index, (dr, dc) in enumerate(NEIGHBOURS):
+        if dc == 0:
+            buffer = wide_bufs.at[wide_index]
+            wide_index += 1
+        else:
+            buffer = narrow_bufs.at[narrow_index]
+            narrow_index += 1
+        copy = pltpu.make_async_remote_copy(
+            src_ref=canvas_ref.at[:, src_rows[dr], src_cols[dc]],
+            dst_ref=buffer,
+            send_sem=send_sems.at[index],
+            recv_sem=recv_sems.at[index],
+            device_id=(me_r + dr, me_c + dc),
+            device_id_type=pl.DeviceIdType.MESH,
+        )
+        copies.append((copy, buffer))
+
+        @pl.when(exists(me_r + dr, me_c + dc, n_r, n_c))
+        def _():
+            copy.start()
+
+    out_ref[...] = canvas_ref[:, margin : margin + rows, margin : margin + cols]
+    for index, (dr, dc) in enumerate(NEIGHBOURS):
+        copy, buffer = copies[index]
+
+        @pl.when(exists(me_r + dr, me_c + dc, n_r, n_c))
+        def _():
+            copy.wait_send()
+
+        @pl.when(exists(me_r - dr, me_c - dc, n_r, n_c))
+        def _():
+            copy.wait_recv()
+            out_ref[:, :, dst_cols[dc]] += buffer[...]
+
+
+def exchange_halo(current, margin):
+    depth, rows, cols = current.shape
+    return pl.pallas_call(
+        halo_kernel,
+        out_shape=jax.ShapeDtypeStruct((depth, rows + 2 * margin, cols + 2 * margin), jnp.float32),
+        in_specs=[VMEM_SPEC],
+        out_specs=VMEM_SPEC,
+        scratch_shapes=[pltpu.SemaphoreType.DMA((8,)), pltpu.SemaphoreType.DMA((8,))],
+        compiler_params=pltpu.CompilerParams(vmem_limit_bytes=60 * 1024 * 1024, has_side_effects=True),
+    )(current)
+
+
+def exchange_fold(canvas, margin):
+    depth, ext_rows, ext_cols = canvas.shape
+    rows = ext_rows - 2 * margin
+    cols = ext_cols - 2 * margin
+    return pl.pallas_call(
+        fold_kernel,
+        out_shape=jax.ShapeDtypeStruct((depth, rows, cols), jnp.float32),
+        in_specs=[VMEM_SPEC],
+        out_specs=VMEM_SPEC,
+        scratch_shapes=[
+            pltpu.VMEM((2, depth, margin, cols), jnp.float32),
+            pltpu.VMEM((6, depth, margin, margin), jnp.float32),
+            pltpu.SemaphoreType.DMA((8,)),
+            pltpu.SemaphoreType.DMA((8,)),
+        ],
+        compiler_params=pltpu.CompilerParams(vmem_limit_bytes=60 * 1024 * 1024, has_side_effects=True),
+    )(canvas)
 
 
 def on_device(object_field, probe_field, amplitudes, centres, counts):
@@ -272,38 +366,23 @@
     own_amps = amplitudes[0, 0]
     sx_size = lax.axis_size("sx")
     sx_index = lax.axis_index("sx")
-    sy_size = lax.axis_size("sy")
-    sy_index = lax.axis_index("sy")
     column_counts = counts[:, 0]
     sx_positions = jnp.arange(sx_size, dtype=jnp.int32)
     own_count = jnp.sum(jnp.where(sx_positions == sx_index, column_counts, 0))
     ext_shape = (block_rows + size_probe, block_cols + size_probe)
 
-    illumination = fold_canvas(power_canvas(ext_shape, spots, own_count, probe_field), margin, True)[0]
+    power = power_canvas(ext_shape, spots, own_count, probe_field)
     current = object_field
-    wide = jnp.concatenate(
-        [
-            from_prev(current[..., block_cols - margin :], "sy"),
-            current,
-            from_next(current[..., :margin], "sy"),
-        ],
-        axis=2,
-    )
-    col_index = jnp.arange(block_cols + size_probe, dtype=jnp.int32)
-    inside = ((col_index >= margin) | (sy_index > 0)) & (
-        (col_index < block_cols + margin) | (sy_index < sy_size - 1)
-    )
     for sweep_index in range(ITERS):
-        extended = jnp.concatenate([from_prev(wide, "sx"), wide, from_next(wide, "sx")], axis=1)
+        extended = exchange_halo(current, margin)
         canvas = gradient_canvas(ext_shape, spots, own_count, extended, probe_field, own_amps, tables)
-        last = sweep_index == ITERS - 1
-        gradient = fold_canvas(canvas, margin, not last)
-        if last:
-            current = wide[..., margin : margin + block_cols] - gradient / (
-                illumination[:, margin : margin + block_cols] + DAMPING
-            )
+        if sweep_index == 0:
+            folded = exchange_fold(jnp.concatenate([canvas, power], axis=0), margin)
+            illumination = folded[2]
+            gradient = folded[0:2]
         else:
-            wide = jnp.where(inside, wide - gradient / (illumination + DAMPING), 0.0)
+            gradient = exchange_fold(canvas, margin)
+        current = current - gradient / (illumination + DAMPING)
     return current
 
 

time: 181 us -> 196 us (1.083)
  the two profiles are of different devices: /device:TPU:28 before, /device:TPU:25 now
where the time goes in v3:
time: 196 us
  Pallas kernels  184 us (94%)
  other arithmetic  11.6 us (6%)
    pallas_call x2, Pallas kernels, exchange_fold(): pl.pallas_call(fold_kernel, out_shape=jax.ShapeDtypeStruct((depth, rows,...  78 us
    pallas_call x2, Pallas kernels, exchange_halo(): pl.pallas_call(halo_kernel, out_shape=jax.ShapeDtypeStruct((depth, rows +...  71.2 us
    pallas_call x2, Pallas kernels, gradient_canvas(): pl.pallas_call(gradient_kernel, out_shape=jax.ShapeDtypeStruct((2,) + ext...  31.3 us

profile of v3, /device:TPU:25, one launch (start us, length us, event | category | flops | bytes accessed | tf_op | source)
XLA Modules:
  0.0 195.7 jit_solution(720009084164449937)
XLA Ops:
  0.0 1.3 fusion.6
  1.3 1.8 negate_multiply_fusion
  3.1 3.5 %shard_map.57 = f32[1,384,768]{2,1,0:T(8,128)} custom-call(s32[2,2]{1,0:T(2,128)} %bitcast.9, s32[1]{0:T(128)} %bitcast.2.count_ref, f32[2,256,256]{2,1,0:T(8,128)} %probe_ref.5), custom_call_target="tpu_custom_call" | custom-call | tf_op jit(solution)/shard_map/pallas_call | solution.py:215
  6.6 37.4 %shard_map.55.ext_ref = f32[2,384,768]{2,1,0:T(8,128)} custom-call(f32[2,128,512]{2,1,0:T(8,128)} %cur_ref.1), custom_call_target="tpu_custom_call" | custom-call | tf_op jit(solution)/shard_map/pallas_call | solution.py:330
  43.9 0.0 copy-start
  44.0 15.7 %shard_map.56 = f32[2,384,768]{2,1,0:T(8,128)} custom-call(s32[2,2]{1,0:T(2,128)} %bitcast.10, s32[1]{0:T(128)} %bitcast.2.count_ref, f32[2,384,768]{2,1,0:T(8,128)} %shard_map.55.ext_ref, f32[2,256,256]{2,1,0:T(8,128)} %probe_ref.5, f32[2,256,256]{2,1,0:T(8,128)} %bitcast.7, f32[256,256]{1,0:T(8,128)} %get-tuple-element.6.fr_ref, ...), custom_call_target="tpu_custom_call" | custom-call | tf_op jit(solution)/shard_map/pallas_call | solution.py:205
  59.7 0.0 copy-done
  59.7 3.6 %pad_maximum_fusion.canvas_ref = f32[3,384,768]{2,1,0:T(8,128)} fusion(f32[1,384,768]{2,1,0:T(8,128)S(1)} %copy-done, f32[2,384,768]{2,1,0:T(8,128)} %shard_map.56), kind=kLoop, calls=%fused_computation | loop fusion | flops 884736 | bytes 7077888 | tf_op jit(solution)/shard_map/concatenate | solution.py:380
  63.3 0.0 copy-start.2
  63.3 44.1 %shard_map.58 = f32[3,128,512]{2,1,0:T(8,128)} custom-call(f32[3,384,768]{2,1,0:T(8,128)} %pad_maximum_fusion.canvas_ref), custom_call_target="tpu_custom_call" | custom-call | tf_op jit(solution)/shard_map/pallas_call | solution.py:344
  107.5 1.0 add_bitcast_fusion
  108.4 0.0 copy-done.2
  108.4 2.0 divide_subtract_fusion.1.cur_ref
  110.4 33.8 %shard_map.59.ext_ref = f32[2,384,768]{2,1,0:T(8,128)} custom-call(f32[2,128,512]{2,1,0:T(8,128)} %divide_subtract_fusion.1.cur_ref), custom_call_target="tpu_custom_call" | custom-call | tf_op jit(solution)/shard_map/pallas_call | solution.py:330
  144.2 15.6 %shard_map.60.canvas_ref = f32[2,384,768]{2,1,0:T(8,128)} custom-call(s32[2,2]{1,0:T(2,128)} %bitcast.11, s32[1]{0:T(128)} %bitcast.2.count_ref, f32[2,384,768]{2,1,0:T(8,128)} %shard_map.59.ext_ref, f32[2,256,256]{2,1,0:T(8,128)} %probe_ref.5, f32[2,256,256]{2,1,0:T(8,128)} %bitcast.8, f32[256,256]{1,0:T(8,128)} %get-tuple-element.6.fr_ref, ...), custom_call_target="tpu_custom_call" | custom-call | tf_op jit(solution)/shard_map/pallas_call | solution.py:205
  159.8 0.0 copy-start.1
  159.8 33.9 %shard_map.61 = f32[2,128,512]{2,1,0:T(8,128)} custom-call(f32[2,384,768]{2,1,0:T(8,128)} %shard_map.60.canvas_ref), custom_call_target="tpu_custom_call" | custom-call | tf_op jit(solution)/shard_map/pallas_call | solution.py:344
  193.7 0.0 copy-done.1
  193.7 2.0 divide_subtract_fusion
Async XLA Ops:
  43.9 15.7 %copy-start = (f32[1,384,768]{2,1,0:T(8,128)S(1)}, f32[1,384,768]{2,1,0:T(8,128)}, u32[]{:S(2)}) copy-start(f32[1,384,768]{2,1,0:T(8,128)} %shard_map.57) | copy-start | bytes 3538948
  63.3 45.1 %copy-start.2 = (f32[2,128,512]{2,1,0:T(8,128)S(1)}, f32[2,128,512]{2,1,0:T(8,128)}, u32[]{:S(2)}) copy-start(f32[2,128,512]{2,1,0:T(8,128)} %cur_ref.1) | copy-start | bytes 1572868
  159.8 33.9 %copy-start.1 = (f32[2,128,512]{2,1,0:T(8,128)S(1)}, f32[2,128,512]{2,1,0:T(8,128)}, u32[]{:S(2)}) copy-start(f32[2,128,512]{2,1,0:T(8,128)} %divide_subtract_fusion.1.cur_ref) | copy-start | bytes 1572868

commit v4 on v3

--- a/solution.py
+++ b/solution.py
@@ -237,12 +237,29 @@
     return (row_dev >= 0) & (row_dev < row_count) & (col_dev >= 0) & (col_dev < col_count)
 
 
+def neighbour_barrier(me_r, me_c, n_r, n_c):
+    barrier = pltpu.get_barrier_semaphore()
+    greeted = jnp.int32(0)
+    for dr, dc in NEIGHBOURS:
+        present = exists(me_r + dr, me_c + dc, n_r, n_c)
+
+        @pl.when(present)
+        def _():
+            pl.semaphore_signal(
+                barrier, inc=1, device_id=(me_r + dr, me_c + dc), device_id_type=pl.DeviceIdType.MESH
+            )
+
+        greeted = greeted + present.astype(jnp.int32)
+    pl.semaphore_wait(barrier, greeted)
+
+
 def halo_kernel(cur_ref, ext_ref, send_sems, recv_sems):
     rows = cur_ref.shape[1]
     cols = cur_ref.shape[2]
     margin = (ext_ref.shape[2] - cols) // 2
     me_r, me_c, n_r, n_c = mesh_place()
     ext_ref[:, margin : margin + rows, margin : margin + cols] = cur_ref[...]
+    neighbour_barrier(me_r, me_c, n_r, n_c)
     src_cols = {-1: slice(0, margin), 0: slice(0, cols), 1: slice(cols - margin, cols)}
     dst_rows = {-1: slice(margin + rows, 2 * margin + rows), 0: slice(margin, margin + rows), 1: slice(0, margin)}
     dst_cols = {-1: slice(margin + cols, 2 * margin + cols), 0: slice(margin, margin + cols), 1: slice(0, margin)}
@@ -287,6 +304,7 @@
     src_rows = {-1: slice(0, margin), 0: slice(margin, margin + rows), 1: slice(margin + rows, 2 * margin + rows)}
     src_cols = {-1: slice(0, margin), 0: slice(margin, margin + cols), 1: slice(margin + cols, 2 * margin + cols)}
     dst_cols = {-1: slice(cols - margin, cols), 0: slice(0, cols), 1: slice(0, margin)}
+    neighbour_barrier(me_r, me_c, n_r, n_c)
     copies = []
     wide_index = 0
     narrow_index = 0
@@ -333,7 +351,9 @@
         in_specs=[VMEM_SPEC],
         out_specs=VMEM_SPEC,
         scratch_shapes=[pltpu.SemaphoreType.DMA((8,)), pltpu.SemaphoreType.DMA((8,))],
-        compiler_params=pltpu.CompilerParams(vmem_limit_bytes=60 * 1024 * 1024, has_side_effects=True),
+        compiler_params=pltpu.CompilerParams(
+            vmem_limit_bytes=60 * 1024 * 1024, has_side_effects=True, collective_id=0
+        ),
     )(current)
 
 
@@ -352,7 +372,9 @@
             pltpu.SemaphoreType.DMA((8,)),
             pltpu.SemaphoreType.DMA((8,)),
         ],
-        compiler_params=pltpu.CompilerParams(vmem_limit_bytes=60 * 1024 * 1024, has_side_effects=True),
+        compiler_params=pltpu.CompilerParams(
+            vmem_limit_bytes=60 * 1024 * 1024, has_side_effects=True, collective_id=depth
+        ),
     )(canvas)
 
 

time: 196 us -> 152 us (0.78); the launches traced: 196 us -> 150 us
  Pallas kernels: 184 us -> 138 us
    pallas_call x2, Pallas kernels: 71.2 us -> 46.8 us  [exchange_halo(): pl.pallas_call(halo_kernel, out_shape=jax.ShapeDtypeStruct((depth, rows +...]
    pallas_call x2, Pallas kernels: 78 us -> 56.3 us  [exchange_fold(): pl.pallas_call(fold_kernel, out_shape=jax.ShapeDtypeStruct((depth, rows,...]
where the time goes in v4:
time: 152 us; the launch traced here: 150 us
  Pallas kernels  138 us (91%)
  other arithmetic  11.6 us (8%)
    pallas_call x2, Pallas kernels, exchange_fold(): pl.pallas_call(fold_kernel, out_shape=jax.ShapeDtypeStruct((depth, rows,...  56.3 us
    pallas_call x2, Pallas kernels, exchange_halo(): pl.pallas_call(halo_kernel, out_shape=jax.ShapeDtypeStruct((depth, rows +...  46.8 us
    pallas_call x2, Pallas kernels, gradient_canvas(): pl.pallas_call(gradient_kernel, out_shape=jax.ShapeDtypeStruct((2,) + ext...  31.3 us
    sub x2, other arithmetic, on_device(): current = current - gradient / (illumination + DAMPING)  3.9 us
    concatenate x1, other arithmetic, on_device(): folded = exchange_fold(jnp.concatenate([canvas, power], axis=0), margin)  3.64 us
    pallas_call x1, Pallas kernels, power_canvas(): pl.pallas_call(power_kernel, out_shape=jax.ShapeDtypeStruct((1,) + ext_sh...  3.47 us

profile of v4, /device:TPU:25, one launch (start us, length us, event | category | flops | bytes accessed | tf_op | source)
XLA Modules:
  0.0 149.6 jit_solution(6062368630094896282)
XLA Ops:
  0.0 1.3 fusion.6
  1.3 1.8 %negate_multiply_fusion = (f32[256,256]{1,0:T(8,128)}, f32[256,256]{1,0:T(8,128)}) fusion(), kind=kLoop, calls=%fused_computation.10 | loop fusion | flops 1114112 | bytes 524288 | tf_op jit(solution)/shard_map/mul | solution.py:39
  3.1 3.5 %shard_map.57 = f32[1,384,768]{2,1,0:T(8,128)} custom-call(s32[2,2]{1,0:T(2,128)} %bitcast.9, s32[1]{0:T(128)} %bitcast.2.count_ref, f32[2,256,256]{2,1,0:T(8,128)} %probe_ref.5), custom_call_target="tpu_custom_call" | custom-call | tf_op jit(solution)/shard_map/pallas_call | solution.py:215
  6.6 26.8 %shard_map.55.ext_ref = f32[2,384,768]{2,1,0:T(8,128)} custom-call(f32[2,128,512]{2,1,0:T(8,128)} %cur_ref.1), custom_call_target="tpu_custom_call" | custom-call | tf_op jit(solution)/shard_map/pallas_call | solution.py:348
  33.4 0.0 copy-start
  33.4 15.7 %shard_map.56 = f32[2,384,768]{2,1,0:T(8,128)} custom-call(s32[2,2]{1,0:T(2,128)} %bitcast.10, s32[1]{0:T(128)} %bitcast.2.count_ref, f32[2,384,768]{2,1,0:T(8,128)} %shard_map.55.ext_ref, f32[2,256,256]{2,1,0:T(8,128)} %probe_ref.5, f32[2,256,256]{2,1,0:T(8,128)} %bitcast.7, f32[256,256]{1,0:T(8,128)} %get-tuple-element.6.fr_ref, ...), custom_call_target="tpu_custom_call" | custom-call | tf_op jit(solution)/shard_map/pallas_call | solution.py:205
  49.1 0.0 copy-done
  49.1 3.6 %pad_maximum_fusion.canvas_ref = f32[3,384,768]{2,1,0:T(8,128)} fusion(f32[1,384,768]{2,1,0:T(8,128)S(1)} %copy-done, f32[2,384,768]{2,1,0:T(8,128)} %shard_map.56), kind=kLoop, calls=%fused_computation | loop fusion | flops 884736 | bytes 7077888 | tf_op jit(solution)/shard_map/concatenate | solution.py:402
  52.7 0.0 copy-start.2
  52.7 36.0 %shard_map.58 = f32[3,128,512]{2,1,0:T(8,128)} custom-call(f32[3,384,768]{2,1,0:T(8,128)} %pad_maximum_fusion.canvas_ref), custom_call_target="tpu_custom_call" | custom-call | tf_op jit(solution)/shard_map/pallas_call | solution.py:364
  88.7 1.0 add_bitcast_fusion
  89.7 0.0 copy-done.2
  89.7 2.0 %divide_subtract_fusion.1.cur_ref = f32[2,128,512]{2,1,0:T(8,128)} fusion(f32[2,128,512]{2,1,0:T(8,128)S(1)} %copy-done.2, f32[3,128,512]{2,1,0:T(8,128)} %shard_map.58, f32[128,512]{1,0:T(8,128)S(1)} %add_bitcast_fusion), kind=kLoop, calls=%fused_computation.2 | loop fusion | flops 262144 | bytes 1835008 | tf_op jit(solution)/shard_map/sub | solution.py:407
  91.6 20.0 %shard_map.59.ext_ref = f32[2,384,768]{2,1,0:T(8,128)} custom-call(f32[2,128,512]{2,1,0:T(8,128)} %divide_subtract_fusion.1.cur_ref), custom_call_target="tpu_custom_call" | custom-call | tf_op jit(solution)/shard_map/pallas_call | solution.py:348
  111.6 15.6 %shard_map.60.canvas_ref = f32[2,384,768]{2,1,0:T(8,128)} custom-call(s32[2,2]{1,0:T(2,128)} %bitcast.11, s32[1]{0:T(128)} %bitcast.2.count_ref, f32[2,384,768]{2,1,0:T(8,128)} %shard_map.59.ext_ref, f32[2,256,256]{2,1,0:T(8,128)} %probe_ref.5, f32[2,256,256]{2,1,0:T(8,128)} %bitcast.8, f32[256,256]{1,0:T(8,128)} %get-tuple-element.6.fr_ref, ...), custom_call_target="tpu_custom_call" | custom-call | tf_op jit(solution)/shard_map/pallas_call | solution.py:205
  127.3 0.0 copy-start.1
  127.3 20.4 %shard_map.61 = f32[2,128,512]{2,1,0:T(8,128)} custom-call(f32[2,384,768]{2,1,0:T(8,128)} %shard_map.60.canvas_ref), custom_call_target="tpu_custom_call" | custom-call | tf_op jit(solution)/shard_map/pallas_call | solution.py:364
  147.7 0.0 copy-done.1
  147.7 2.0 %divide_subtract_fusion = f32[2,128,512]{2,1,0:T(8,128)} fusion(f32[2,128,512]{2,1,0:T(8,128)S(1)} %copy-done.1, f32[2,128,512]{2,1,0:T(8,128)} %shard_map.61, f32[128,512]{1,0:T(8,128)S(1)} %add_bitcast_fusion), kind=kLoop, calls=%fused_computation.1 | loop fusion | flops 262144 | bytes 1835008 | tf_op jit(solution)/shard_map/sub | solution.py:407
Async XLA Ops:
  33.4 15.7 %copy-start = (f32[1,384,768]{2,1,0:T(8,128)S(1)}, f32[1,384,768]{2,1,0:T(8,128)}, u32[]{:S(2)}) copy-start(f32[1,384,768]{2,1,0:T(8,128)} %shard_map.57) | copy-start | bytes 3538948
  52.7 36.9 %copy-start.2 = (f32[2,128,512]{2,1,0:T(8,128)S(1)}, f32[2,128,512]{2,1,0:T(8,128)}, u32[]{:S(2)}) copy-start(f32[2,128,512]{2,1,0:T(8,128)} %cur_ref.1) | copy-start | bytes 1572868
  127.3 20.4 %copy-start.1 = (f32[2,128,512]{2,1,0:T(8,128)S(1)}, f32[2,128,512]{2,1,0:T(8,128)}, u32[]{:S(2)}) copy-start(f32[2,128,512]{2,1,0:T(8,128)} %divide_subtract_fusion.1.cur_ref) | copy-start | bytes 1572868

commit v5 on v4

--- a/solution.py
+++ b/solution.py
@@ -153,9 +153,24 @@
     return take, put
 
 
-def gradient_kernel(spots_ref, count_ref, ext_ref, probe_ref, amps_ref, fr_ref, fi_ref, out_ref):
+def split_bf16(values):
+    scaled = values * 65537.0
+    high = scaled - (scaled - values)
+    return high.astype(jnp.bfloat16), (values - high).astype(jnp.bfloat16)
+
+
+def dot_split(left_parts, right_parts):
+    left_high, left_low = left_parts
+    right_high, right_low = right_parts
+    total = jnp.dot(left_high, right_high, preferred_element_type=jnp.float32)
+    total += jnp.dot(left_high, right_low, preferred_element_type=jnp.float32)
+    return total + jnp.dot(left_low, right_high, preferred_element_type=jnp.float32)
+
+
+def gradient_kernel(spots_ref, count_ref, ext_ref, probe_ref, amps_ref, tables_ref, out_ref):
     size = probe_ref.shape[1]
     out_ref[...] = jnp.zeros(out_ref.shape, jnp.float32)
+    with_power = out_ref.shape[0] > 2
     for slot in range(amps_ref.shape[0]):
 
         @pl.when(slot < count_ref[0])
@@ -163,25 +178,40 @@
             take, put = window_tools(size, spots_ref[slot, 0], spots_ref[slot, 1])
             probe_real = probe_ref[0]
             probe_imag = probe_ref[1]
-            table_real = fr_ref[...]
-            table_imag = fi_ref[...]
+            real_parts = (tables_ref[0], tables_ref[1])
+            imag_parts = (tables_ref[2], tables_ref[3])
+
+            def left(field_real, field_imag, sign):
+                both = split_bf16(jnp.concatenate([field_real, field_imag], axis=1))
+                by_real = dot_split(real_parts, both)
+                by_imag = dot_split(imag_parts, both)
+                out_real = by_real[:, :size] - sign * by_imag[:, size:]
+                out_imag = by_real[:, size:] + sign * by_imag[:, :size]
+                return out_real, out_imag
+
+            def right(field_real, field_imag, sign):
+                both = split_bf16(jnp.concatenate([field_real, field_imag], axis=0))
+                by_real = dot_split(both, real_parts)
+                by_imag = dot_split(both, imag_parts)
+                out_real = by_real[:size] - sign * by_imag[size:]
+                out_imag = by_imag[:size] * sign + by_real[size:]
+                return out_real, out_imag
+
             obj_real = take(ext_ref, 0)
             obj_imag = take(ext_ref, 1)
             exit_real = probe_real * obj_real - probe_imag * obj_imag
             exit_imag = probe_real * obj_imag + probe_imag * obj_real
-            half_real = dot_exact(table_real, exit_real) - dot_exact(table_imag, exit_imag)
-            half_imag = dot_exact(table_real, exit_imag) + dot_exact(table_imag, exit_real)
-            far_real = dot_exact(half_real, table_real) - dot_exact(half_imag, table_imag)
-            far_imag = dot_exact(half_real, table_imag) + dot_exact(half_imag, table_real)
+            half_real, half_imag = left(exit_real, exit_imag, 1.0)
+            far_real, far_imag = right(half_real, half_imag, 1.0)
             factor = 1.0 - amps_ref[slot] / jnp.sqrt(far_real * far_real + far_imag * far_imag + SMOOTH)
             miss_real = far_real * factor
             miss_imag = far_imag * factor
-            back_real = dot_exact(table_real, miss_real) + dot_exact(table_imag, miss_imag)
-            back_imag = dot_exact(table_real, miss_imag) - dot_exact(table_imag, miss_real)
-            near_real = dot_exact(back_real, table_real) + dot_exact(back_imag, table_imag)
-            near_imag = dot_exact(back_imag, table_real) - dot_exact(back_real, table_imag)
+            back_real, back_imag = left(miss_real, miss_imag, -1.0)
+            near_real, near_imag = right(back_real, back_imag, -1.0)
             put(out_ref, 0, probe_real * near_real + probe_imag * near_imag)
             put(out_ref, 1, probe_real * near_imag - probe_imag * near_real)
+            if with_power:
+                put(out_ref, 2, probe_real * probe_real + probe_imag * probe_imag)
 
 
 def power_kernel(spots_ref, count_ref, probe_ref, out_ref):
@@ -201,14 +231,15 @@
 KERNEL_PARAMS = pltpu.CompilerParams(vmem_limit_bytes=60 * 1024 * 1024)
 
 
-def gradient_canvas(ext_shape, spots, count, extended, probe_field, own_amps, tables):
+def gradient_canvas(channels, ext_shape, spots, count, extended, probe_field, own_amps, tables):
+    parts = jnp.stack(split_bf16(tables[0]) + split_bf16(tables[1]))
     return pl.pallas_call(
         gradient_kernel,
-        out_shape=jax.ShapeDtypeStruct((2,) + ext_shape, jnp.float32),
-        in_specs=[SMEM_SPEC, SMEM_SPEC] + [VMEM_SPEC] * 5,
+        out_shape=jax.ShapeDtypeStruct((channels,) + ext_shape, jnp.float32),
+        in_specs=[SMEM_SPEC, SMEM_SPEC] + [VMEM_SPEC] * 4,
         out_specs=VMEM_SPEC,
         compiler_params=KERNEL_PARAMS,
-    )(spots, count.reshape(1), extended, probe_field, own_amps, tables[0], tables[1])
+    )(spots, count.reshape(1), extended, probe_field, own_amps, parts)
 
 
 def power_canvas(ext_shape, spots, count, probe_field):
@@ -393,18 +424,17 @@
     own_count = jnp.sum(jnp.where(sx_positions == sx_index, column_counts, 0))
     ext_shape = (block_rows + size_probe, block_cols + size_probe)
 
-    power = power_canvas(ext_shape, spots, own_count, probe_field)
     current = object_field
     for sweep_index in range(ITERS):
         extended = exchange_halo(current, margin)
-        canvas = gradient_canvas(ext_shape, spots, own_count, extended, probe_field, own_amps, tables)
+        channels = 3 if sweep_index == 0 else 2
+        canvas = gradient_canvas(
+            channels, ext_shape, spots, own_count, extended, probe_field, own_amps, tables
+        )
+        folded = exchange_fold(canvas, margin)
         if sweep_index == 0:
-            folded = exchange_fold(jnp.concatenate([canvas, power], axis=0), margin)
             illumination = folded[2]
-            gradient = folded[0:2]
-        else:
-            gradient = exchange_fold(canvas, margin)
-        current = current - gradient / (illumination + DAMPING)
+        current = current - folded[0:2] / (illumination + DAMPING)
     return current
 
 

time: 152 us -> 140 us (0.921)
  Pallas kernels: 138 us -> 129 us
  other arithmetic: 11.6 us -> 9.4 us
    pallas_call x3 -> x2, Pallas kernels: 34.8 us -> 17.1 us  [gradient_canvas(): pl.pallas_call(gradient_kernel, out_shape=jax.ShapeDtypeStruct((channels,...]
    pallas_call x2, Pallas kernels: 56.3 us -> 64.1 us  [exchange_fold(): pl.pallas_call(fold_kernel, out_shape=jax.ShapeDtypeStruct((depth, rows,...]
    concatenate x1 -> x0, other arithmetic: 3.64 us -> none  [on_device(): folded = exchange_fold(jnp.concatenate([canvas, power], axis=0), margin)]
    convert_element_type x0 -> x2, other arithmetic: none -> 2.35 us  [split_bf16(): return (high.astype(jnp.bfloat16), (values - high).astype(jnp.bfloat16))]
    mul x1 -> x0, other arithmetic: 1.78 us -> none  [dft_tables(): return (jnp.cos(angles) * scaling, -jnp.sin(angles) * scaling)]
where the time goes in v5:
time: 140 us; the launch traced here: 138 us
  Pallas kernels  129 us (92%)
  other arithmetic  9.4 us (7%)
    pallas_call x2, Pallas kernels, exchange_fold(): pl.pallas_call(fold_kernel, out_shape=jax.ShapeDtypeStruct((depth, rows,...  64.1 us
    pallas_call x2, Pallas kernels, exchange_halo(): pl.pallas_call(halo_kernel, out_shape=jax.ShapeDtypeStruct((depth, rows +...  47.8 us
    pallas_call x2, Pallas kernels, gradient_canvas(): pl.pallas_call(gradient_kernel, out_shape=jax.ShapeDtypeStruct((channels,...  17.1 us
    sub x2, other arithmetic, on_device(): current = current - folded[0:2] / (illumination + DAMPING)  3.92 us

profile of v5, /device:TPU:25, one launch (start us, length us, event | category | flops | bytes accessed | tf_op | source)
XLA Modules:
  0.0 138.4 jit_solution(16371415482983823892)
XLA Ops:
  0.0 1.3 fusion.9
  1.3 1.2 fusion.6
  2.5 1.2 subtract_convert_fusion
  3.7 0.9 pad_maximum_fusion.tables_ref
  4.5 26.8 %shard_map.55.ext_ref = f32[2,384,768]{2,1,0:T(8,128)} custom-call(f32[2,128,512]{2,1,0:T(8,128)} %cur_ref.1), custom_call_target="tpu_custom_call" | custom-call | tf_op jit(solution)/shard_map/pallas_call | solution.py:379
  31.3 8.7 %shard_map.56.canvas_ref = f32[3,384,768]{2,1,0:T(8,128)} custom-call(s32[2,2]{1,0:T(2,128)} %bitcast.9, s32[1]{0:T(128)} %bitcast.2.count_ref, f32[2,384,768]{2,1,0:T(8,128)} %shard_map.55.ext_ref, f32[2,256,256]{2,1,0:T(8,128)} %probe_ref.3, f32[2,256,256]{2,1,0:T(8,128)} %bitcast.7, bf16[4,256,256]{2,1,0:T(8,128)(2,1)} %pad_maximum_fusion.tables_ref), custom_call_target="tpu_custom_call" | custom-call | tf_op jit(solution)/shard_map/pallas_call | solution.py:236
  40.1 0.0 copy-start.1
  40.1 38.2 %shard_map.57 = f32[3,128,512]{2,1,0:T(8,128)} custom-call(f32[3,384,768]{2,1,0:T(8,128)} %shard_map.56.canvas_ref), custom_call_target="tpu_custom_call" | custom-call | tf_op jit(solution)/shard_map/pallas_call | solution.py:395
  78.3 1.0 add_bitcast_fusion
  79.2 0.0 copy-done.1
  79.2 2.0 %divide_subtract_fusion.1.cur_ref = f32[2,128,512]{2,1,0:T(8,128)} fusion(f32[2,128,512]{2,1,0:T(8,128)S(1)} %copy-done.1, f32[3,128,512]{2,1,0:T(8,128)} %shard_map.57, f32[128,512]{1,0:T(8,128)S(1)} %add_bitcast_fusion), kind=kLoop, calls=%fused_computation.2 | loop fusion | flops 262144 | bytes 1835008 | tf_op jit(solution)/shard_map/sub | solution.py:437
  81.2 21.0 %shard_map.58.ext_ref = f32[2,384,768]{2,1,0:T(8,128)} custom-call(f32[2,128,512]{2,1,0:T(8,128)} %divide_subtract_fusion.1.cur_ref), custom_call_target="tpu_custom_call" | custom-call | tf_op jit(solution)/shard_map/pallas_call | solution.py:379
  102.2 8.4 %shard_map.59.canvas_ref = f32[2,384,768]{2,1,0:T(8,128)} custom-call(s32[2,2]{1,0:T(2,128)} %bitcast.10, s32[1]{0:T(128)} %bitcast.2.count_ref, f32[2,384,768]{2,1,0:T(8,128)} %shard_map.58.ext_ref, f32[2,256,256]{2,1,0:T(8,128)} %probe_ref.3, f32[2,256,256]{2,1,0:T(8,128)} %bitcast.8, bf16[4,256,256]{2,1,0:T(8,128)(2,1)} %pad_maximum_fusion.tables_ref), custom_call_target="tpu_custom_call" | custom-call | tf_op jit(solution)/shard_map/pallas_call | solution.py:236
  110.6 0.0 copy-start
  110.6 25.9 %shard_map.60 = f32[2,128,512]{2,1,0:T(8,128)} custom-call(f32[2,384,768]{2,1,0:T(8,128)} %shard_map.59.canvas_ref), custom_call_target="tpu_custom_call" | custom-call | tf_op jit(solution)/shard_map/pallas_call | solution.py:395
  136.5 0.0 copy-done
  136.5 2.0 %divide_subtract_fusion = f32[2,128,512]{2,1,0:T(8,128)} fusion(f32[2,128,512]{2,1,0:T(8,128)S(1)} %copy-done, f32[2,128,512]{2,1,0:T(8,128)} %shard_map.60, f32[128,512]{1,0:T(8,128)S(1)} %add_bitcast_fusion), kind=kLoop, calls=%fused_computation.1 | loop fusion | flops 262144 | bytes 1835008 | tf_op jit(solution)/shard_map/sub | solution.py:437
Async XLA Ops:
  40.1 39.2 %copy-start.1 = (f32[2,128,512]{2,1,0:T(8,128)S(1)}, f32[2,128,512]{2,1,0:T(8,128)}, u32[]{:S(2)}) copy-start(f32[2,128,512]{2,1,0:T(8,128)} %cur_ref.1) | copy-start | bytes 1572868
  110.6 25.9 %copy-start = (f32[2,128,512]{2,1,0:T(8,128)S(1)}, f32[2,128,512]{2,1,0:T(8,128)}, u32[]{:S(2)}) copy-start(f32[2,128,512]{2,1,0:T(8,128)} %divide_subtract_fusion.1.cur_ref) | copy-start | bytes 1572868

commit v6 on v5

--- a/solution.py
+++ b/solution.py
@@ -226,6 +226,23 @@
             put(out_ref, 0, power)
 
 
+def illumination_kernel(corners_ref, live_ref, probe_ref, out_ref, canvas_ref):
+    size = probe_ref.shape[1]
+    rows, cols = out_ref.shape
+    top = 2 * (size // 2)
+    left = cols + size // 2
+    canvas_ref[...] = jnp.zeros(canvas_ref.shape, jnp.float32)
+    power = probe_ref[0] * probe_ref[0] + probe_ref[1] * probe_ref[1]
+    for window in range(live_ref.shape[0]):
+
+        @pl.when(live_ref[window] > 0)
+        def _():
+            _, put = window_tools(size, corners_ref[window, 0], corners_ref[window, 1])
+            put(canvas_ref, 0, power)
+
+    out_ref[...] = canvas_ref[0, top : top + rows, left : left + cols]
+
+
 VMEM_SPEC = pl.BlockSpec(memory_space=pltpu.VMEM)
 SMEM_SPEC = pl.BlockSpec(memory_space=pltpu.SMEM)
 KERNEL_PARAMS = pltpu.CompilerParams(vmem_limit_bytes=60 * 1024 * 1024)
@@ -240,6 +257,44 @@
         out_specs=VMEM_SPEC,
         compiler_params=KERNEL_PARAMS,
     )(spots, count.reshape(1), extended, probe_field, own_amps, parts)
+
+
+def illumination_block(block_shape, centres, counts, probe_field):
+    rows, cols = block_shape
+    size = probe_field.shape[1]
+    margin = size // 2
+    me_r, me_c, n_r, n_c = mesh_place()
+    corners = []
+    live = []
+    for dr in (-1, 0, 1):
+        for dc in (-1, 0, 1):
+            row_dev = me_r + dr
+            col_dev = me_c + dc
+            present = exists(row_dev, col_dev, n_r, n_c)
+            safe_r = jnp.clip(row_dev, 0, n_r - 1)
+            safe_c = jnp.clip(col_dev, 0, n_c - 1)
+            spots = centres[safe_r, safe_c]
+            count = jnp.where(present, counts[safe_r, safe_c], 0)
+            for slot in range(spots.shape[0]):
+                corners.append(
+                    jnp.stack(
+                        [
+                            dr * rows + spots[slot, 0] - margin + 2 * margin,
+                            dc * cols + spots[slot, 1] - margin + cols + margin,
+                        ]
+                    )
+                )
+                live.append((slot < count).astype(jnp.int32))
+    canvas_rows = 2 * rows + margin + size + 8
+    canvas_cols = 3 * cols + size
+    return pl.pallas_call(
+        illumination_kernel,
+        out_shape=jax.ShapeDtypeStruct((rows, cols), jnp.float32),
+        in_specs=[SMEM_SPEC, SMEM_SPEC, VMEM_SPEC],
+        out_specs=VMEM_SPEC,
+        scratch_shapes=[pltpu.VMEM((1, canvas_rows, canvas_cols), jnp.float32)],
+        compiler_params=KERNEL_PARAMS,
+    )(jnp.stack(corners).astype(jnp.int32), jnp.stack(live), probe_field)
 
 
 def power_canvas(ext_shape, spots, count, probe_field):
@@ -415,26 +470,19 @@
     block_rows = object_field.shape[1]
     block_cols = object_field.shape[2]
     tables = dft_tables(size_probe)
-    spots = centres[0, 0]
+    me_r, me_c, _, _ = mesh_place()
+    spots = centres[me_r, me_c]
     own_amps = amplitudes[0, 0]
-    sx_size = lax.axis_size("sx")
-    sx_index = lax.axis_index("sx")
-    column_counts = counts[:, 0]
-    sx_positions = jnp.arange(sx_size, dtype=jnp.int32)
-    own_count = jnp.sum(jnp.where(sx_positions == sx_index, column_counts, 0))
+    own_count = counts[me_r, me_c]
     ext_shape = (block_rows + size_probe, block_cols + size_probe)
 
+    illumination = illumination_block((block_rows, block_cols), centres, counts, probe_field)
     current = object_field
     for sweep_index in range(ITERS):
         extended = exchange_halo(current, margin)
-        channels = 3 if sweep_index == 0 else 2
-        canvas = gradient_canvas(
-            channels, ext_shape, spots, own_count, extended, probe_field, own_amps, tables
-        )
-        folded = exchange_fold(canvas, margin)
-        if sweep_index == 0:
-            illumination = folded[2]
-        current = current - folded[0:2] / (illumination + DAMPING)
+        canvas = gradient_canvas(2, ext_shape, spots, own_count, extended, probe_field, own_amps, tables)
+        gradient = exchange_fold(canvas, margin)
+        current = current - gradient / (illumination + DAMPING)
     return current
 
 
@@ -446,8 +494,8 @@
             P(None, "sx", "sy"),
             P(),
             P("sx", "sy", None, None, None),
-            P("sx", "sy", None, None),
-            P(None, "sy"),
+            P(),
+            P(),
         ),
         out_specs=P(None, "sx", "sy"),
         check_vma=False,

time: 140 us -> 796 us (5.69)
  blocking collectives: 0 us -> 607 us
  between operations: 0.07 us -> 20.9 us
  local copies, waits for them, and re-layouts: 0.01 us -> 9.14 us
    another operation x0 -> x1, blocking collectives: none -> 595 us
    pallas_call x2, Pallas kernels: 47.8 us -> 67.4 us  [exchange_halo(): pl.pallas_call(halo_kernel, out_shape=jax.ShapeDtypeStruct((depth, rows +...]
    pallas_call x2, Pallas kernels: 64.1 us -> 45.7 us  [exchange_fold(): pl.pallas_call(fold_kernel, out_shape=jax.ShapeDtypeStruct((depth, rows,...]
    unnamed x0 -> x1, blocking collectives: none -> 11.7 us
    another operation x0 -> x10, other arithmetic: none -> 9.03 us  [the longest x9 8.5 us: illumination_block(): jnp.stack(corners).astype(jnp.int32)]
where the time goes in v6:
time: 796 us; the launch traced here: 790 us
  blocking collectives  607 us (76%)
  Pallas kernels  136 us (17%)
  between operations  20.9 us (3%)
  other arithmetic  17.1 us (2%)
  local copies, waits for them, and re-layouts  9.14 us (1%)
    another operation x1, blocking collectives  595 us
    pallas_call x2, Pallas kernels, exchange_halo(): pl.pallas_call(halo_kernel, out_shape=jax.ShapeDtypeStruct((depth, rows +...  67.4 us
    pallas_call x2, Pallas kernels, exchange_fold(): pl.pallas_call(fold_kernel, out_shape=jax.ShapeDtypeStruct((depth, rows,...  45.7 us
    pallas_call x2, Pallas kernels, gradient_canvas(): pl.pallas_call(gradient_kernel, out_shape=jax.ShapeDtypeStruct((channels,...  16.8 us

profile of v6, /device:TPU:25, one launch (start us, length us, event | category | flops | bytes accessed | tf_op | source)
XLA Modules:
  0.0 789.7 jit_solution(13769998417709747831)
XLA Ops:
  0.0 11.7 %all-gather.3 = s32[8,1,32]{2,1,0:T(1,128)S(1)} all-gather(s32[1,1,32]{2,1,0:T(1,128)} %bitcast.130), channel_id=2, replica_groups=mesh['sx'=32,'sy'=8] {'sy'}, dimensions={0}, use_global_device_ids=true | all-gather | bytes 1152 | tf_op args[4]
  11.7 0.7 constant_dynamic-slice_fusion
  18.7 595.1 %all-gather.2 = s32[256,1,2,2]{3,2,1,0:T(2,128)S(1)} all-gather(s32[1,1,2,2]{3,2,1,0:T(2,128)} %param.8), channel_id=3, replica_groups=mesh['sx'=32,'sy'=8] {'sx','sy'}, dimensions={0}, use_global_device_ids=true | all-gather | bytes 4112 | tf_op jit(solution)/call_exported
  624.2 0.7 fusion.24
  626.1 1.4 add_bitcast_fusion.6
  629.4 1.4 add_bitcast_fusion.4
  632.8 1.4 add_bitcast_fusion.2
  634.2 0.7 fusion.27
  634.9 2.6 add_bitcast_fusion
  639.4 1.4 add_bitcast_fusion.12
  644.0 1.8 stack.381.corners_ref
  645.8 5.8 shard_map.58
  651.6 1.0 broadcast_add_fusion
  652.5 1.2 fusion.6
  653.7 1.2 subtract_convert_fusion
  654.9 0.9 pad_maximum_fusion.tables_ref
  655.8 41.0 %shard_map.55.ext_ref = f32[2,384,768]{2,1,0:T(8,128)} custom-call(f32[2,128,512]{2,1,0:T(8,128)} %cur_ref.1), custom_call_target="tpu_custom_call" | custom-call | tf_op jit(solution)/shard_map/pallas_call | solution.py:434
  696.8 8.4 %shard_map.56.canvas_ref = f32[2,384,768]{2,1,0:T(8,128)} custom-call(s32[2,2]{1,0:T(2,128)} %fusion.9.spots_ref, s32[1]{0:T(128)} %bitcast.4.count_ref, f32[2,384,768]{2,1,0:T(8,128)} %shard_map.55.ext_ref, f32[2,256,256]{2,1,0:T(8,128)} %probe_ref.5, f32[2,256,256]{2,1,0:T(8,128)} %bitcast.126, bf16[4,256,256]{2,1,0:T(8,128)(2,1)} %pad_maximum_fusion.tables_ref), custom_call_target="tpu_custom_call" | custom-call | tf_op jit(solution)/shard_map/pallas_call | solution.py:253
  705.2 25.0 %shard_map.57 = f32[2,128,512]{2,1,0:T(8,128)} custom-call(f32[2,384,768]{2,1,0:T(8,128)} %shard_map.56.canvas_ref), custom_call_target="tpu_custom_call" | custom-call | tf_op jit(solution)/shard_map/pallas_call | solution.py:450
  730.2 1.9 divide_subtract_fusion.1.cur_ref
  732.2 26.4 %shard_map.59.ext_ref = f32[2,384,768]{2,1,0:T(8,128)} custom-call(f32[2,128,512]{2,1,0:T(8,128)} %divide_subtract_fusion.1.cur_ref), custom_call_target="tpu_custom_call" | custom-call | tf_op jit(solution)/shard_map/pallas_call | solution.py:434
  758.5 8.4 %shard_map.60.canvas_ref = f32[2,384,768]{2,1,0:T(8,128)} custom-call(s32[2,2]{1,0:T(2,128)} %fusion.9.spots_ref, s32[1]{0:T(128)} %bitcast.4.count_ref, f32[2,384,768]{2,1,0:T(8,128)} %shard_map.59.ext_ref, f32[2,256,256]{2,1,0:T(8,128)} %probe_ref.5, f32[2,256,256]{2,1,0:T(8,128)} %bitcast.127, bf16[4,256,256]{2,1,0:T(8,128)(2,1)} %pad_maximum_fusion.tables_ref), custom_call_target="tpu_custom_call" | custom-call | tf_op jit(solution)/shard_map/pallas_call | solution.py:253
  767.0 20.7 %shard_map.61 = f32[2,128,512]{2,1,0:T(8,128)} custom-call(f32[2,384,768]{2,1,0:T(8,128)} %shard_map.60.canvas_ref), custom_call_target="tpu_custom_call" | custom-call | tf_op jit(solution)/shard_map/pallas_call | solution.py:450
  787.7 2.0 divide_subtract_fusion
  (19 shorter events, 6.1 us)
Async XLA Ops:
  705.2 25.0 %copy-start.1 = (f32[2,128,512]{2,1,0:T(8,128)S(1)}, f32[2,128,512]{2,1,0:T(8,128)}, u32[]{:S(2)}) copy-start(f32[2,128,512]{2,1,0:T(8,128)} %cur_ref.1) | copy-start | bytes 1572868
  767.0 20.7 %copy-start = (f32[2,128,512]{2,1,0:T(8,128)S(1)}, f32[2,128,512]{2,1,0:T(8,128)}, u32[]{:S(2)}) copy-start(f32[2,128,512]{2,1,0:T(8,128)} %divide_subtract_fusion.1.cur_ref) | copy-start | bytes 1572868

commit v7 on v5

--- a/solution.py
+++ b/solution.py
@@ -252,9 +252,6 @@
     )(spots, count.reshape(1), probe_field)
 
 
-NEIGHBOURS = [(-1, -1), (-1, 0), (-1, 1), (0, -1), (0, 1), (1, -1), (1, 0), (1, 1)]
-
-
 def mesh_place():
     return (
         lax.axis_index("sx"),
@@ -268,10 +265,14 @@
     return (row_dev >= 0) & (row_dev < row_count) & (col_dev >= 0) & (col_dev < col_count)
 
 
+ROW_NEIGHBOURS = [(-1, 0), (1, 0)]
+COL_NEIGHBOURS = [(0, -1), (0, 1)]
+
+
 def neighbour_barrier(me_r, me_c, n_r, n_c):
     barrier = pltpu.get_barrier_semaphore()
     greeted = jnp.int32(0)
-    for dr, dc in NEIGHBOURS:
+    for dr, dc in ROW_NEIGHBOURS + COL_NEIGHBOURS:
         present = exists(me_r + dr, me_c + dc, n_r, n_c)
 
         @pl.when(present)
@@ -284,21 +285,13 @@
     pl.semaphore_wait(barrier, greeted)
 
 
-def halo_kernel(cur_ref, ext_ref, send_sems, recv_sems):
-    rows = cur_ref.shape[1]
-    cols = cur_ref.shape[2]
-    margin = (ext_ref.shape[2] - cols) // 2
-    me_r, me_c, n_r, n_c = mesh_place()
-    ext_ref[:, margin : margin + rows, margin : margin + cols] = cur_ref[...]
-    neighbour_barrier(me_r, me_c, n_r, n_c)
-    src_cols = {-1: slice(0, margin), 0: slice(0, cols), 1: slice(cols - margin, cols)}
-    dst_rows = {-1: slice(margin + rows, 2 * margin + rows), 0: slice(margin, margin + rows), 1: slice(0, margin)}
-    dst_cols = {-1: slice(margin + cols, 2 * margin + cols), 0: slice(margin, margin + cols), 1: slice(0, margin)}
+def swap(place, pieces, send_sems, recv_sems):
+    me_r, me_c, n_r, n_c = place
     copies = []
-    for index, (dr, dc) in enumerate(NEIGHBOURS):
+    for index, ((dr, dc), source, target) in enumerate(pieces):
         copy = pltpu.make_async_remote_copy(
-            src_ref=cur_ref.at[:, :, src_cols[dc]],
-            dst_ref=ext_ref.at[:, dst_rows[dr], dst_cols[dc]],
+            src_ref=source,
+            dst_ref=target,
             send_sem=send_sems.at[index],
             recv_sem=recv_sems.at[index],
             device_id=(me_r + dr, me_c + dc),
@@ -310,68 +303,103 @@
         def _():
             copy.start()
 
+    for index, ((dr, dc), _, _) in enumerate(pieces):
+        copy = copies[index]
+
+        @pl.when(exists(me_r + dr, me_c + dc, n_r, n_c))
+        def _():
+            copy.wait_send()
+
+        @pl.when(exists(me_r - dr, me_c - dc, n_r, n_c))
+        def _():
+            copy.wait_recv()
+
+
+def halo_kernel(cur_ref, ext_ref, send_sems, recv_sems):
+    rows = cur_ref.shape[1]
+    cols = cur_ref.shape[2]
+    margin = (ext_ref.shape[2] - cols) // 2
+    place = mesh_place()
+    me_r, me_c, n_r, n_c = place
+    middle = slice(margin, margin + rows)
+    ext_ref[:, middle, margin : margin + cols] = cur_ref[...]
+    unreached = [
+        ((0, 1), (slice(None), middle, slice(0, margin))),
+        ((0, -1), (slice(None), middle, slice(margin + cols, 2 * margin + cols))),
+        ((1, 0), (slice(None), slice(0, margin), slice(None))),
+        ((-1, 0), (slice(None), slice(margin + rows, 2 * margin + rows), slice(None))),
+    ]
+    for (dr, dc), region in unreached:
+
         @pl.when(jnp.logical_not(exists(me_r - dr, me_c - dc, n_r, n_c)))
         def _():
-            region = (slice(None), dst_rows[dr], dst_cols[dc])
             ext_ref[region] = jnp.zeros(ext_ref[region].shape, jnp.float32)
 
-    for index, (dr, dc) in enumerate(NEIGHBOURS):
-        copy = copies[index]
-
-        @pl.when(exists(me_r + dr, me_c + dc, n_r, n_c))
-        def _():
-            copy.wait_send()
-
-        @pl.when(exists(me_r - dr, me_c - dc, n_r, n_c))
-        def _():
-            copy.wait_recv()
-
-
-def fold_kernel(canvas_ref, out_ref, wide_bufs, narrow_bufs, send_sems, recv_sems):
+    neighbour_barrier(me_r, me_c, n_r, n_c)
+    swap(
+        place,
+        [
+            ((0, -1), cur_ref.at[:, :, 0:margin], ext_ref.at[:, middle, margin + cols : 2 * margin + cols]),
+            ((0, 1), cur_ref.at[:, :, cols - margin : cols], ext_ref.at[:, middle, 0:margin]),
+        ],
+        send_sems.at[0:2],
+        recv_sems.at[0:2],
+    )
+    swap(
+        place,
+        [
+            ((-1, 0), ext_ref.at[:, middle, :], ext_ref.at[:, margin + rows : 2 * margin + rows, :]),
+            ((1, 0), ext_ref.at[:, middle, :], ext_ref.at[:, 0:margin, :]),
+        ],
+        send_sems.at[2:4],
+        recv_sems.at[2:4],
+    )
+
+
+def fold_kernel(canvas_ref, out_ref, row_bufs, col_bufs, band_ref, send_sems, recv_sems):
     rows = out_ref.shape[1]
     cols = out_ref.shape[2]
     margin = (canvas_ref.shape[2] - cols) // 2
-    me_r, me_c, n_r, n_c = mesh_place()
-    src_rows = {-1: slice(0, margin), 0: slice(margin, margin + rows), 1: slice(margin + rows, 2 * margin + rows)}
-    src_cols = {-1: slice(0, margin), 0: slice(margin, margin + cols), 1: slice(margin + cols, 2 * margin + cols)}
-    dst_cols = {-1: slice(cols - margin, cols), 0: slice(0, cols), 1: slice(0, margin)}
+    place = mesh_place()
+    me_r, me_c, n_r, n_c = place
     neighbour_barrier(me_r, me_c, n_r, n_c)
-    copies = []
-    wide_index = 0
-    narrow_index = 0
-    for index, (dr, dc) in enumerate(NEIGHBOURS):
-        if dc == 0:
-            buffer = wide_bufs.at[wide_index]
-            wide_index += 1
-        else:
-            buffer = narrow_bufs.at[narrow_index]
-            narrow_index += 1
-        copy = pltpu.make_async_remote_copy(
-            src_ref=canvas_ref.at[:, src_rows[dr], src_cols[dc]],
-            dst_ref=buffer,
-            send_sem=send_sems.at[index],
-            recv_sem=recv_sems.at[index],
-            device_id=(me_r + dr, me_c + dc),
-            device_id_type=pl.DeviceIdType.MESH,
-        )
-        copies.append((copy, buffer))
-
-        @pl.when(exists(me_r + dr, me_c + dc, n_r, n_c))
-        def _():
-            copy.start()
-
-    out_ref[...] = canvas_ref[:, margin : margin + rows, margin : margin + cols]
-    for index, (dr, dc) in enumerate(NEIGHBOURS):
-        copy, buffer = copies[index]
-
-        @pl.when(exists(me_r + dr, me_c + dc, n_r, n_c))
-        def _():
-            copy.wait_send()
-
-        @pl.when(exists(me_r - dr, me_c - dc, n_r, n_c))
-        def _():
-            copy.wait_recv()
-            out_ref[:, :, dst_cols[dc]] += buffer[...]
+    swap(
+        place,
+        [
+            ((-1, 0), canvas_ref.at[:, 0:margin, :], row_bufs.at[0]),
+            ((1, 0), canvas_ref.at[:, margin + rows : 2 * margin + rows, :], row_bufs.at[1]),
+        ],
+        send_sems.at[0:2],
+        recv_sems.at[0:2],
+    )
+    band_ref[...] = canvas_ref[:, margin : margin + rows, :]
+
+    @pl.when(exists(me_r + 1, me_c, n_r, n_c))
+    def _():
+        band_ref[...] += row_bufs[0]
+
+    @pl.when(exists(me_r - 1, me_c, n_r, n_c))
+    def _():
+        band_ref[...] += row_bufs[1]
+
+    swap(
+        place,
+        [
+            ((0, -1), band_ref.at[:, :, 0:margin], col_bufs.at[0]),
+            ((0, 1), band_ref.at[:, :, margin + cols : 2 * margin + cols], col_bufs.at[1]),
+        ],
+        send_sems.at[2:4],
+        recv_sems.at[2:4],
+    )
+    out_ref[...] = band_ref[:, :, margin : margin + cols]
+
+    @pl.when(exists(me_r, me_c + 1, n_r, n_c))
+    def _():
+        out_ref[:, :, cols - margin : cols] += col_bufs[0]
+
+    @pl.when(exists(me_r, me_c - 1, n_r, n_c))
+    def _():
+        out_ref[:, :, 0:margin] += col_bufs[1]
 
 
 def exchange_halo(current, margin):
@@ -381,7 +409,7 @@
         out_shape=jax.ShapeDtypeStruct((depth, rows + 2 * margin, cols + 2 * margin), jnp.float32),
         in_specs=[VMEM_SPEC],
         out_specs=VMEM_SPEC,
-        scratch_shapes=[pltpu.SemaphoreType.DMA((8,)), pltpu.SemaphoreType.DMA((8,))],
+        scratch_shapes=[pltpu.SemaphoreType.DMA((4,)), pltpu.SemaphoreType.DMA((4,))],
         compiler_params=pltpu.CompilerParams(
             vmem_limit_bytes=60 * 1024 * 1024, has_side_effects=True, collective_id=0
         ),
@@ -398,10 +426,11 @@
         in_specs=[VMEM_SPEC],
         out_specs=VMEM_SPEC,
         scratch_shapes=[
-            pltpu.VMEM((2, depth, margin, cols), jnp.float32),
-            pltpu.VMEM((6, depth, margin, margin), jnp.float32),
-            pltpu.SemaphoreType.DMA((8,)),
-            pltpu.SemaphoreType.DMA((8,)),
+            pltpu.VMEM((2, depth, margin, ext_cols), jnp.float32),
+            pltpu.VMEM((2, depth, rows, margin), jnp.float32),
+            pltpu.VMEM((depth, rows, ext_cols), jnp.float32),
+            pltpu.SemaphoreType.DMA((4,)),
+            pltpu.SemaphoreType.DMA((4,)),
         ],
         compiler_params=pltpu.CompilerParams(
             vmem_limit_bytes=60 * 1024 * 1024, has_side_effects=True, collective_id=depth

time: 140 us -> 137 us (0.979)
  the two profiles are of different devices: /device:TPU:25 before, /device:TPU:30 now
where the time goes in v7:
time: 137 us
  Pallas kernels  127 us (93%)
  other arithmetic  9.4 us (7%)
    pallas_call x2, Pallas kernels, exchange_fold(): pl.pallas_call(fold_kernel, out_shape=jax.ShapeDtypeStruct((depth, rows,...  52.3 us
    pallas_call x2, Pallas kernels, exchange_halo(): pl.pallas_call(halo_kernel, out_shape=jax.ShapeDtypeStruct((depth, rows +...  49.6 us
    pallas_call x2, Pallas kernels, gradient_canvas(): pl.pallas_call(gradient_kernel, out_shape=jax.ShapeDtypeStruct((channels,...  25.2 us
    sub x2, other arithmetic, on_device(): current = current - folded[0:2] / (illumination + DAMPING)  3.92 us

profile of v7, /device:TPU:30, one launch (start us, length us, event | category | flops | bytes accessed | tf_op | source)
XLA Modules:
  0.0 136.6 jit_solution(11807232107810564893)
XLA Ops:
  0.0 1.3 fusion.9
  1.3 1.2 fusion.6
  2.5 1.2 subtract_convert_fusion
  3.7 0.9 pad_maximum_fusion.tables_ref
  4.5 25.8 %shard_map.55.ext_ref = f32[2,384,768]{2,1,0:T(8,128)} custom-call(f32[2,128,512]{2,1,0:T(8,128)} %cur_ref.1), custom_call_target="tpu_custom_call" | custom-call | tf_op jit(solution)/shard_map/pallas_call | solution.py:407
  30.3 12.8 %shard_map.56.canvas_ref = f32[3,384,768]{2,1,0:T(8,128)} custom-call(s32[2,2]{1,0:T(2,128)} %bitcast.9, s32[1]{0:T(128)} %bitcast.2.count_ref, f32[2,384,768]{2,1,0:T(8,128)} %shard_map.55.ext_ref, f32[2,256,256]{2,1,0:T(8,128)} %probe_ref.3, f32[2,256,256]{2,1,0:T(8,128)} %bitcast.7, bf16[4,256,256]{2,1,0:T(8,128)(2,1)} %pad_maximum_fusion.tables_ref), custom_call_target="tpu_custom_call" | custom-call | tf_op jit(solution)/shard_map/pallas_call | solution.py:236
  43.1 0.0 copy-start.1
  43.2 29.2 %shard_map.57 = f32[3,128,512]{2,1,0:T(8,128)} custom-call(f32[3,384,768]{2,1,0:T(8,128)} %shard_map.56.canvas_ref), custom_call_target="tpu_custom_call" | custom-call | tf_op jit(solution)/shard_map/pallas_call | solution.py:423
  72.3 1.0 add_bitcast_fusion
  73.3 0.0 copy-done.1
  73.3 2.0 %divide_subtract_fusion.1.cur_ref = f32[2,128,512]{2,1,0:T(8,128)} fusion(f32[2,128,512]{2,1,0:T(8,128)S(1)} %copy-done.1, f32[3,128,512]{2,1,0:T(8,128)} %shard_map.57, f32[128,512]{1,0:T(8,128)S(1)} %add_bitcast_fusion), kind=kLoop, calls=%fused_computation.2 | loop fusion | flops 262144 | bytes 1835008 | tf_op jit(solution)/shard_map/sub | solution.py:466
  75.3 23.9 %shard_map.58.ext_ref = f32[2,384,768]{2,1,0:T(8,128)} custom-call(f32[2,128,512]{2,1,0:T(8,128)} %divide_subtract_fusion.1.cur_ref), custom_call_target="tpu_custom_call" | custom-call | tf_op jit(solution)/shard_map/pallas_call | solution.py:407
  99.1 12.3 %shard_map.59.canvas_ref = f32[2,384,768]{2,1,0:T(8,128)} custom-call(s32[2,2]{1,0:T(2,128)} %bitcast.10, s32[1]{0:T(128)} %bitcast.2.count_ref, f32[2,384,768]{2,1,0:T(8,128)} %shard_map.58.ext_ref, f32[2,256,256]{2,1,0:T(8,128)} %probe_ref.3, f32[2,256,256]{2,1,0:T(8,128)} %bitcast.8, bf16[4,256,256]{2,1,0:T(8,128)(2,1)} %pad_maximum_fusion.tables_ref), custom_call_target="tpu_custom_call" | custom-call | tf_op jit(solution)/shard_map/pallas_call | solution.py:236
  111.5 0.0 copy-start
  111.5 23.1 %shard_map.60 = f32[2,128,512]{2,1,0:T(8,128)} custom-call(f32[2,384,768]{2,1,0:T(8,128)} %shard_map.59.canvas_ref), custom_call_target="tpu_custom_call" | custom-call | tf_op jit(solution)/shard_map/pallas_call | solution.py:423
  134.6 0.0 copy-done
  134.6 2.0 %divide_subtract_fusion = f32[2,128,512]{2,1,0:T(8,128)} fusion(f32[2,128,512]{2,1,0:T(8,128)S(1)} %copy-done, f32[2,128,512]{2,1,0:T(8,128)} %shard_map.60, f32[128,512]{1,0:T(8,128)S(1)} %add_bitcast_fusion), kind=kLoop, calls=%fused_computation.1 | loop fusion | flops 262144 | bytes 1835008 | tf_op jit(solution)/shard_map/sub | solution.py:466
Async XLA Ops:
  43.1 30.1 %copy-start.1 = (f32[2,128,512]{2,1,0:T(8,128)S(1)}, f32[2,128,512]{2,1,0:T(8,128)}, u32[]{:S(2)}) copy-start(f32[2,128,512]{2,1,0:T(8,128)} %cur_ref.1) | copy-start | bytes 1572868
  111.5 23.1 %copy-start = (f32[2,128,512]{2,1,0:T(8,128)S(1)}, f32[2,128,512]{2,1,0:T(8,128)}, u32[]{:S(2)}) copy-start(f32[2,128,512]{2,1,0:T(8,128)} %divide_subtract_fusion.1.cur_ref) | copy-start | bytes 1572868

commit v8 on v7

--- a/solution.py
+++ b/solution.py
@@ -402,6 +402,119 @@
         out_ref[:, :, 0:margin] += col_bufs[1]
 
 
+def fold_step_kernel(canvas_ref, cur_ref, ext_ref, light_ref, row_bufs, col_bufs, edge_bufs, band_ref, send_sems, recv_sems):
+    depth = canvas_ref.shape[0]
+    rows = cur_ref.shape[1]
+    cols = cur_ref.shape[2]
+    margin = (canvas_ref.shape[2] - cols) // 2
+    place = mesh_place()
+    me_r, me_c, n_r, n_c = place
+    for dr, region in ((1, slice(0, margin)), (-1, slice(margin + rows, 2 * margin + rows))):
+
+        @pl.when(jnp.logical_not(exists(me_r - dr, me_c, n_r, n_c)))
+        def _():
+            ext_ref[:, region, :] = jnp.zeros(ext_ref[:, region, :].shape, jnp.float32)
+
+    for side, present in ((0, exists(me_r, me_c + 1, n_r, n_c)), (1, exists(me_r, me_c - 1, n_r, n_c))):
+
+        @pl.when(jnp.logical_not(present))
+        def _():
+            col_bufs[side] = jnp.zeros(col_bufs.shape[1:], jnp.float32)
+            edge_bufs[side] = jnp.zeros(edge_bufs.shape[1:], jnp.float32)
+
+    neighbour_barrier(me_r, me_c, n_r, n_c)
+    swap(
+        place,
+        [
+            ((-1, 0), canvas_ref.at[:, 0:margin, :], row_bufs.at[0]),
+            ((1, 0), canvas_ref.at[:, margin + rows : 2 * margin + rows, :], row_bufs.at[1]),
+        ],
+        send_sems.at[0:2],
+        recv_sems.at[0:2],
+    )
+    band_ref[...] = canvas_ref[:, margin : margin + rows, :]
+
+    @pl.when(exists(me_r + 1, me_c, n_r, n_c))
+    def _():
+        band_ref[...] += row_bufs[0]
+
+    @pl.when(exists(me_r - 1, me_c, n_r, n_c))
+    def _():
+        band_ref[...] += row_bufs[1]
+
+    ext_cols = cols + 2 * margin
+    swap(
+        place,
+        [
+            ((0, -1), band_ref.at[:, :, 0 : 2 * margin], col_bufs.at[0]),
+            ((0, 1), band_ref.at[:, :, ext_cols - 2 * margin : ext_cols], col_bufs.at[1]),
+            ((0, -1), cur_ref.at[:, :, 0:margin], edge_bufs.at[0]),
+            ((0, 1), cur_ref.at[:, :, cols - margin : cols], edge_bufs.at[1]),
+        ],
+        send_sems.at[2:6],
+        recv_sems.at[2:6],
+    )
+    has_left = exists(me_r, me_c - 1, n_r, n_c)
+    has_right = exists(me_r, me_c + 1, n_r, n_c)
+    from_right = jnp.where(has_right, col_bufs[0], 0.0)
+    from_left = jnp.where(has_left, col_bufs[1], 0.0)
+    band = band_ref[...]
+    total = jnp.concatenate(
+        [
+            band[:, :, 0:margin] + from_left[:, :, 0:margin],
+            band[:, :, margin : 2 * margin] + from_left[:, :, margin:],
+            band[:, :, 2 * margin : ext_cols - 2 * margin],
+            band[:, :, ext_cols - 2 * margin : ext_cols - margin] + from_right[:, :, 0:margin],
+            band[:, :, ext_cols - margin :] + from_right[:, :, margin:],
+        ],
+        axis=2,
+    )
+    light = total[depth - 1]
+    values = jnp.concatenate([edge_bufs[1], cur_ref[...], edge_bufs[0]], axis=2)
+    updated = values - total[0 : depth - 1] / (light + DAMPING)
+    col_index = lax.broadcasted_iota(jnp.int32, updated.shape, 2)
+    inside = ((col_index >= margin) | has_left) & ((col_index < margin + cols) | has_right)
+    middle = slice(margin, margin + rows)
+    ext_ref[:, middle, :] = jnp.where(inside, updated, 0.0)
+    light_ref[...] = light[:, margin : margin + cols]
+    swap(
+        place,
+        [
+            ((-1, 0), ext_ref.at[:, middle, :], ext_ref.at[:, margin + rows : 2 * margin + rows, :]),
+            ((1, 0), ext_ref.at[:, middle, :], ext_ref.at[:, 0:margin, :]),
+        ],
+        send_sems.at[6:8],
+        recv_sems.at[6:8],
+    )
+
+
+def fold_and_step(canvas, current, margin):
+    depth, ext_rows, ext_cols = canvas.shape
+    rows = ext_rows - 2 * margin
+    cols = ext_cols - 2 * margin
+    fields = current.shape[0]
+    return pl.pallas_call(
+        fold_step_kernel,
+        out_shape=(
+            jax.ShapeDtypeStruct((fields, ext_rows, ext_cols), jnp.float32),
+            jax.ShapeDtypeStruct((rows, cols), jnp.float32),
+        ),
+        in_specs=[VMEM_SPEC, VMEM_SPEC],
+        out_specs=(VMEM_SPEC, VMEM_SPEC),
+        scratch_shapes=[
+            pltpu.VMEM((2, depth, margin, ext_cols), jnp.float32),
+            pltpu.VMEM((2, depth, rows, 2 * margin), jnp.float32),
+            pltpu.VMEM((2, fields, rows, margin), jnp.float32),
+            pltpu.VMEM((depth, rows, ext_cols), jnp.float32),
+            pltpu.SemaphoreType.DMA((8,)),
+            pltpu.SemaphoreType.DMA((8,)),
+        ],
+        compiler_params=pltpu.CompilerParams(
+            vmem_limit_bytes=60 * 1024 * 1024, has_side_effects=True, collective_id=5
+        ),
+    )(canvas, current)
+
+
 def exchange_halo(current, margin):
     depth, rows, cols = current.shape
     return pl.pallas_call(
@@ -453,17 +566,16 @@
     own_count = jnp.sum(jnp.where(sx_positions == sx_index, column_counts, 0))
     ext_shape = (block_rows + size_probe, block_cols + size_probe)
 
-    current = object_field
-    for sweep_index in range(ITERS):
-        extended = exchange_halo(current, margin)
-        channels = 3 if sweep_index == 0 else 2
-        canvas = gradient_canvas(
-            channels, ext_shape, spots, own_count, extended, probe_field, own_amps, tables
-        )
-        folded = exchange_fold(canvas, margin)
-        if sweep_index == 0:
-            illumination = folded[2]
-        current = current - folded[0:2] / (illumination + DAMPING)
+    extended = exchange_halo(object_field, margin)
+    canvas = gradient_canvas(3, ext_shape, spots, own_count, extended, probe_field, own_amps, tables)
+    extended, illumination = fold_and_step(canvas, object_field, margin)
+    for sweep_index in range(1, ITERS):
+        canvas = gradient_canvas(2, ext_shape, spots, own_count, extended, probe_field, own_amps, tables)
+        gradient = exchange_fold(canvas, margin)
+        current = extended[:, margin : margin + block_rows, margin : margin + block_cols]
+        current = current - gradient / (illumination + DAMPING)
+        if sweep_index < ITERS - 1:
+            extended = exchange_halo(current, margin)
     return current
 
 

time: 137 us -> 139 us (1.015)
  the two profiles are of different devices: /device:TPU:30 before, /device:TPU:25 now
where the time goes in v8:
time: 139 us; the launch traced here: 136 us
  Pallas kernels  128 us (92%)
  other arithmetic  7.6 us (5%)
    pallas_call x1, Pallas kernels, fold_and_step(): pl.pallas_call(fold_step_kernel, out_shape=(jax.ShapeDtypeStruct((fields,...  55.9 us
    pallas_call x2, Pallas kernels, gradient_canvas(): pl.pallas_call(gradient_kernel, out_shape=jax.ShapeDtypeStruct((channels,...  25.2 us
    pallas_call x1, Pallas kernels, exchange_halo(): pl.pallas_call(halo_kernel, out_shape=jax.ShapeDtypeStruct((depth, rows +...  24.5 us
    pallas_call x1, Pallas kernels, exchange_fold(): pl.pallas_call(fold_kernel, out_shape=jax.ShapeDtypeStruct((depth, rows,...  22.6 us

profile of v8, /device:TPU:25, one launch (start us, length us, event | category | flops | bytes accessed | tf_op | source)
XLA Modules:
  0.0 135.9 jit_solution(1222123921119431712)
XLA Ops:
  0.0 1.3 fusion.9
  1.3 1.2 fusion.6
  2.5 1.2 subtract_convert_fusion
  3.7 0.9 pad_maximum_fusion.tables_ref
  4.5 24.5 %shard_map.55.ext_ref = f32[2,384,768]{2,1,0:T(8,128)} custom-call(f32[2,128,512]{2,1,0:T(8,128)} %cur_ref.3), custom_call_target="tpu_custom_call" | custom-call | tf_op jit(solution)/shard_map/pallas_call | solution.py:520
  29.0 12.8 %shard_map.56.canvas_ref = f32[3,384,768]{2,1,0:T(8,128)} custom-call(s32[2,2]{1,0:T(2,128)} %bitcast.7, s32[1]{0:T(128)} %bitcast.2.count_ref, f32[2,384,768]{2,1,0:T(8,128)} %shard_map.55.ext_ref, f32[2,256,256]{2,1,0:T(8,128)} %probe_ref.3, f32[2,256,256]{2,1,0:T(8,128)} %bitcast.5, bf16[4,256,256]{2,1,0:T(8,128)(2,1)} %pad_maximum_fusion.tables_ref), custom_call_target="tpu_custom_call" | custom-call | tf_op jit(solution)/shard_map/pallas_call | solution.py:236
  41.9 55.9 %shard_map.57 = (f32[2,384,768]{2,1,0:T(8,128)}, f32[128,512]{1,0:T(8,128)}) custom-call(f32[3,384,768]{2,1,0:T(8,128)} %shard_map.56.canvas_ref, f32[2,128,512]{2,1,0:T(8,128)} %cur_ref.3), custom_call_target="tpu_custom_call" | custom-call | tf_op jit(solution)/shard_map/pallas_call | solution.py:496
  97.8 1.0 broadcast_add_fusion
  98.8 12.3 %shard_map.58.canvas_ref = f32[2,384,768]{2,1,0:T(8,128)} custom-call(s32[2,2]{1,0:T(2,128)} %bitcast.8, s32[1]{0:T(128)} %bitcast.2.count_ref, f32[2,384,768]{2,1,0:T(8,128)} %get-tuple-element.7.ext_ref, f32[2,256,256]{2,1,0:T(8,128)} %probe_ref.3, f32[2,256,256]{2,1,0:T(8,128)} %bitcast.6, bf16[4,256,256]{2,1,0:T(8,128)(2,1)} %pad_maximum_fusion.tables_ref), custom_call_target="tpu_custom_call" | custom-call | tf_op jit(solution)/shard_map/pallas_call | solution.py:236
  111.1 22.6 %shard_map.59 = f32[2,128,512]{2,1,0:T(8,128)} custom-call(f32[2,384,768]{2,1,0:T(8,128)} %shard_map.58.canvas_ref), custom_call_target="tpu_custom_call" | custom-call | tf_op jit(solution)/shard_map/pallas_call | solution.py:536
  133.7 2.1 %divide_subtract_fusion = f32[2,128,512]{2,1,0:T(8,128)} fusion(f32[2,128,512]{2,1,0:T(8,128)} %shard_map.59, f32[2,384,768]{2,1,0:T(8,128)} %get-tuple-element.7.ext_ref, f32[128,512]{1,0:T(8,128)S(1)} %broadcast_add_fusion), kind=kLoop, calls=%fused_computation.1 | loop fusion | flops 262144 | bytes 1835008 | tf_op jit(solution)/shard_map/sub | solution.py:576

commit v9 on v7

--- a/solution.py
+++ b/solution.py
@@ -356,12 +356,14 @@
     )
 
 
-def fold_kernel(canvas_ref, out_ref, row_bufs, col_bufs, band_ref, send_sems, recv_sems):
+def fold_kernel(canvas_ref, out_ref, row_bufs, col_bufs, band_ref, send_sems, recv_sems, band_sem):
     rows = out_ref.shape[1]
     cols = out_ref.shape[2]
     margin = (canvas_ref.shape[2] - cols) // 2
     place = mesh_place()
     me_r, me_c, n_r, n_c = place
+    own_band = pltpu.make_async_copy(canvas_ref.at[:, margin : margin + rows, :], band_ref, band_sem)
+    own_band.start()
     neighbour_barrier(me_r, me_c, n_r, n_c)
     swap(
         place,
@@ -372,7 +374,7 @@
         send_sems.at[0:2],
         recv_sems.at[0:2],
     )
-    band_ref[...] = canvas_ref[:, margin : margin + rows, :]
+    own_band.wait()
 
     @pl.when(exists(me_r + 1, me_c, n_r, n_c))
     def _():
@@ -423,7 +425,7 @@
     return pl.pallas_call(
         fold_kernel,
         out_shape=jax.ShapeDtypeStruct((depth, rows, cols), jnp.float32),
-        in_specs=[VMEM_SPEC],
+        in_specs=[pl.BlockSpec(memory_space=pl.ANY)],
         out_specs=VMEM_SPEC,
         scratch_shapes=[
             pltpu.VMEM((2, depth, margin, ext_cols), jnp.float32),
@@ -431,6 +433,7 @@
             pltpu.VMEM((depth, rows, ext_cols), jnp.float32),
             pltpu.SemaphoreType.DMA((4,)),
             pltpu.SemaphoreType.DMA((4,)),
+            pltpu.SemaphoreType.DMA(()),
         ],
         compiler_params=pltpu.CompilerParams(
             vmem_limit_bytes=60 * 1024 * 1024, has_side_effects=True, collective_id=depth

time: 137 us -> 133 us (0.971)
  the two profiles are of different devices: /device:TPU:30 before, /device:TPU:28 now
where the time goes in v9:
time: 133 us
  Pallas kernels  124 us (93%)
  other arithmetic  9.4 us (7%)
    pallas_call x2, Pallas kernels, exchange_fold(): pl.pallas_call(fold_kernel, out_shape=jax.ShapeDtypeStruct((depth, rows,...  50.6 us
    pallas_call x2, Pallas kernels, exchange_halo(): pl.pallas_call(halo_kernel, out_shape=jax.ShapeDtypeStruct((depth, rows +...  47.9 us
    pallas_call x2, Pallas kernels, gradient_canvas(): pl.pallas_call(gradient_kernel, out_shape=jax.ShapeDtypeStruct((channels,...  25.1 us
    sub x2, other arithmetic, on_device(): current = current - folded[0:2] / (illumination + DAMPING)  3.92 us

profile of v9, /device:TPU:28, one launch (start us, length us, event | category | flops | bytes accessed | tf_op | source)
XLA Modules:
  0.0 133.1 jit_solution(10308384825096218184)
XLA Ops:
  0.0 1.3 fusion.9
  1.3 1.2 fusion.6
  2.5 1.2 subtract_convert_fusion
  3.7 0.9 pad_maximum_fusion.tables_ref
  4.5 25.6 %shard_map.55.ext_ref = f32[2,384,768]{2,1,0:T(8,128)} custom-call(f32[2,128,512]{2,1,0:T(8,128)} %cur_ref.1), custom_call_target="tpu_custom_call" | custom-call | tf_op jit(solution)/shard_map/pallas_call | solution.py:409
  30.1 12.8 %shard_map.56.canvas_ref = f32[3,384,768]{2,1,0:T(8,128)} custom-call(s32[2,2]{1,0:T(2,128)} %bitcast.9, s32[1]{0:T(128)} %bitcast.2.count_ref, f32[2,384,768]{2,1,0:T(8,128)} %shard_map.55.ext_ref, f32[2,256,256]{2,1,0:T(8,128)} %probe_ref.3, f32[2,256,256]{2,1,0:T(8,128)} %bitcast.7, bf16[4,256,256]{2,1,0:T(8,128)(2,1)} %pad_maximum_fusion.tables_ref), custom_call_target="tpu_custom_call" | custom-call | tf_op jit(solution)/shard_map/pallas_call | solution.py:236
  42.9 0.0 copy-start.1
  42.9 28.5 %shard_map.57 = f32[3,128,512]{2,1,0:T(8,128)} custom-call(f32[3,384,768]{2,1,0:T(8,128)} %shard_map.56.canvas_ref), custom_call_target="tpu_custom_call" | custom-call | tf_op jit(solution)/shard_map/pallas_call | solution.py:425
  71.4 1.0 add_bitcast_fusion
  72.4 0.0 copy-done.1
  72.4 2.0 %divide_subtract_fusion.1.cur_ref = f32[2,128,512]{2,1,0:T(8,128)} fusion(f32[2,128,512]{2,1,0:T(8,128)S(1)} %copy-done.1, f32[3,128,512]{2,1,0:T(8,128)} %shard_map.57, f32[128,512]{1,0:T(8,128)S(1)} %add_bitcast_fusion), kind=kLoop, calls=%fused_computation.2 | loop fusion | flops 262144 | bytes 1835008 | tf_op jit(solution)/shard_map/sub | solution.py:469
  74.4 22.4 %shard_map.58.ext_ref = f32[2,384,768]{2,1,0:T(8,128)} custom-call(f32[2,128,512]{2,1,0:T(8,128)} %divide_subtract_fusion.1.cur_ref), custom_call_target="tpu_custom_call" | custom-call | tf_op jit(solution)/shard_map/pallas_call | solution.py:409
  96.7 12.3 %shard_map.59.canvas_ref = f32[2,384,768]{2,1,0:T(8,128)} custom-call(s32[2,2]{1,0:T(2,128)} %bitcast.10, s32[1]{0:T(128)} %bitcast.2.count_ref, f32[2,384,768]{2,1,0:T(8,128)} %shard_map.58.ext_ref, f32[2,256,256]{2,1,0:T(8,128)} %probe_ref.3, f32[2,256,256]{2,1,0:T(8,128)} %bitcast.8, bf16[4,256,256]{2,1,0:T(8,128)(2,1)} %pad_maximum_fusion.tables_ref), custom_call_target="tpu_custom_call" | custom-call | tf_op jit(solution)/shard_map/pallas_call | solution.py:236
  109.0 0.0 copy-start
  109.0 22.1 %shard_map.60 = f32[2,128,512]{2,1,0:T(8,128)} custom-call(f32[2,384,768]{2,1,0:T(8,128)} %shard_map.59.canvas_ref), custom_call_target="tpu_custom_call" | custom-call | tf_op jit(solution)/shard_map/pallas_call | solution.py:425
  131.1 0.0 copy-done
  131.2 2.0 %divide_subtract_fusion = f32[2,128,512]{2,1,0:T(8,128)} fusion(f32[2,128,512]{2,1,0:T(8,128)S(1)} %copy-done, f32[2,128,512]{2,1,0:T(8,128)} %shard_map.60, f32[128,512]{1,0:T(8,128)S(1)} %add_bitcast_fusion), kind=kLoop, calls=%fused_computation.1 | loop fusion | flops 262144 | bytes 1835008 | tf_op jit(solution)/shard_map/sub | solution.py:469
Async XLA Ops:
  42.9 29.5 %copy-start.1 = (f32[2,128,512]{2,1,0:T(8,128)S(1)}, f32[2,128,512]{2,1,0:T(8,128)}, u32[]{:S(2)}) copy-start(f32[2,128,512]{2,1,0:T(8,128)} %cur_ref.1) | copy-start | bytes 1572868
  109.0 22.1 %copy-start = (f32[2,128,512]{2,1,0:T(8,128)S(1)}, f32[2,128,512]{2,1,0:T(8,128)}, u32[]{:S(2)}) copy-start(f32[2,128,512]{2,1,0:T(8,128)} %divide_subtract_fusion.1.cur_ref) | copy-start | bytes 1572868

commit v10 on v9

--- a/solution.py
+++ b/solution.py
@@ -315,36 +315,52 @@
             copy.wait_recv()
 
 
-def halo_kernel(cur_ref, ext_ref, send_sems, recv_sems):
+def halo_kernel(cur_ref, ext_ref, zeros_ref, send_sems, recv_sems, local_sems):
     rows = cur_ref.shape[1]
     cols = cur_ref.shape[2]
     margin = (ext_ref.shape[2] - cols) // 2
+    ext_cols = cols + 2 * margin
     place = mesh_place()
     me_r, me_c, n_r, n_c = place
     middle = slice(margin, margin + rows)
-    ext_ref[:, middle, margin : margin + cols] = cur_ref[...]
+    own = pltpu.make_async_copy(cur_ref, ext_ref.at[:, middle, margin : margin + cols], local_sems.at[0])
+    own.start()
+    zeros_ref[...] = jnp.zeros(zeros_ref.shape, jnp.float32)
     unreached = [
-        ((0, 1), (slice(None), middle, slice(0, margin))),
-        ((0, -1), (slice(None), middle, slice(margin + cols, 2 * margin + cols))),
-        ((1, 0), (slice(None), slice(0, margin), slice(None))),
-        ((-1, 0), (slice(None), slice(margin + rows, 2 * margin + rows), slice(None))),
+        ((0, 1), ext_ref.at[:, middle, 0:margin], zeros_ref.at[:, :, 0:margin]),
+        ((0, -1), ext_ref.at[:, middle, margin + cols : ext_cols], zeros_ref.at[:, :, 0:margin]),
+        ((1, 0), ext_ref.at[:, 0:margin, :], zeros_ref),
+        ((-1, 0), ext_ref.at[:, margin + rows : 2 * margin + rows, :], zeros_ref),
     ]
-    for (dr, dc), region in unreached:
-
-        @pl.when(jnp.logical_not(exists(me_r - dr, me_c - dc, n_r, n_c)))
-        def _():
-            ext_ref[region] = jnp.zeros(ext_ref[region].shape, jnp.float32)
+    blanks = []
+    for index, ((dr, dc), target, source) in enumerate(unreached):
+        blank = pltpu.make_async_copy(source, target, local_sems.at[index + 1])
+        missing = jnp.logical_not(exists(me_r - dr, me_c - dc, n_r, n_c))
+        blanks.append((blank, missing))
 
     neighbour_barrier(me_r, me_c, n_r, n_c)
+    for blank, missing in blanks:
+
+        @pl.when(missing)
+        def _():
+            blank.start()
+
     swap(
         place,
         [
-            ((0, -1), cur_ref.at[:, :, 0:margin], ext_ref.at[:, middle, margin + cols : 2 * margin + cols]),
+            ((0, -1), cur_ref.at[:, :, 0:margin], ext_ref.at[:, middle, margin + cols : ext_cols]),
             ((0, 1), cur_ref.at[:, :, cols - margin : cols], ext_ref.at[:, middle, 0:margin]),
         ],
         send_sems.at[0:2],
         recv_sems.at[0:2],
     )
+    own.wait()
+    for blank, missing in blanks:
+
+        @pl.when(missing)
+        def _():
+            blank.wait()
+
     swap(
         place,
         [
@@ -410,8 +426,13 @@
         halo_kernel,
         out_shape=jax.ShapeDtypeStruct((depth, rows + 2 * margin, cols + 2 * margin), jnp.float32),
         in_specs=[VMEM_SPEC],
-        out_specs=VMEM_SPEC,
-        scratch_shapes=[pltpu.SemaphoreType.DMA((4,)), pltpu.SemaphoreType.DMA((4,))],
+        out_specs=pl.BlockSpec(memory_space=pl.ANY),
+        scratch_shapes=[
+            pltpu.VMEM((depth, margin, cols + 2 * margin), jnp.float32),
+            pltpu.SemaphoreType.DMA((4,)),
+            pltpu.SemaphoreType.DMA((4,)),
+            pltpu.SemaphoreType.DMA((5,)),
+        ],
         compiler_params=pltpu.CompilerParams(
             vmem_limit_bytes=60 * 1024 * 1024, has_side_effects=True, collective_id=0
         ),

time: 133 us -> 132 us (level)
  Pallas kernels: 124 us -> 122 us
    pallas_call x2, Pallas kernels: 47.9 us -> 46.1 us  [exchange_halo(): pl.pallas_call(halo_kernel, out_shape=jax.ShapeDtypeStruct((depth, rows +...]
where the time goes in v10:
time: 132 us
  Pallas kernels  122 us (92%)
  other arithmetic  9.4 us (7%)
    pallas_call x2, Pallas kernels, exchange_fold(): pl.pallas_call(fold_kernel, out_shape=jax.ShapeDtypeStruct((depth, rows,...  51.1 us
    pallas_call x2, Pallas kernels, exchange_halo(): pl.pallas_call(halo_kernel, out_shape=jax.ShapeDtypeStruct((depth, rows +...  46.1 us
    pallas_call x2, Pallas kernels, gradient_canvas(): pl.pallas_call(gradient_kernel, out_shape=jax.ShapeDtypeStruct((channels,...  25.2 us
    sub x2, other arithmetic, on_device(): current = current - folded[0:2] / (illumination + DAMPING)  3.92 us

profile of v10, /device:TPU:28, one launch (start us, length us, event | category | flops | bytes accessed | tf_op | source)
XLA Modules:
  0.0 131.8 jit_solution(4692957191535266041)
XLA Ops:
  0.0 1.3 fusion.9
  1.3 1.2 fusion.6
  2.5 1.2 subtract_convert_fusion
  3.7 0.9 pad_maximum_fusion.tables_ref
  4.5 24.6 %shard_map.55.ext_ref = f32[2,384,768]{2,1,0:T(8,128)} custom-call(f32[2,128,512]{2,1,0:T(8,128)} %cur_ref.1), custom_call_target="tpu_custom_call" | custom-call | tf_op jit(solution)/shard_map/pallas_call | solution.py:425
  29.2 12.8 %shard_map.56.canvas_ref = f32[3,384,768]{2,1,0:T(8,128)} custom-call(s32[2,2]{1,0:T(2,128)} %bitcast.9, s32[1]{0:T(128)} %bitcast.2.count_ref, f32[2,384,768]{2,1,0:T(8,128)} %shard_map.55.ext_ref, f32[2,256,256]{2,1,0:T(8,128)} %probe_ref.3, f32[2,256,256]{2,1,0:T(8,128)} %bitcast.7, bf16[4,256,256]{2,1,0:T(8,128)(2,1)} %pad_maximum_fusion.tables_ref), custom_call_target="tpu_custom_call" | custom-call | tf_op jit(solution)/shard_map/pallas_call | solution.py:236
  42.0 0.0 copy-start.1
  42.0 28.4 %shard_map.57 = f32[3,128,512]{2,1,0:T(8,128)} custom-call(f32[3,384,768]{2,1,0:T(8,128)} %shard_map.56.canvas_ref), custom_call_target="tpu_custom_call" | custom-call | tf_op jit(solution)/shard_map/pallas_call | solution.py:446
  70.4 1.0 add_bitcast_fusion
  71.4 0.0 copy-done.1
  71.4 2.0 %divide_subtract_fusion.1.cur_ref = f32[2,128,512]{2,1,0:T(8,128)} fusion(f32[2,128,512]{2,1,0:T(8,128)S(1)} %copy-done.1, f32[3,128,512]{2,1,0:T(8,128)} %shard_map.57, f32[128,512]{1,0:T(8,128)S(1)} %add_bitcast_fusion), kind=kLoop, calls=%fused_computation.2 | loop fusion | flops 262144 | bytes 1835008 | tf_op jit(solution)/shard_map/sub | solution.py:490
  73.4 21.4 %shard_map.58.ext_ref = f32[2,384,768]{2,1,0:T(8,128)} custom-call(f32[2,128,512]{2,1,0:T(8,128)} %divide_subtract_fusion.1.cur_ref), custom_call_target="tpu_custom_call" | custom-call | tf_op jit(solution)/shard_map/pallas_call | solution.py:425
  94.8 12.3 %shard_map.59.canvas_ref = f32[2,384,768]{2,1,0:T(8,128)} custom-call(s32[2,2]{1,0:T(2,128)} %bitcast.10, s32[1]{0:T(128)} %bitcast.2.count_ref, f32[2,384,768]{2,1,0:T(8,128)} %shard_map.58.ext_ref, f32[2,256,256]{2,1,0:T(8,128)} %probe_ref.3, f32[2,256,256]{2,1,0:T(8,128)} %bitcast.8, bf16[4,256,256]{2,1,0:T(8,128)(2,1)} %pad_maximum_fusion.tables_ref), custom_call_target="tpu_custom_call" | custom-call | tf_op jit(solution)/shard_map/pallas_call | solution.py:236
  107.2 0.0 copy-start
  107.2 22.7 %shard_map.60 = f32[2,128,512]{2,1,0:T(8,128)} custom-call(f32[2,384,768]{2,1,0:T(8,128)} %shard_map.59.canvas_ref), custom_call_target="tpu_custom_call" | custom-call | tf_op jit(solution)/shard_map/pallas_call | solution.py:446
  129.8 0.0 copy-done
  129.9 2.0 %divide_subtract_fusion = f32[2,128,512]{2,1,0:T(8,128)} fusion(f32[2,128,512]{2,1,0:T(8,128)S(1)} %copy-done, f32[2,128,512]{2,1,0:T(8,128)} %shard_map.60, f32[128,512]{1,0:T(8,128)S(1)} %add_bitcast_fusion), kind=kLoop, calls=%fused_computation.1 | loop fusion | flops 262144 | bytes 1835008 | tf_op jit(solution)/shard_map/sub | solution.py:490
Async XLA Ops:
  42.0 29.4 %copy-start.1 = (f32[2,128,512]{2,1,0:T(8,128)S(1)}, f32[2,128,512]{2,1,0:T(8,128)}, u32[]{:S(2)}) copy-start(f32[2,128,512]{2,1,0:T(8,128)} %cur_ref.1) | copy-start | bytes 1572868
  107.2 22.7 %copy-start = (f32[2,128,512]{2,1,0:T(8,128)S(1)}, f32[2,128,512]{2,1,0:T(8,128)}, u32[]{:S(2)}) copy-start(f32[2,128,512]{2,1,0:T(8,128)} %divide_subtract_fusion.1.cur_ref) | copy-start | bytes 1572868

commit v11 on v10

--- a/solution.py
+++ b/solution.py
@@ -372,7 +372,7 @@
     )
 
 
-def fold_kernel(canvas_ref, out_ref, row_bufs, col_bufs, band_ref, send_sems, recv_sems, band_sem):
+def fold_kernel(canvas_ref, cur_ref, light_in_ref, out_ref, light_ref, row_bufs, col_bufs, band_ref, total_ref, send_sems, recv_sems, band_sem):
     rows = out_ref.shape[1]
     cols = out_ref.shape[2]
     margin = (canvas_ref.shape[2] - cols) // 2
@@ -409,15 +409,22 @@
         send_sems.at[2:4],
         recv_sems.at[2:4],
     )
-    out_ref[...] = band_ref[:, :, margin : margin + cols]
+    total_ref[...] = band_ref[:, :, margin : margin + cols]
 
     @pl.when(exists(me_r, me_c + 1, n_r, n_c))
     def _():
-        out_ref[:, :, cols - margin : cols] += col_bufs[0]
+        total_ref[:, :, cols - margin : cols] += col_bufs[0]
 
     @pl.when(exists(me_r, me_c - 1, n_r, n_c))
     def _():
-        out_ref[:, :, 0:margin] += col_bufs[1]
+        total_ref[:, :, 0:margin] += col_bufs[1]
+
+    fields = cur_ref.shape[0]
+    if total_ref.shape[0] > fields:
+        light_ref[...] = total_ref[fields]
+    else:
+        light_ref[...] = light_in_ref[...]
+    out_ref[...] = cur_ref[...] - total_ref[0:fields] / (light_ref[...] + DAMPING)
 
 
 def exchange_halo(current, margin):
@@ -439,19 +446,22 @@
     )(current)
 
 
-def exchange_fold(canvas, margin):
+def fold_and_step(canvas, current, light, margin):
     depth, ext_rows, ext_cols = canvas.shape
-    rows = ext_rows - 2 * margin
-    cols = ext_cols - 2 * margin
+    fields, rows, cols = current.shape
     return pl.pallas_call(
         fold_kernel,
-        out_shape=jax.ShapeDtypeStruct((depth, rows, cols), jnp.float32),
-        in_specs=[pl.BlockSpec(memory_space=pl.ANY)],
-        out_specs=VMEM_SPEC,
+        out_shape=(
+            jax.ShapeDtypeStruct((fields, rows, cols), jnp.float32),
+            jax.ShapeDtypeStruct((rows, cols), jnp.float32),
+        ),
+        in_specs=[pl.BlockSpec(memory_space=pl.ANY), VMEM_SPEC, VMEM_SPEC],
+        out_specs=(VMEM_SPEC, VMEM_SPEC),
         scratch_shapes=[
             pltpu.VMEM((2, depth, margin, ext_cols), jnp.float32),
             pltpu.VMEM((2, depth, rows, margin), jnp.float32),
             pltpu.VMEM((depth, rows, ext_cols), jnp.float32),
+            pltpu.VMEM((depth, rows, cols), jnp.float32),
             pltpu.SemaphoreType.DMA((4,)),
             pltpu.SemaphoreType.DMA((4,)),
             pltpu.SemaphoreType.DMA(()),
@@ -459,7 +469,7 @@
         compiler_params=pltpu.CompilerParams(
             vmem_limit_bytes=60 * 1024 * 1024, has_side_effects=True, collective_id=depth
         ),
-    )(canvas)
+    )(canvas, current, light)
 
 
 def on_device(object_field, probe_field, amplitudes, centres, counts):
@@ -478,16 +488,14 @@
     ext_shape = (block_rows + size_probe, block_cols + size_probe)
 
     current = object_field
+    illumination = jnp.zeros((block_rows, block_cols), jnp.float32)
     for sweep_index in range(ITERS):
         extended = exchange_halo(current, margin)
         channels = 3 if sweep_index == 0 else 2
         canvas = gradient_canvas(
             channels, ext_shape, spots, own_count, extended, probe_field, own_amps, tables
         )
-        folded = exchange_fold(canvas, margin)
-        if sweep_index == 0:
-            illumination = folded[2]
-        current = current - folded[0:2] / (illumination + DAMPING)
+        current, illumination = fold_and_step(canvas, current, illumination, margin)
     return current
 
 

time: 132 us -> 132 us (level)
  the two profiles are of different devices: /device:TPU:28 before, /device:TPU:22 now
where the time goes in v11:
time: 132 us; the launch traced here: 131 us
  Pallas kernels  124 us (94%)
  other arithmetic  4.51 us (3%)
  local copies, waits for them, and re-layouts  2.59 us (2%)
    pallas_call x2, Pallas kernels, fold_and_step(): pl.pallas_call(fold_kernel, out_shape=(jax.ShapeDtypeStruct((fields, rows...  59.5 us
    pallas_call x2, Pallas kernels, exchange_halo(): pl.pallas_call(halo_kernel, out_shape=jax.ShapeDtypeStruct((depth, rows +...  47.6 us
    pallas_call x2, Pallas kernels, gradient_canvas(): pl.pallas_call(gradient_kernel, out_shape=jax.ShapeDtypeStruct((channels,...  17.1 us

profile of v11, /device:TPU:22, one launch (start us, length us, event | category | flops | bytes accessed | tf_op | source)
XLA Modules:
  0.0 131.4 jit_solution(6361855595014909982)
XLA Ops:
  0.0 1.2 subtract_convert_fusion
  1.2 1.2 fusion.6
  2.4 0.9 pad_maximum_fusion.tables_ref
  3.2 1.3 fusion.9
  4.5 24.6 %shard_map.55.ext_ref = f32[2,384,768]{2,1,0:T(8,128)} custom-call(f32[2,128,512]{2,1,0:T(8,128)} %cur_ref.3), custom_call_target="tpu_custom_call" | custom-call | tf_op jit(solution)/shard_map/pallas_call | solution.py:432
  29.2 8.7 %shard_map.56.canvas_ref = f32[3,384,768]{2,1,0:T(8,128)} custom-call(s32[2,2]{1,0:T(2,128)} %bitcast.7, s32[1]{0:T(128)} %bitcast.2.count_ref, f32[2,384,768]{2,1,0:T(8,128)} %shard_map.55.ext_ref, f32[2,256,256]{2,1,0:T(8,128)} %probe_ref.3, f32[2,256,256]{2,1,0:T(8,128)} %bitcast.5, bf16[4,256,256]{2,1,0:T(8,128)(2,1)} %pad_maximum_fusion.tables_ref), custom_call_target="tpu_custom_call" | custom-call | tf_op jit(solution)/shard_map/pallas_call | solution.py:236
  37.9 0.7 broadcast_in_dim.10.light_in_ref
  38.6 32.7 %shard_map.57 = (f32[2,128,512]{2,1,0:T(8,128)}, f32[128,512]{1,0:T(8,128)}) custom-call(f32[3,384,768]{2,1,0:T(8,128)} %shard_map.56.canvas_ref, f32[2,128,512]{2,1,0:T(8,128)} %cur_ref.3, f32[128,512]{1,0:T(8,128)} %broadcast_in_dim.10.light_in_ref), custom_call_target="tpu_custom_call" | custom-call | tf_op jit(solution)/shard_map/pallas_call | solution.py:452
  71.3 23.0 %shard_map.58.ext_ref = f32[2,384,768]{2,1,0:T(8,128)} custom-call(f32[2,128,512]{2,1,0:T(8,128)} %get-tuple-element.8.cur_ref), custom_call_target="tpu_custom_call" | custom-call | tf_op jit(solution)/shard_map/pallas_call | solution.py:432
  94.3 8.4 %shard_map.59.canvas_ref = f32[2,384,768]{2,1,0:T(8,128)} custom-call(s32[2,2]{1,0:T(2,128)} %bitcast.8, s32[1]{0:T(128)} %bitcast.2.count_ref, f32[2,384,768]{2,1,0:T(8,128)} %shard_map.58.ext_ref, f32[2,256,256]{2,1,0:T(8,128)} %probe_ref.3, f32[2,256,256]{2,1,0:T(8,128)} %bitcast.6, bf16[4,256,256]{2,1,0:T(8,128)(2,1)} %pad_maximum_fusion.tables_ref), custom_call_target="tpu_custom_call" | custom-call | tf_op jit(solution)/shard_map/pallas_call | solution.py:236
  102.7 26.8 %shard_map.60 = (f32[2,128,512]{2,1,0:T(8,128)}, f32[128,512]{1,0:T(8,128)}) custom-call(f32[2,384,768]{2,1,0:T(8,128)} %shard_map.59.canvas_ref, f32[2,128,512]{2,1,0:T(8,128)} %get-tuple-element.8.cur_ref, f32[128,512]{1,0:T(8,128)} %get-tuple-element.9.light_in_ref), custom_call_target="tpu_custom_call" | custom-call | tf_op jit(solution)/shard_map/pallas_call | solution.py:452
  129.5 1.9 %copy.7 = f32[2,128,512]{2,1,0:T(8,128)} copy(f32[2,128,512]{2,1,0:T(8,128)} %get-tuple-element.10) | data formatting | bytes 1048576

commit v12 on v11

--- a/solution.py
+++ b/solution.py
@@ -285,7 +285,7 @@
     pl.semaphore_wait(barrier, greeted)
 
 
-def swap(place, pieces, send_sems, recv_sems):
+def start_copies(place, pieces, send_sems, recv_sems):
     me_r, me_c, n_r, n_c = place
     copies = []
     for index, ((dr, dc), source, target) in enumerate(pieces):
@@ -297,14 +297,18 @@
             device_id=(me_r + dr, me_c + dc),
             device_id_type=pl.DeviceIdType.MESH,
         )
-        copies.append(copy)
+        copies.append(((dr, dc), copy))
 
         @pl.when(exists(me_r + dr, me_c + dc, n_r, n_c))
         def _():
             copy.start()
 
-    for index, ((dr, dc), _, _) in enumerate(pieces):
-        copy = copies[index]
+    return copies
+
+
+def wait_copies(place, copies):
+    me_r, me_c, n_r, n_c = place
+    for (dr, dc), copy in copies:
 
         @pl.when(exists(me_r + dr, me_c + dc, n_r, n_c))
         def _():
@@ -313,6 +317,10 @@
         @pl.when(exists(me_r - dr, me_c - dc, n_r, n_c))
         def _():
             copy.wait_recv()
+
+
+def swap(place, pieces, send_sems, recv_sems):
+    wait_copies(place, start_copies(place, pieces, send_sems, recv_sems))
 
 
 def halo_kernel(cur_ref, ext_ref, zeros_ref, send_sems, recv_sems, local_sems):
@@ -345,14 +353,28 @@
         def _():
             blank.start()
 
+    above = slice(0, margin)
+    below = slice(margin + rows, 2 * margin + rows)
+    inner = slice(margin, margin + cols)
+    left = slice(0, margin)
+    right = slice(margin + cols, ext_cols)
+    bands = start_copies(
+        place,
+        [
+            ((-1, 0), cur_ref, ext_ref.at[:, below, inner]),
+            ((1, 0), cur_ref, ext_ref.at[:, above, inner]),
+        ],
+        send_sems.at[0:2],
+        recv_sems.at[0:2],
+    )
     swap(
         place,
         [
-            ((0, -1), cur_ref.at[:, :, 0:margin], ext_ref.at[:, middle, margin + cols : ext_cols]),
-            ((0, 1), cur_ref.at[:, :, cols - margin : cols], ext_ref.at[:, middle, 0:margin]),
-        ],
-        send_sems.at[0:2],
-        recv_sems.at[0:2],
+            ((0, -1), cur_ref.at[:, :, 0:margin], ext_ref.at[:, middle, right]),
+            ((0, 1), cur_ref.at[:, :, cols - margin : cols], ext_ref.at[:, middle, left]),
+        ],
+        send_sems.at[2:4],
+        recv_sems.at[2:4],
     )
     own.wait()
     for blank, missing in blanks:
@@ -361,15 +383,19 @@
         def _():
             blank.wait()
 
-    swap(
+    corners = start_copies(
         place,
         [
-            ((-1, 0), ext_ref.at[:, middle, :], ext_ref.at[:, margin + rows : 2 * margin + rows, :]),
-            ((1, 0), ext_ref.at[:, middle, :], ext_ref.at[:, 0:margin, :]),
-        ],
-        send_sems.at[2:4],
-        recv_sems.at[2:4],
-    )
+            ((-1, 0), ext_ref.at[:, middle, left], ext_ref.at[:, below, left]),
+            ((-1, 0), ext_ref.at[:, middle, right], ext_ref.at[:, below, right]),
+            ((1, 0), ext_ref.at[:, middle, left], ext_ref.at[:, above, left]),
+            ((1, 0), ext_ref.at[:, middle, right], ext_ref.at[:, above, right]),
+        ],
+        send_sems.at[4:8],
+        recv_sems.at[4:8],
+    )
+    wait_copies(place, bands)
+    wait_copies(place, corners)
 
 
 def fold_kernel(canvas_ref, cur_ref, light_in_ref, out_ref, light_ref, row_bufs, col_bufs, band_ref, total_ref, send_sems, recv_sems, band_sem):
@@ -436,8 +462,8 @@
         out_specs=pl.BlockSpec(memory_space=pl.ANY),
         scratch_shapes=[
             pltpu.VMEM((depth, margin, cols + 2 * margin), jnp.float32),
-            pltpu.SemaphoreType.DMA((4,)),
-            pltpu.SemaphoreType.DMA((4,)),
+            pltpu.SemaphoreType.DMA((8,)),
+            pltpu.SemaphoreType.DMA((8,)),
             pltpu.SemaphoreType.DMA((5,)),
         ],
         compiler_params=pltpu.CompilerParams(

time: 132 us -> 125 us (0.947)
  the two profiles are of different devices: /device:TPU:22 before, /device:TPU:25 now
where the time goes in v12:
time: 125 us
  Pallas kernels  118 us (94%)
  other arithmetic  4.51 us (4%)
  local copies, waits for them, and re-layouts  2.59 us (2%)
    pallas_call x2, Pallas kernels, fold_and_step(): pl.pallas_call(fold_kernel, out_shape=(jax.ShapeDtypeStruct((fields, rows...  48.3 us
    pallas_call x2, Pallas kernels, exchange_halo(): pl.pallas_call(halo_kernel, out_shape=jax.ShapeDtypeStruct((depth, rows +...  44.3 us
    pallas_call x2, Pallas kernels, gradient_canvas(): pl.pallas_call(gradient_kernel, out_shape=jax.ShapeDtypeStruct((channels,...  25.2 us

profile of v12, /device:TPU:25, one launch (start us, length us, event | category | flops | bytes accessed | tf_op | source)
XLA Modules:
  0.0 124.9 jit_solution(9061650222543865955)
XLA Ops:
  0.0 1.2 subtract_convert_fusion
  1.2 1.2 fusion.6
  2.4 0.9 pad_maximum_fusion.tables_ref
  3.2 1.3 %fusion.9 = s32[]{:T(128)} fusion(s32[32,1]{0,1:T(1,128)} %param.9, s32[]{:T(128)S(6)} %axis_index.15), kind=kLoop, calls=%fused_computation.19 | loop fusion | flops 95 | bytes 136 | tf_op jit(solution)/shard_map/reduce_sum | solution.py:513
  4.5 23.7 %shard_map.55.ext_ref = f32[2,384,768]{2,1,0:T(8,128)} custom-call(f32[2,128,512]{2,1,0:T(8,128)} %cur_ref.3), custom_call_target="tpu_custom_call" | custom-call | tf_op jit(solution)/shard_map/pallas_call | solution.py:458
  28.3 12.8 %shard_map.56.canvas_ref = f32[3,384,768]{2,1,0:T(8,128)} custom-call(s32[2,2]{1,0:T(2,128)} %bitcast.7, s32[1]{0:T(128)} %bitcast.2.count_ref, f32[2,384,768]{2,1,0:T(8,128)} %shard_map.55.ext_ref, f32[2,256,256]{2,1,0:T(8,128)} %probe_ref.3, f32[2,256,256]{2,1,0:T(8,128)} %bitcast.5, bf16[4,256,256]{2,1,0:T(8,128)(2,1)} %pad_maximum_fusion.tables_ref), custom_call_target="tpu_custom_call" | custom-call | tf_op jit(solution)/shard_map/pallas_call | solution.py:236
  41.1 0.7 broadcast_in_dim.10.light_in_ref
  41.8 27.2 %shard_map.57 = (f32[2,128,512]{2,1,0:T(8,128)}, f32[128,512]{1,0:T(8,128)}) custom-call(f32[3,384,768]{2,1,0:T(8,128)} %shard_map.56.canvas_ref, f32[2,128,512]{2,1,0:T(8,128)} %cur_ref.3, f32[128,512]{1,0:T(8,128)} %broadcast_in_dim.10.light_in_ref), custom_call_target="tpu_custom_call" | custom-call | tf_op jit(solution)/shard_map/pallas_call | solution.py:478
  69.0 20.5 %shard_map.58.ext_ref = f32[2,384,768]{2,1,0:T(8,128)} custom-call(f32[2,128,512]{2,1,0:T(8,128)} %get-tuple-element.8.cur_ref), custom_call_target="tpu_custom_call" | custom-call | tf_op jit(solution)/shard_map/pallas_call | solution.py:458
  89.5 12.3 %shard_map.59.canvas_ref = f32[2,384,768]{2,1,0:T(8,128)} custom-call(s32[2,2]{1,0:T(2,128)} %bitcast.8, s32[1]{0:T(128)} %bitcast.2.count_ref, f32[2,384,768]{2,1,0:T(8,128)} %shard_map.58.ext_ref, f32[2,256,256]{2,1,0:T(8,128)} %probe_ref.3, f32[2,256,256]{2,1,0:T(8,128)} %bitcast.6, bf16[4,256,256]{2,1,0:T(8,128)(2,1)} %pad_maximum_fusion.tables_ref), custom_call_target="tpu_custom_call" | custom-call | tf_op jit(solution)/shard_map/pallas_call | solution.py:236
  101.9 21.1 %shard_map.60 = (f32[2,128,512]{2,1,0:T(8,128)}, f32[128,512]{1,0:T(8,128)}) custom-call(f32[2,384,768]{2,1,0:T(8,128)} %shard_map.59.canvas_ref, f32[2,128,512]{2,1,0:T(8,128)} %get-tuple-element.8.cur_ref, f32[128,512]{1,0:T(8,128)} %get-tuple-element.9.light_in_ref), custom_call_target="tpu_custom_call" | custom-call | tf_op jit(solution)/shard_map/pallas_call | solution.py:478
  123.0 1.9 %copy.7 = f32[2,128,512]{2,1,0:T(8,128)} copy(f32[2,128,512]{2,1,0:T(8,128)} %get-tuple-element.10) | data formatting | bytes 1048576

commit v13 on v12

--- a/solution.py
+++ b/solution.py
@@ -398,44 +398,68 @@
     wait_copies(place, corners)
 
 
-def fold_kernel(canvas_ref, cur_ref, light_in_ref, out_ref, light_ref, row_bufs, col_bufs, band_ref, total_ref, send_sems, recv_sems, band_sem):
+def fold_kernel(canvas_ref, cur_ref, light_in_ref, out_ref, light_ref, mid_bufs, corner_bufs, col_bufs, band_ref, total_ref, send_sems, recv_sems, band_sem):
     rows = out_ref.shape[1]
     cols = out_ref.shape[2]
     margin = (canvas_ref.shape[2] - cols) // 2
+    ext_cols = cols + 2 * margin
     place = mesh_place()
     me_r, me_c, n_r, n_c = place
     own_band = pltpu.make_async_copy(canvas_ref.at[:, margin : margin + rows, :], band_ref, band_sem)
     own_band.start()
     neighbour_barrier(me_r, me_c, n_r, n_c)
-    swap(
+    top = slice(0, margin)
+    bottom = slice(margin + rows, 2 * margin + rows)
+    left = slice(0, margin)
+    inner = slice(margin, margin + cols)
+    right = slice(margin + cols, ext_cols)
+    corners = start_copies(
         place,
         [
-            ((-1, 0), canvas_ref.at[:, 0:margin, :], row_bufs.at[0]),
-            ((1, 0), canvas_ref.at[:, margin + rows : 2 * margin + rows, :], row_bufs.at[1]),
-        ],
-        send_sems.at[0:2],
-        recv_sems.at[0:2],
-    )
+            ((-1, 0), canvas_ref.at[:, top, left], corner_bufs.at[0, 0]),
+            ((-1, 0), canvas_ref.at[:, top, right], corner_bufs.at[0, 1]),
+            ((1, 0), canvas_ref.at[:, bottom, left], corner_bufs.at[1, 0]),
+            ((1, 0), canvas_ref.at[:, bottom, right], corner_bufs.at[1, 1]),
+        ],
+        send_sems.at[0:4],
+        recv_sems.at[0:4],
+    )
+    mids = start_copies(
+        place,
+        [
+            ((-1, 0), canvas_ref.at[:, top, inner], mid_bufs.at[0]),
+            ((1, 0), canvas_ref.at[:, bottom, inner], mid_bufs.at[1]),
+        ],
+        send_sems.at[4:6],
+        recv_sems.at[4:6],
+    )
+    wait_copies(place, corners)
     own_band.wait()
-
-    @pl.when(exists(me_r + 1, me_c, n_r, n_c))
-    def _():
-        band_ref[...] += row_bufs[0]
-
-    @pl.when(exists(me_r - 1, me_c, n_r, n_c))
-    def _():
-        band_ref[...] += row_bufs[1]
-
-    swap(
+    for slot, source_r in ((0, me_r + 1), (1, me_r - 1)):
+
+        @pl.when(exists(source_r, me_c, n_r, n_c))
+        def _():
+            band_ref[:, :, left] += corner_bufs[slot, 0]
+            band_ref[:, :, right] += corner_bufs[slot, 1]
+
+    strips = start_copies(
         place,
         [
-            ((0, -1), band_ref.at[:, :, 0:margin], col_bufs.at[0]),
-            ((0, 1), band_ref.at[:, :, margin + cols : 2 * margin + cols], col_bufs.at[1]),
-        ],
-        send_sems.at[2:4],
-        recv_sems.at[2:4],
-    )
-    total_ref[...] = band_ref[:, :, margin : margin + cols]
+            ((0, -1), band_ref.at[:, :, left], col_bufs.at[0]),
+            ((0, 1), band_ref.at[:, :, right], col_bufs.at[1]),
+        ],
+        send_sems.at[6:8],
+        recv_sems.at[6:8],
+    )
+    wait_copies(place, mids)
+    total_ref[...] = band_ref[:, :, inner]
+    for slot, source_r in ((0, me_r + 1), (1, me_r - 1)):
+
+        @pl.when(exists(source_r, me_c, n_r, n_c))
+        def _():
+            total_ref[...] += mid_bufs[slot]
+
+    wait_copies(place, strips)
 
     @pl.when(exists(me_r, me_c + 1, n_r, n_c))
     def _():
@@ -484,12 +508,13 @@
         in_specs=[pl.BlockSpec(memory_space=pl.ANY), VMEM_SPEC, VMEM_SPEC],
         out_specs=(VMEM_SPEC, VMEM_SPEC),
         scratch_shapes=[
-            pltpu.VMEM((2, depth, margin, ext_cols), jnp.float32),
+            pltpu.VMEM((2, depth, margin, cols), jnp.float32),
+            pltpu.VMEM((2, 2, depth, margin, margin), jnp.float32),
             pltpu.VMEM((2, depth, rows, margin), jnp.float32),
             pltpu.VMEM((depth, rows, ext_cols), jnp.float32),
             pltpu.VMEM((depth, rows, cols), jnp.float32),
-            pltpu.SemaphoreType.DMA((4,)),
-            pltpu.SemaphoreType.DMA((4,)),
+            pltpu.SemaphoreType.DMA((8,)),
+            pltpu.SemaphoreType.DMA((8,)),
             pltpu.SemaphoreType.DMA(()),
         ],
         compiler_params=pltpu.CompilerParams(

time: 125 us -> 116 us (0.928)
  Pallas kernels: 118 us -> 108 us
    pallas_call x2, Pallas kernels: 48.3 us -> 41.5 us  [fold_and_step(): pl.pallas_call(fold_kernel, out_shape=(jax.ShapeDtypeStruct((fields, rows...]
    pallas_call x2, Pallas kernels: 44.3 us -> 41.3 us  [exchange_halo(): pl.pallas_call(halo_kernel, out_shape=jax.ShapeDtypeStruct((depth, rows +...]
where the time goes in v13:
time: 116 us; the launch traced here: 115 us
  Pallas kernels  108 us (93%)
  other arithmetic  4.51 us (4%)
  local copies, waits for them, and re-layouts  2.59 us (2%)
    pallas_call x2, Pallas kernels, fold_and_step(): pl.pallas_call(fold_kernel, out_shape=(jax.ShapeDtypeStruct((fields, rows...  41.5 us
    pallas_call x2, Pallas kernels, exchange_halo(): pl.pallas_call(halo_kernel, out_shape=jax.ShapeDtypeStruct((depth, rows +...  41.3 us
    pallas_call x2, Pallas kernels, gradient_canvas(): pl.pallas_call(gradient_kernel, out_shape=jax.ShapeDtypeStruct((channels,...  25.2 us
    convert_element_type x2, other arithmetic, split_bf16(): return (high.astype(jnp.bfloat16), (values - high).astype(jnp.bfloat16))  2.35 us

profile of v13, /device:TPU:25, one launch (start us, length us, event | category | flops | bytes accessed | tf_op | source)
XLA Modules:
  0.0 115.2 jit_solution(14550051578008234014)
XLA Ops:
  0.0 1.2 %subtract_convert_fusion = (bf16[1,256,256]{2,1,0:T(8,128)(2,1)S(1)}, bf16[1,256,256]{2,1,0:T(8,128)(2,1)S(1)}) fusion(), kind=kLoop, calls=%fused_computation.9 | loop fusion | flops 1769472 | bytes 262144 | tf_op jit(solution)/shard_map/convert_element_type | solution.py:159
  1.2 1.2 %fusion.6 = (bf16[1,256,256]{2,1,0:T(8,128)(2,1)S(1)}, bf16[1,256,256]{2,1,0:T(8,128)(2,1)S(1)}) fusion(), kind=kLoop, calls=%fused_computation.15 | loop fusion | flops 1638400 | bytes 262144 | tf_op jit(solution)/shard_map/convert_element_type | solution.py:159
  2.4 0.9 pad_maximum_fusion.tables_ref
  3.2 1.3 %fusion.9 = s32[]{:T(128)} fusion(s32[32,1]{0,1:T(1,128)} %param.9, s32[]{:T(128)S(6)} %axis_index.15), kind=kLoop, calls=%fused_computation.19 | loop fusion | flops 95 | bytes 136 | tf_op jit(solution)/shard_map/reduce_sum | solution.py:538
  4.5 23.7 %shard_map.55.ext_ref = f32[2,384,768]{2,1,0:T(8,128)} custom-call(f32[2,128,512]{2,1,0:T(8,128)} %cur_ref.3), custom_call_target="tpu_custom_call" | custom-call | tf_op jit(solution)/shard_map/pallas_call | solution.py:482
  28.3 12.8 %shard_map.56.canvas_ref = f32[3,384,768]{2,1,0:T(8,128)} custom-call(s32[2,2]{1,0:T(2,128)} %bitcast.7, s32[1]{0:T(128)} %bitcast.2.count_ref, f32[2,384,768]{2,1,0:T(8,128)} %shard_map.55.ext_ref, f32[2,256,256]{2,1,0:T(8,128)} %probe_ref.3, f32[2,256,256]{2,1,0:T(8,128)} %bitcast.5, bf16[4,256,256]{2,1,0:T(8,128)(2,1)} %pad_maximum_fusion.tables_ref), custom_call_target="tpu_custom_call" | custom-call | tf_op jit(solution)/shard_map/pallas_call | solution.py:236
  41.1 0.7 broadcast_in_dim.10.light_in_ref
  41.8 26.4 %shard_map.57 = (f32[2,128,512]{2,1,0:T(8,128)}, f32[128,512]{1,0:T(8,128)}) custom-call(f32[3,384,768]{2,1,0:T(8,128)} %shard_map.56.canvas_ref, f32[2,128,512]{2,1,0:T(8,128)} %cur_ref.3, f32[128,512]{1,0:T(8,128)} %broadcast_in_dim.10.light_in_ref), custom_call_target="tpu_custom_call" | custom-call | tf_op jit(solution)/shard_map/pallas_call | solution.py:502
  68.3 17.6 %shard_map.58.ext_ref = f32[2,384,768]{2,1,0:T(8,128)} custom-call(f32[2,128,512]{2,1,0:T(8,128)} %get-tuple-element.8.cur_ref), custom_call_target="tpu_custom_call" | custom-call | tf_op jit(solution)/shard_map/pallas_call | solution.py:482
  85.8 12.3 %shard_map.59.canvas_ref = f32[2,384,768]{2,1,0:T(8,128)} custom-call(s32[2,2]{1,0:T(2,128)} %bitcast.8, s32[1]{0:T(128)} %bitcast.2.count_ref, f32[2,384,768]{2,1,0:T(8,128)} %shard_map.58.ext_ref, f32[2,256,256]{2,1,0:T(8,128)} %probe_ref.3, f32[2,256,256]{2,1,0:T(8,128)} %bitcast.6, bf16[4,256,256]{2,1,0:T(8,128)(2,1)} %pad_maximum_fusion.tables_ref), custom_call_target="tpu_custom_call" | custom-call | tf_op jit(solution)/shard_map/pallas_call | solution.py:236
  98.2 15.1 %shard_map.60 = (f32[2,128,512]{2,1,0:T(8,128)}, f32[128,512]{1,0:T(8,128)}) custom-call(f32[2,384,768]{2,1,0:T(8,128)} %shard_map.59.canvas_ref, f32[2,128,512]{2,1,0:T(8,128)} %get-tuple-element.8.cur_ref, f32[128,512]{1,0:T(8,128)} %get-tuple-element.9.light_in_ref), custom_call_target="tpu_custom_call" | custom-call | tf_op jit(solution)/shard_map/pallas_call | solution.py:502
  113.3 1.9 %copy.7 = f32[2,128,512]{2,1,0:T(8,128)} copy(f32[2,128,512]{2,1,0:T(8,128)} %get-tuple-element.10) | data formatting | bytes 1048576

commit v14 on v13

--- a/solution.py
+++ b/solution.py
@@ -1,6 +1,8 @@
 import math
 
 import jax
+import ml_dtypes
+import numpy as np
 import jax.numpy as jnp
 from jax import lax
 from jax.sharding import PartitionSpec as P
@@ -231,15 +233,28 @@
 KERNEL_PARAMS = pltpu.CompilerParams(vmem_limit_bytes=60 * 1024 * 1024)
 
 
+def split_tables(length):
+    index_values = np.arange(length, dtype=np.int32)
+    product_mod = index_values[:, None] * index_values[None, :] % length
+    angles = product_mod.astype(np.float32) * np.float32(2.0 * math.pi / length)
+    scaling = np.float32(1.0 / math.sqrt(length))
+    parts = []
+    for table in (np.cos(angles) * scaling, -np.sin(angles) * scaling):
+        table = table.astype(np.float32)
+        scaled = table * np.float32(65537.0)
+        high = scaled - (scaled - table)
+        parts += [high.astype(ml_dtypes.bfloat16), (table - high).astype(ml_dtypes.bfloat16)]
+    return jnp.asarray(np.stack(parts))
+
+
 def gradient_canvas(channels, ext_shape, spots, count, extended, probe_field, own_amps, tables):
-    parts = jnp.stack(split_bf16(tables[0]) + split_bf16(tables[1]))
     return pl.pallas_call(
         gradient_kernel,
         out_shape=jax.ShapeDtypeStruct((channels,) + ext_shape, jnp.float32),
         in_specs=[SMEM_SPEC, SMEM_SPEC] + [VMEM_SPEC] * 4,
         out_specs=VMEM_SPEC,
         compiler_params=KERNEL_PARAMS,
-    )(spots, count.reshape(1), extended, probe_field, own_amps, parts)
+    )(spots, count.reshape(1), extended, probe_field, own_amps, tables)
 
 
 def power_canvas(ext_shape, spots, count, probe_field):
@@ -398,7 +413,15 @@
     wait_copies(place, corners)
 
 
-def fold_kernel(canvas_ref, cur_ref, light_in_ref, out_ref, light_ref, mid_bufs, corner_bufs, col_bufs, band_ref, total_ref, send_sems, recv_sems, band_sem):
+def fold_kernel(canvas_ref, cur_ref, *refs):
+    if len(refs) == 10:
+        light_in_ref, refs = None, refs
+    else:
+        light_in_ref, refs = refs[0], refs[1:]
+    fold_body(canvas_ref, cur_ref, light_in_ref, *refs)
+
+
+def fold_body(canvas_ref, cur_ref, light_in_ref, out_ref, light_ref, mid_bufs, corner_bufs, col_bufs, band_ref, total_ref, send_sems, recv_sems, band_sem):
     rows = out_ref.shape[1]
     cols = out_ref.shape[2]
     margin = (canvas_ref.shape[2] - cols) // 2
@@ -505,7 +528,7 @@
             jax.ShapeDtypeStruct((fields, rows, cols), jnp.float32),
             jax.ShapeDtypeStruct((rows, cols), jnp.float32),
         ),
-        in_specs=[pl.BlockSpec(memory_space=pl.ANY), VMEM_SPEC, VMEM_SPEC],
+        in_specs=[pl.BlockSpec(memory_space=pl.ANY), VMEM_SPEC] + ([] if light is None else [VMEM_SPEC]),
         out_specs=(VMEM_SPEC, VMEM_SPEC),
         scratch_shapes=[
             pltpu.VMEM((2, depth, margin, cols), jnp.float32),
@@ -520,7 +543,7 @@
         compiler_params=pltpu.CompilerParams(
             vmem_limit_bytes=60 * 1024 * 1024, has_side_effects=True, collective_id=depth
         ),
-    )(canvas, current, light)
+    )(canvas, current, *([] if light is None else [light]))
 
 
 def on_device(object_field, probe_field, amplitudes, centres, counts):
@@ -528,7 +551,7 @@
     margin = size_probe // 2
     block_rows = object_field.shape[1]
     block_cols = object_field.shape[2]
-    tables = dft_tables(size_probe)
+    tables = split_tables(size_probe)
     spots = centres[0, 0]
     own_amps = amplitudes[0, 0]
     sx_size = lax.axis_size("sx")
@@ -539,7 +562,7 @@
     ext_shape = (block_rows + size_probe, block_cols + size_probe)
 
     current = object_field
-    illumination = jnp.zeros((block_rows, block_cols), jnp.float32)
+    illumination = None
     for sweep_index in range(ITERS):
         extended = exchange_halo(current, margin)
         channels = 3 if sweep_index == 0 else 2

time: 116 us -> 111 us (0.957)
  other arithmetic: 4.51 us -> 1.29 us
    convert_element_type x2 -> x0, other arithmetic: 2.35 us -> none  [split_bf16(): return (high.astype(jnp.bfloat16), (values - high).astype(jnp.bfloat16))]
where the time goes in v14:
time: 111 us
  Pallas kernels  107 us (96%)
  local copies, waits for them, and re-layouts  1.87 us (2%)
  other arithmetic  1.29 us (1%)
    pallas_call x2, Pallas kernels, exchange_halo(): pl.pallas_call(halo_kernel, out_shape=jax.ShapeDtypeStruct((depth, rows +...  41.5 us
    pallas_call x2, Pallas kernels, fold_and_step(): pl.pallas_call(fold_kernel, out_shape=(jax.ShapeDtypeStruct((fields, rows...  40.5 us
    pallas_call x2, Pallas kernels, gradient_canvas(): pl.pallas_call(gradient_kernel, out_shape=jax.ShapeDtypeStruct((channels,...  25.3 us

profile of v14, /device:TPU:25, one launch (start us, length us, event | category | flops | bytes accessed | tf_op | source)
XLA Modules:
  0.0 110.5 jit_solution(1695709417320239087)
XLA Ops:
  0.0 1.3 %fusion = s32[]{:T(128)} fusion(s32[32,1]{0,1:T(1,128)} %param.10, s32[]{:T(128)S(6)} %axis_index.15), kind=kLoop, calls=%fused_computation.1 | loop fusion | flops 95 | bytes 136 | tf_op jit(solution)/shard_map/reduce_sum | solution.py:561
  1.3 23.7 %shard_map.64.ext_ref = f32[2,384,768]{2,1,0:T(8,128)} custom-call(f32[2,128,512]{2,1,0:T(8,128)} %cur_ref.3), custom_call_target="tpu_custom_call" | custom-call | tf_op jit(solution)/shard_map/pallas_call | solution.py:505
  25.0 12.9 %shard_map.65.canvas_ref = f32[3,384,768]{2,1,0:T(8,128)} custom-call(s32[2,2]{1,0:T(2,128)} %bitcast.7, s32[1]{0:T(128)} %bitcast.2.count_ref, f32[2,384,768]{2,1,0:T(8,128)} %shard_map.64.ext_ref, f32[2,256,256]{2,1,0:T(8,128)} %probe_ref.3, f32[2,256,256]{2,1,0:T(8,128)} %bitcast.5, bf16[4,256,256]{2,1,0:T(8,128)(2,1)} %constant.10.clone.tables_ref), custom_call_target="tpu_custom_call" | custom-call | tf_op jit(solution)/shard_map/pallas_call | solution.py:251
  38.0 26.0 %shard_map.66 = (f32[2,128,512]{2,1,0:T(8,128)}, f32[128,512]{1,0:T(8,128)}) custom-call(f32[3,384,768]{2,1,0:T(8,128)} %shard_map.65.canvas_ref, f32[2,128,512]{2,1,0:T(8,128)} %cur_ref.3), custom_call_target="tpu_custom_call" | custom-call | tf_op jit(solution)/shard_map/pallas_call | solution.py:525
  63.9 17.7 %shard_map.67.ext_ref = f32[2,384,768]{2,1,0:T(8,128)} custom-call(f32[2,128,512]{2,1,0:T(8,128)} %get-tuple-element.8.cur_ref), custom_call_target="tpu_custom_call" | custom-call | tf_op jit(solution)/shard_map/pallas_call | solution.py:505
  81.7 12.4 %shard_map.68.canvas_ref = f32[2,384,768]{2,1,0:T(8,128)} custom-call(s32[2,2]{1,0:T(2,128)} %bitcast.8, s32[1]{0:T(128)} %bitcast.2.count_ref, f32[2,384,768]{2,1,0:T(8,128)} %shard_map.67.ext_ref, f32[2,256,256]{2,1,0:T(8,128)} %probe_ref.3, f32[2,256,256]{2,1,0:T(8,128)} %bitcast.6, bf16[4,256,256]{2,1,0:T(8,128)(2,1)} %constant.10.clone.tables_ref), custom_call_target="tpu_custom_call" | custom-call | tf_op jit(solution)/shard_map/pallas_call | solution.py:251
  94.1 14.6 %shard_map.69 = (f32[2,128,512]{2,1,0:T(8,128)}, f32[128,512]{1,0:T(8,128)}) custom-call(f32[2,384,768]{2,1,0:T(8,128)} %shard_map.68.canvas_ref, f32[2,128,512]{2,1,0:T(8,128)} %get-tuple-element.8.cur_ref, f32[128,512]{1,0:T(8,128)} %get-tuple-element.9.refs_0_), custom_call_target="tpu_custom_call" | custom-call | tf_op jit(solution)/shard_map/pallas_call | solution.py:525
  108.6 1.9 %copy.8 = f32[2,128,512]{2,1,0:T(8,128)} copy(f32[2,128,512]{2,1,0:T(8,128)} %get-tuple-element.10) | data formatting | bytes 1048576

commit v15 on v14

--- a/solution.py
+++ b/solution.py
@@ -172,10 +172,11 @@
 def gradient_kernel(spots_ref, count_ref, ext_ref, probe_ref, amps_ref, tables_ref, out_ref):
     size = probe_ref.shape[1]
     out_ref[...] = jnp.zeros(out_ref.shape, jnp.float32)
+    live = count_ref[lax.axis_index("sx")]
     with_power = out_ref.shape[0] > 2
     for slot in range(amps_ref.shape[0]):
 
-        @pl.when(slot < count_ref[0])
+        @pl.when(slot < live)
         def _():
             take, put = window_tools(size, spots_ref[slot, 0], spots_ref[slot, 1])
             probe_real = probe_ref[0]
@@ -254,7 +255,7 @@
         in_specs=[SMEM_SPEC, SMEM_SPEC] + [VMEM_SPEC] * 4,
         out_specs=VMEM_SPEC,
         compiler_params=KERNEL_PARAMS,
-    )(spots, count.reshape(1), extended, probe_field, own_amps, tables)
+    )(spots, count, extended, probe_field, own_amps, tables)
 
 
 def power_canvas(ext_shape, spots, count, probe_field):
@@ -554,11 +555,7 @@
     tables = split_tables(size_probe)
     spots = centres[0, 0]
     own_amps = amplitudes[0, 0]
-    sx_size = lax.axis_size("sx")
-    sx_index = lax.axis_index("sx")
     column_counts = counts[:, 0]
-    sx_positions = jnp.arange(sx_size, dtype=jnp.int32)
-    own_count = jnp.sum(jnp.where(sx_positions == sx_index, column_counts, 0))
     ext_shape = (block_rows + size_probe, block_cols + size_probe)
 
     current = object_field
@@ -567,7 +564,7 @@
         extended = exchange_halo(current, margin)
         channels = 3 if sweep_index == 0 else 2
         canvas = gradient_canvas(
-            channels, ext_shape, spots, own_count, extended, probe_field, own_amps, tables
+            channels, ext_shape, spots, column_counts, extended, probe_field, own_amps, tables
         )
         current, illumination = fold_and_step(canvas, current, illumination, margin)
     return current

time: 111 us -> 110 us (level)
  other arithmetic: 1.29 us -> 0 us
    pallas_call x2, Pallas kernels: 40.5 us -> 41.9 us  [fold_and_step(): pl.pallas_call(fold_kernel, out_shape=(jax.ShapeDtypeStruct((fields, rows...]
    pallas_call x2, Pallas kernels: 25.3 us -> 24 us  [gradient_canvas(): pl.pallas_call(gradient_kernel, out_shape=jax.ShapeDtypeStruct((channels,...]
    reduce_sum x1 -> x0, other arithmetic: 1.29 us -> none  [on_device(): own_count = jnp.sum(jnp.where(sx_positions == sx_index, column_counts, 0))]
where the time goes in v15:
time: 110 us; the launch traced here: 109 us
  Pallas kernels  107 us (97%)
  local copies, waits for them, and re-layouts  1.87 us (2%)
    pallas_call x2, Pallas kernels, fold_and_step(): pl.pallas_call(fold_kernel, out_shape=(jax.ShapeDtypeStruct((fields, rows...  41.9 us
    pallas_call x2, Pallas kernels, exchange_halo(): pl.pallas_call(halo_kernel, out_shape=jax.ShapeDtypeStruct((depth, rows +...  41.5 us
    pallas_call x2, Pallas kernels, gradient_canvas(): pl.pallas_call(gradient_kernel, out_shape=jax.ShapeDtypeStruct((channels,...  24 us

profile of v15, /device:TPU:25, one launch (start us, length us, event | category | flops | bytes accessed | tf_op | source)
XLA Modules:
  0.0 109.3 jit_solution(17269025496976432634)
XLA Ops:
  0.0 23.7 %shard_map.64.ext_ref = f32[2,384,768]{2,1,0:T(8,128)} custom-call(f32[2,128,512]{2,1,0:T(8,128)} %cur_ref.3), custom_call_target="tpu_custom_call" | custom-call | tf_op jit(solution)/shard_map/pallas_call | solution.py:506
  23.8 12.2 %shard_map.65.canvas_ref = f32[3,384,768]{2,1,0:T(8,128)} custom-call(s32[2,2]{1,0:T(2,128)} %bitcast.5, s32[32]{0:T(128)} %bitcast.7, f32[2,384,768]{2,1,0:T(8,128)} %shard_map.64.ext_ref, f32[2,256,256]{2,1,0:T(8,128)} %probe_ref.3, f32[2,256,256]{2,1,0:T(8,128)} %bitcast.3, bf16[4,256,256]{2,1,0:T(8,128)(2,1)} %constant.2.clone.tables_ref), custom_call_target="tpu_custom_call" | custom-call | tf_op jit(solution)/shard_map/pallas_call | solution.py:252
  36.0 26.0 %shard_map.66 = (f32[2,128,512]{2,1,0:T(8,128)}, f32[128,512]{1,0:T(8,128)}) custom-call(f32[3,384,768]{2,1,0:T(8,128)} %shard_map.65.canvas_ref, f32[2,128,512]{2,1,0:T(8,128)} %cur_ref.3), custom_call_target="tpu_custom_call" | custom-call | tf_op jit(solution)/shard_map/pallas_call | solution.py:526
  62.0 17.7 %shard_map.67.ext_ref = f32[2,384,768]{2,1,0:T(8,128)} custom-call(f32[2,128,512]{2,1,0:T(8,128)} %get-tuple-element.8.cur_ref), custom_call_target="tpu_custom_call" | custom-call | tf_op jit(solution)/shard_map/pallas_call | solution.py:506
  79.7 11.7 %shard_map.68.canvas_ref = f32[2,384,768]{2,1,0:T(8,128)} custom-call(s32[2,2]{1,0:T(2,128)} %bitcast.6, s32[32]{0:T(128)} %bitcast.8, f32[2,384,768]{2,1,0:T(8,128)} %shard_map.67.ext_ref, f32[2,256,256]{2,1,0:T(8,128)} %probe_ref.3, f32[2,256,256]{2,1,0:T(8,128)} %bitcast.4, bf16[4,256,256]{2,1,0:T(8,128)(2,1)} %constant.2.clone.tables_ref), custom_call_target="tpu_custom_call" | custom-call | tf_op jit(solution)/shard_map/pallas_call | solution.py:252
  91.5 15.9 %shard_map.69 = (f32[2,128,512]{2,1,0:T(8,128)}, f32[128,512]{1,0:T(8,128)}) custom-call(f32[2,384,768]{2,1,0:T(8,128)} %shard_map.68.canvas_ref, f32[2,128,512]{2,1,0:T(8,128)} %get-tuple-element.8.cur_ref, f32[128,512]{1,0:T(8,128)} %get-tuple-element.9.refs_0_), custom_call_target="tpu_custom_call" | custom-call | tf_op jit(solution)/shard_map/pallas_call | solution.py:526
  107.4 1.9 %copy.8 = f32[2,128,512]{2,1,0:T(8,128)} copy(f32[2,128,512]{2,1,0:T(8,128)} %get-tuple-element.10) | data formatting | bytes 1048576

commit v16 on v15

--- a/solution.py
+++ b/solution.py
@@ -184,33 +184,33 @@
             real_parts = (tables_ref[0], tables_ref[1])
             imag_parts = (tables_ref[2], tables_ref[3])
 
-            def left(field_real, field_imag, sign):
+            def left(field_real, field_imag, conjugate):
                 both = split_bf16(jnp.concatenate([field_real, field_imag], axis=1))
                 by_real = dot_split(real_parts, both)
                 by_imag = dot_split(imag_parts, both)
-                out_real = by_real[:, :size] - sign * by_imag[:, size:]
-                out_imag = by_real[:, size:] + sign * by_imag[:, :size]
-                return out_real, out_imag
-
-            def right(field_real, field_imag, sign):
+                if conjugate:
+                    return by_real[:, :size] + by_imag[:, size:], by_real[:, size:] - by_imag[:, :size]
+                return by_real[:, :size] - by_imag[:, size:], by_real[:, size:] + by_imag[:, :size]
+
+            def right(field_real, field_imag, conjugate):
                 both = split_bf16(jnp.concatenate([field_real, field_imag], axis=0))
                 by_real = dot_split(both, real_parts)
                 by_imag = dot_split(both, imag_parts)
-                out_real = by_real[:size] - sign * by_imag[size:]
-                out_imag = by_imag[:size] * sign + by_real[size:]
-                return out_real, out_imag
+                if conjugate:
+                    return by_real[:size] + by_imag[size:], by_real[size:] - by_imag[:size]
+                return by_real[:size] - by_imag[size:], by_imag[:size] + by_real[size:]
 
             obj_real = take(ext_ref, 0)
             obj_imag = take(ext_ref, 1)
             exit_real = probe_real * obj_real - probe_imag * obj_imag
             exit_imag = probe_real * obj_imag + probe_imag * obj_real
-            half_real, half_imag = left(exit_real, exit_imag, 1.0)
-            far_real, far_imag = right(half_real, half_imag, 1.0)
-            factor = 1.0 - amps_ref[slot] / jnp.sqrt(far_real * far_real + far_imag * far_imag + SMOOTH)
+            half_real, half_imag = left(exit_real, exit_imag, False)
+            far_real, far_imag = right(half_real, half_imag, False)
+            factor = 1.0 - amps_ref[slot] * lax.rsqrt(far_real * far_real + far_imag * far_imag + SMOOTH)
             miss_real = far_real * factor
             miss_imag = far_imag * factor
-            back_real, back_imag = left(miss_real, miss_imag, -1.0)
-            near_real, near_imag = right(back_real, back_imag, -1.0)
+            back_real, back_imag = left(miss_real, miss_imag, True)
+            near_real, near_imag = right(back_real, back_imag, True)
             put(out_ref, 0, probe_real * near_real + probe_imag * near_imag)
             put(out_ref, 1, probe_real * near_imag - probe_imag * near_real)
             if with_power:

time: 110 us -> 110 us (level)
  no operation moved by 1% of the time
where the time goes in v16:
time: 110 us; the launch traced here: 109 us
  Pallas kernels  107 us (97%)
  local copies, waits for them, and re-layouts  1.87 us (2%)
    pallas_call x2, Pallas kernels, fold_and_step(): pl.pallas_call(fold_kernel, out_shape=(jax.ShapeDtypeStruct((fields, rows...  42.2 us
    pallas_call x2, Pallas kernels, exchange_halo(): pl.pallas_call(halo_kernel, out_shape=jax.ShapeDtypeStruct((depth, rows +...  41.3 us
    pallas_call x2, Pallas kernels, gradient_canvas(): pl.pallas_call(gradient_kernel, out_shape=jax.ShapeDtypeStruct((channels,...  23.8 us

profile of v16, /device:TPU:25, one launch (start us, length us, event | category | flops | bytes accessed | tf_op | source)
XLA Modules:
  0.0 109.1 jit_solution(9175432358811583656)
XLA Ops:
  0.0 23.7 %shard_map.64.ext_ref = f32[2,384,768]{2,1,0:T(8,128)} custom-call(f32[2,128,512]{2,1,0:T(8,128)} %cur_ref.3), custom_call_target="tpu_custom_call" | custom-call | tf_op jit(solution)/shard_map/pallas_call | solution.py:506
  23.8 12.2 %shard_map.65.canvas_ref = f32[3,384,768]{2,1,0:T(8,128)} custom-call(s32[2,2]{1,0:T(2,128)} %bitcast.5, s32[32]{0:T(128)} %bitcast.7, f32[2,384,768]{2,1,0:T(8,128)} %shard_map.64.ext_ref, f32[2,256,256]{2,1,0:T(8,128)} %probe_ref.3, f32[2,256,256]{2,1,0:T(8,128)} %bitcast.3, bf16[4,256,256]{2,1,0:T(8,128)(2,1)} %constant.2.clone.tables_ref), custom_call_target="tpu_custom_call" | custom-call | tf_op jit(solution)/shard_map/pallas_call | solution.py:252
  35.9 26.4 %shard_map.66 = (f32[2,128,512]{2,1,0:T(8,128)}, f32[128,512]{1,0:T(8,128)}) custom-call(f32[3,384,768]{2,1,0:T(8,128)} %shard_map.65.canvas_ref, f32[2,128,512]{2,1,0:T(8,128)} %cur_ref.3), custom_call_target="tpu_custom_call" | custom-call | tf_op jit(solution)/shard_map/pallas_call | solution.py:526
  62.3 17.6 %shard_map.67.ext_ref = f32[2,384,768]{2,1,0:T(8,128)} custom-call(f32[2,128,512]{2,1,0:T(8,128)} %get-tuple-element.8.cur_ref), custom_call_target="tpu_custom_call" | custom-call | tf_op jit(solution)/shard_map/pallas_call | solution.py:506
  79.8 11.6 %shard_map.68.canvas_ref = f32[2,384,768]{2,1,0:T(8,128)} custom-call(s32[2,2]{1,0:T(2,128)} %bitcast.6, s32[32]{0:T(128)} %bitcast.8, f32[2,384,768]{2,1,0:T(8,128)} %shard_map.67.ext_ref, f32[2,256,256]{2,1,0:T(8,128)} %probe_ref.3, f32[2,256,256]{2,1,0:T(8,128)} %bitcast.4, bf16[4,256,256]{2,1,0:T(8,128)(2,1)} %constant.2.clone.tables_ref), custom_call_target="tpu_custom_call" | custom-call | tf_op jit(solution)/shard_map/pallas_call | solution.py:252
  91.4 15.8 %shard_map.69 = (f32[2,128,512]{2,1,0:T(8,128)}, f32[128,512]{1,0:T(8,128)}) custom-call(f32[2,384,768]{2,1,0:T(8,128)} %shard_map.68.canvas_ref, f32[2,128,512]{2,1,0:T(8,128)} %get-tuple-element.8.cur_ref, f32[128,512]{1,0:T(8,128)} %get-tuple-element.9.refs_0_), custom_call_target="tpu_custom_call" | custom-call | tf_op jit(solution)/shard_map/pallas_call | solution.py:526
  107.3 1.9 %copy.8 = f32[2,128,512]{2,1,0:T(8,128)} copy(f32[2,128,512]{2,1,0:T(8,128)} %get-tuple-element.10) | data formatting | bytes 1048576

commit v17 on v15

--- a/solution.py
+++ b/solution.py
@@ -169,9 +169,12 @@
     return total + jnp.dot(left_low, right_high, preferred_element_type=jnp.float32)
 
 
-def gradient_kernel(spots_ref, count_ref, ext_ref, probe_ref, amps_ref, tables_ref, out_ref):
+def gradient_kernel(spots_ref, count_ref, ext_hbm, probe_ref, amps_ref, tables_ref, out_ref, ext_ref, ext_sem):
     size = probe_ref.shape[1]
+    fetch = pltpu.make_async_copy(ext_hbm, ext_ref, ext_sem)
+    fetch.start()
     out_ref[...] = jnp.zeros(out_ref.shape, jnp.float32)
+    fetch.wait()
     live = count_ref[lax.axis_index("sx")]
     with_power = out_ref.shape[0] > 2
     for slot in range(amps_ref.shape[0]):
@@ -252,8 +255,9 @@
     return pl.pallas_call(
         gradient_kernel,
         out_shape=jax.ShapeDtypeStruct((channels,) + ext_shape, jnp.float32),
-        in_specs=[SMEM_SPEC, SMEM_SPEC] + [VMEM_SPEC] * 4,
+        in_specs=[SMEM_SPEC, SMEM_SPEC, pl.BlockSpec(memory_space=pl.ANY)] + [VMEM_SPEC] * 3,
         out_specs=VMEM_SPEC,
+        scratch_shapes=[pltpu.VMEM(extended.shape, jnp.float32), pltpu.SemaphoreType.DMA(())],
         compiler_params=KERNEL_PARAMS,
     )(spots, count, extended, probe_field, own_amps, tables)
 

time: 110 us -> 112 us (1.018)
  Pallas kernels: 107 us -> 109 us
    pallas_call x2, Pallas kernels: 41.9 us -> 50.5 us  [fold_and_step(): pl.pallas_call(fold_kernel, out_shape=(jax.ShapeDtypeStruct((fields, rows...]
    pallas_call x2, Pallas kernels: 24 us -> 17.5 us  [gradient_canvas(): pl.pallas_call(gradient_kernel, out_shape=jax.ShapeDtypeStruct((channels,...]
where the time goes in v17:
time: 112 us; the launch traced here: 111 us
  Pallas kernels  109 us (97%)
  local copies, waits for them, and re-layouts  1.87 us (2%)
    pallas_call x2, Pallas kernels, fold_and_step(): pl.pallas_call(fold_kernel, out_shape=(jax.ShapeDtypeStruct((fields, rows...  50.5 us
    pallas_call x2, Pallas kernels, exchange_halo(): pl.pallas_call(halo_kernel, out_shape=jax.ShapeDtypeStruct((depth, rows +...  41.3 us
    pallas_call x2, Pallas kernels, gradient_canvas(): pl.pallas_call(gradient_kernel, out_shape=jax.ShapeDtypeStruct((channels,...  17.5 us

profile of v17, /device:TPU:25, one launch (start us, length us, event | category | flops | bytes accessed | tf_op | source)
XLA Modules:
  0.0 111.2 jit_solution(3535570057710522078)
XLA Ops:
  0.0 23.7 %shard_map.64.ext_hbm = f32[2,384,768]{2,1,0:T(8,128)} custom-call(f32[2,128,512]{2,1,0:T(8,128)} %cur_ref.3), custom_call_target="tpu_custom_call" | custom-call | tf_op jit(solution)/shard_map/pallas_call | solution.py:510
  23.8 8.9 %shard_map.65.canvas_ref = f32[3,384,768]{2,1,0:T(8,128)} custom-call(s32[2,2]{1,0:T(2,128)} %bitcast.5, s32[32]{0:T(128)} %bitcast.7, f32[2,384,768]{2,1,0:T(8,128)} %shard_map.64.ext_hbm, f32[2,256,256]{2,1,0:T(8,128)} %probe_ref.3, f32[2,256,256]{2,1,0:T(8,128)} %bitcast.3, bf16[4,256,256]{2,1,0:T(8,128)(2,1)} %constant.2.clone.tables_ref), custom_call_target="tpu_custom_call" | custom-call | tf_op jit(solution)/shard_map/pallas_call | solution.py:255
  32.6 30.6 %shard_map.66 = (f32[2,128,512]{2,1,0:T(8,128)}, f32[128,512]{1,0:T(8,128)}) custom-call(f32[3,384,768]{2,1,0:T(8,128)} %shard_map.65.canvas_ref, f32[2,128,512]{2,1,0:T(8,128)} %cur_ref.3), custom_call_target="tpu_custom_call" | custom-call | tf_op jit(solution)/shard_map/pallas_call | solution.py:530
  63.3 17.6 %shard_map.67.ext_hbm = f32[2,384,768]{2,1,0:T(8,128)} custom-call(f32[2,128,512]{2,1,0:T(8,128)} %get-tuple-element.8.cur_ref), custom_call_target="tpu_custom_call" | custom-call | tf_op jit(solution)/shard_map/pallas_call | solution.py:510
  80.8 8.6 %shard_map.68.canvas_ref = f32[2,384,768]{2,1,0:T(8,128)} custom-call(s32[2,2]{1,0:T(2,128)} %bitcast.6, s32[32]{0:T(128)} %bitcast.8, f32[2,384,768]{2,1,0:T(8,128)} %shard_map.67.ext_hbm, f32[2,256,256]{2,1,0:T(8,128)} %probe_ref.3, f32[2,256,256]{2,1,0:T(8,128)} %bitcast.4, bf16[4,256,256]{2,1,0:T(8,128)(2,1)} %constant.2.clone.tables_ref), custom_call_target="tpu_custom_call" | custom-call | tf_op jit(solution)/shard_map/pallas_call | solution.py:255
  89.4 19.9 %shard_map.69 = (f32[2,128,512]{2,1,0:T(8,128)}, f32[128,512]{1,0:T(8,128)}) custom-call(f32[2,384,768]{2,1,0:T(8,128)} %shard_map.68.canvas_ref, f32[2,128,512]{2,1,0:T(8,128)} %get-tuple-element.8.cur_ref, f32[128,512]{1,0:T(8,128)} %get-tuple-element.9.refs_0_), custom_call_target="tpu_custom_call" | custom-call | tf_op jit(solution)/shard_map/pallas_call | solution.py:530
  109.4 1.9 %copy.8 = f32[2,128,512]{2,1,0:T(8,128)} copy(f32[2,128,512]{2,1,0:T(8,128)} %get-tuple-element.10) | data formatting | bytes 1048576

commit v18 on v15

--- a/solution.py
+++ b/solution.py
@@ -1,3 +1,4 @@
+import functools
 import math
 
 import jax
@@ -414,15 +415,19 @@
     wait_copies(place, corners)
 
 
-def fold_kernel(canvas_ref, cur_ref, *refs):
+def fold_kernel(apply_step, canvas_ref, cur_ref, *refs):
     if len(refs) == 10:
         light_in_ref, refs = None, refs
     else:
         light_in_ref, refs = refs[0], refs[1:]
-    fold_body(canvas_ref, cur_ref, light_in_ref, *refs)
-
-
-def fold_body(canvas_ref, cur_ref, light_in_ref, out_ref, light_ref, mid_bufs, corner_bufs, col_bufs, band_ref, total_ref, send_sems, recv_sems, band_sem):
+    fold_body(apply_step, canvas_ref, cur_ref, light_in_ref, *refs)
+
+
+def step_kernel(cur_ref, grad_ref, light_ref, out_ref):
+    out_ref[...] = cur_ref[...] - grad_ref[...] / (light_ref[...] + DAMPING)
+
+
+def fold_body(apply_step, canvas_ref, cur_ref, light_in_ref, out_ref, light_ref, mid_bufs, corner_bufs, col_bufs, band_ref, total_ref, send_sems, recv_sems, band_sem):
     rows = out_ref.shape[1]
     cols = out_ref.shape[2]
     margin = (canvas_ref.shape[2] - cols) // 2
@@ -498,7 +503,10 @@
         light_ref[...] = total_ref[fields]
     else:
         light_ref[...] = light_in_ref[...]
-    out_ref[...] = cur_ref[...] - total_ref[0:fields] / (light_ref[...] + DAMPING)
+    if apply_step:
+        out_ref[...] = cur_ref[...] - total_ref[0:fields] / (light_ref[...] + DAMPING)
+    else:
+        out_ref[...] = total_ref[0:fields]
 
 
 def exchange_halo(current, margin):
@@ -520,11 +528,11 @@
     )(current)
 
 
-def fold_and_step(canvas, current, light, margin):
+def fold_and_step(canvas, current, light, margin, apply_step=True):
     depth, ext_rows, ext_cols = canvas.shape
     fields, rows, cols = current.shape
     return pl.pallas_call(
-        fold_kernel,
+        functools.partial(fold_kernel, apply_step),
         out_shape=(
             jax.ShapeDtypeStruct((fields, rows, cols), jnp.float32),
             jax.ShapeDtypeStruct((rows, cols), jnp.float32),
@@ -566,7 +574,16 @@
         canvas = gradient_canvas(
             channels, ext_shape, spots, column_counts, extended, probe_field, own_amps, tables
         )
-        current, illumination = fold_and_step(canvas, current, illumination, margin)
+        if sweep_index < ITERS - 1:
+            current, illumination = fold_and_step(canvas, current, illumination, margin)
+        else:
+            gradient, _ = fold_and_step(canvas, current, illumination, margin, apply_step=False)
+            current = pl.pallas_call(
+                step_kernel,
+                out_shape=jax.ShapeDtypeStruct(current.shape, jnp.float32),
+                in_specs=[VMEM_SPEC] * 3,
+                out_specs=VMEM_SPEC,
+            )(current, gradient, illumination)
     return current
 
 

time: 110 us -> 108 us (0.982)
  local copies, waits for them, and re-layouts: 1.87 us -> 0 us
    unnamed x1 -> x0, local copies, waits for them, and re-layouts: 1.87 us -> none
    pallas_call x2 -> x3, Pallas kernels: 41.9 us -> 42 us  [the longest x2 39.9 us: fold_and_step(): pl.pallas_call(functools.partial(fold_kernel, apply_step), out_shape=(jax...]
where the time goes in v18:
time: 108 us
  Pallas kernels  108 us (100%)
    pallas_call x2, Pallas kernels, exchange_halo(): pl.pallas_call(halo_kernel, out_shape=jax.ShapeDtypeStruct((depth, rows +...  42.1 us
    pallas_call x2, Pallas kernels, fold_and_step(): pl.pallas_call(functools.partial(fold_kernel, apply_step), out_shape=(jax...  39.9 us
    pallas_call x2, Pallas kernels, gradient_canvas(): pl.pallas_call(gradient_kernel, out_shape=jax.ShapeDtypeStruct((channels,...  24 us

profile of v18, /device:TPU:25, one launch (start us, length us, event | category | flops | bytes accessed | tf_op | source)
XLA Modules:
  0.0 108.2 jit_solution(403150249573622397)
XLA Ops:
  0.0 23.7 %shard_map.64.ext_ref = f32[2,384,768]{2,1,0:T(8,128)} custom-call(f32[2,128,512]{2,1,0:T(8,128)} %cur_ref.3), custom_call_target="tpu_custom_call" | custom-call | tf_op jit(solution)/shard_map/pallas_call | solution.py:514
  23.8 12.3 %shard_map.65.canvas_ref = f32[3,384,768]{2,1,0:T(8,128)} custom-call(s32[2,2]{1,0:T(2,128)} %bitcast.5, s32[32]{0:T(128)} %bitcast.7, f32[2,384,768]{2,1,0:T(8,128)} %shard_map.64.ext_ref, f32[2,256,256]{2,1,0:T(8,128)} %probe_ref.3, f32[2,256,256]{2,1,0:T(8,128)} %bitcast.3, bf16[4,256,256]{2,1,0:T(8,128)(2,1)} %constant.2.clone.tables_ref), custom_call_target="tpu_custom_call" | custom-call | tf_op jit(solution)/shard_map/pallas_call | solution.py:253
  36.0 23.2 %shard_map.66 = (f32[2,128,512]{2,1,0:T(8,128)}, f32[128,512]{1,0:T(8,128)}) custom-call(f32[3,384,768]{2,1,0:T(8,128)} %shard_map.65.canvas_ref, f32[2,128,512]{2,1,0:T(8,128)} %cur_ref.3), custom_call_target="tpu_custom_call" | custom-call | tf_op jit(solution)/shard_map/pallas_call | solution.py:534
  59.3 18.3 %shard_map.67.ext_ref = f32[2,384,768]{2,1,0:T(8,128)} custom-call(f32[2,128,512]{2,1,0:T(8,128)} %get-tuple-element.8.cur_ref), custom_call_target="tpu_custom_call" | custom-call | tf_op jit(solution)/shard_map/pallas_call | solution.py:514
  77.6 11.8 %shard_map.68.canvas_ref = f32[2,384,768]{2,1,0:T(8,128)} custom-call(s32[2,2]{1,0:T(2,128)} %bitcast.6, s32[32]{0:T(128)} %bitcast.8, f32[2,384,768]{2,1,0:T(8,128)} %shard_map.67.ext_ref, f32[2,256,256]{2,1,0:T(8,128)} %probe_ref.3, f32[2,256,256]{2,1,0:T(8,128)} %bitcast.4, bf16[4,256,256]{2,1,0:T(8,128)(2,1)} %constant.2.clone.tables_ref), custom_call_target="tpu_custom_call" | custom-call | tf_op jit(solution)/shard_map/pallas_call | solution.py:253
  89.4 16.7 %shard_map.69 = (f32[2,128,512]{2,1,0:T(8,128)}, f32[128,512]{1,0:T(8,128)}) custom-call(f32[2,384,768]{2,1,0:T(8,128)} %shard_map.68.canvas_ref, f32[2,128,512]{2,1,0:T(8,128)} %get-tuple-element.8.cur_ref, f32[128,512]{1,0:T(8,128)} %get-tuple-element.9.refs_0_.light_ref), custom_call_target="tpu_custom_call" | custom-call | tf_op jit(solution)/shard_map/pallas_call | solution.py:534
  106.1 2.1 %shard_map.70 = f32[2,128,512]{2,1,0:T(8,128)} custom-call(f32[2,128,512]{2,1,0:T(8,128)} %get-tuple-element.8.cur_ref, f32[2,128,512]{2,1,0:T(8,128)} %get-tuple-element.10.grad_ref, f32[128,512]{1,0:T(8,128)} %get-tuple-element.9.refs_0_.light_ref), custom_call_target="tpu_custom_call" | custom-call | tf_op jit(solution)/shard_map/pallas_call | solution.py:581

commit v19 on v15

--- a/solution.py
+++ b/solution.py
@@ -169,8 +169,33 @@
     return total + jnp.dot(left_low, right_high, preferred_element_type=jnp.float32)
 
 
-def gradient_kernel(spots_ref, count_ref, ext_ref, probe_ref, amps_ref, tables_ref, out_ref):
+def light_block(size, infos_ref, probe_ref, light_ref, power_ref):
+    rows, cols = light_ref.shape
+    margin = size // 2
+    power_ref[...] = jnp.zeros(power_ref.shape, jnp.float32)
+    power = probe_ref[0] * probe_ref[0] + probe_ref[1] * probe_ref[1]
+    for place in range(9):
+        dr = place // 3 - 1
+        dc = place % 3 - 1
+        for slot in range(2):
+
+            @pl.when(slot < infos_ref[place, 0, 4])
+            def _():
+                row = dr * rows + infos_ref[place, 0, 2 * slot] + margin
+                col = dc * cols + infos_ref[place, 0, 2 * slot + 1] + cols
+                _, put = window_tools(size, row, col)
+                put(power_ref, 0, power)
+
+    light_ref[...] = power_ref[0, size : size + rows, cols + margin : 2 * cols + margin]
+
+
+def gradient_kernel(spots_ref, count_ref, ext_ref, probe_ref, amps_ref, tables_ref, *rest):
     size = probe_ref.shape[1]
+    if len(rest) > 1:
+        infos_ref, out_ref, light_ref, power_ref = rest
+        light_block(size, infos_ref, probe_ref, light_ref, power_ref)
+    else:
+        (out_ref,) = rest
     out_ref[...] = jnp.zeros(out_ref.shape, jnp.float32)
     live = count_ref[lax.axis_index("sx")]
     with_power = out_ref.shape[0] > 2
@@ -248,14 +273,29 @@
     return jnp.asarray(np.stack(parts))
 
 
-def gradient_canvas(channels, ext_shape, spots, count, extended, probe_field, own_amps, tables):
+def gradient_canvas(channels, ext_shape, spots, count, extended, probe_field, own_amps, tables, infos=None):
+    rows = ext_shape[0] - probe_field.shape[1]
+    cols = ext_shape[1] - probe_field.shape[1]
+    size = probe_field.shape[1]
+    out_shape = jax.ShapeDtypeStruct((channels,) + ext_shape, jnp.float32)
+    in_specs = [SMEM_SPEC, SMEM_SPEC] + [VMEM_SPEC] * 4
+    args = [spots, count, extended, probe_field, own_amps, tables]
+    scratch = []
+    out_specs = VMEM_SPEC
+    if infos is not None:
+        out_shape = (out_shape, jax.ShapeDtypeStruct((rows, cols), jnp.float32))
+        out_specs = (VMEM_SPEC, VMEM_SPEC)
+        in_specs.append(SMEM_SPEC)
+        args.append(infos)
+        scratch = [pltpu.VMEM((1, 2 * rows + size // 2 + size + 8, 3 * cols + size), jnp.float32)]
     return pl.pallas_call(
         gradient_kernel,
-        out_shape=jax.ShapeDtypeStruct((channels,) + ext_shape, jnp.float32),
-        in_specs=[SMEM_SPEC, SMEM_SPEC] + [VMEM_SPEC] * 4,
-        out_specs=VMEM_SPEC,
+        out_shape=out_shape,
+        in_specs=in_specs,
+        out_specs=out_specs,
+        scratch_shapes=scratch,
         compiler_params=KERNEL_PARAMS,
-    )(spots, count, extended, probe_field, own_amps, tables)
+    )(*args)
 
 
 def power_canvas(ext_shape, spots, count, probe_field):
@@ -339,7 +379,7 @@
     wait_copies(place, start_copies(place, pieces, send_sems, recv_sems))
 
 
-def halo_kernel(cur_ref, ext_ref, zeros_ref, send_sems, recv_sems, local_sems):
+def halo_kernel(cur_ref, info_ref, ext_ref, infos_ref, zeros_ref, send_sems, recv_sems, local_sems):
     rows = cur_ref.shape[1]
     cols = cur_ref.shape[2]
     margin = (ext_ref.shape[2] - cols) // 2
@@ -349,6 +389,8 @@
     middle = slice(margin, margin + rows)
     own = pltpu.make_async_copy(cur_ref, ext_ref.at[:, middle, margin : margin + cols], local_sems.at[0])
     own.start()
+    infos_ref[...] = jnp.zeros(infos_ref.shape, jnp.int32)
+    infos_ref[4] = info_ref[...]
     zeros_ref[...] = jnp.zeros(zeros_ref.shape, jnp.float32)
     unreached = [
         ((0, 1), ext_ref.at[:, middle, 0:margin], zeros_ref.at[:, :, 0:margin]),
@@ -388,9 +430,11 @@
         [
             ((0, -1), cur_ref.at[:, :, 0:margin], ext_ref.at[:, middle, right]),
             ((0, 1), cur_ref.at[:, :, cols - margin : cols], ext_ref.at[:, middle, left]),
-        ],
-        send_sems.at[2:4],
-        recv_sems.at[2:4],
+            ((0, -1), info_ref, infos_ref.at[5]),
+            ((0, 1), info_ref, infos_ref.at[3]),
+        ],
+        send_sems.at[8:12],
+        recv_sems.at[8:12],
     )
     own.wait()
     for blank, missing in blanks:
@@ -406,9 +450,11 @@
             ((-1, 0), ext_ref.at[:, middle, right], ext_ref.at[:, below, right]),
             ((1, 0), ext_ref.at[:, middle, left], ext_ref.at[:, above, left]),
             ((1, 0), ext_ref.at[:, middle, right], ext_ref.at[:, above, right]),
-        ],
-        send_sems.at[4:8],
-        recv_sems.at[4:8],
+            ((-1, 0), infos_ref.at[3:6], infos_ref.at[6:9]),
+            ((1, 0), infos_ref.at[3:6], infos_ref.at[0:3]),
+        ],
+        send_sems.at[2:8],
+        recv_sems.at[2:8],
     )
     wait_copies(place, bands)
     wait_copies(place, corners)
@@ -501,23 +547,26 @@
     out_ref[...] = cur_ref[...] - total_ref[0:fields] / (light_ref[...] + DAMPING)
 
 
-def exchange_halo(current, margin):
+def exchange_halo(current, info, margin):
     depth, rows, cols = current.shape
     return pl.pallas_call(
         halo_kernel,
-        out_shape=jax.ShapeDtypeStruct((depth, rows + 2 * margin, cols + 2 * margin), jnp.float32),
-        in_specs=[VMEM_SPEC],
-        out_specs=pl.BlockSpec(memory_space=pl.ANY),
+        out_shape=(
+            jax.ShapeDtypeStruct((depth, rows + 2 * margin, cols + 2 * margin), jnp.float32),
+            jax.ShapeDtypeStruct((9,) + info.shape, jnp.int32),
+        ),
+        in_specs=[VMEM_SPEC, VMEM_SPEC],
+        out_specs=(pl.BlockSpec(memory_space=pl.ANY), VMEM_SPEC),
         scratch_shapes=[
             pltpu.VMEM((depth, margin, cols + 2 * margin), jnp.float32),
-            pltpu.SemaphoreType.DMA((8,)),
-            pltpu.SemaphoreType.DMA((8,)),
+            pltpu.SemaphoreType.DMA((12,)),
+            pltpu.SemaphoreType.DMA((12,)),
             pltpu.SemaphoreType.DMA((5,)),
         ],
         compiler_params=pltpu.CompilerParams(
             vmem_limit_bytes=60 * 1024 * 1024, has_side_effects=True, collective_id=0
         ),
-    )(current)
+    )(current, info)
 
 
 def fold_and_step(canvas, current, light, margin):
@@ -558,15 +607,22 @@
     column_counts = counts[:, 0]
     ext_shape = (block_rows + size_probe, block_cols + size_probe)
 
+    live = jnp.sum(jnp.where(jnp.arange(column_counts.shape[0]) == lax.axis_index("sx"), column_counts, 0))
+    info = jnp.zeros((8, 128), jnp.int32).at[0, 0:5].set(
+        jnp.concatenate([spots.reshape(-1), live.reshape(1)]).astype(jnp.int32)
+    )
     current = object_field
-    illumination = None
-    for sweep_index in range(ITERS):
-        extended = exchange_halo(current, margin)
-        channels = 3 if sweep_index == 0 else 2
+    extended, infos = exchange_halo(current, info, margin)
+    canvas, illumination = gradient_canvas(
+        2, ext_shape, spots, column_counts, extended, probe_field, own_amps, tables, infos
+    )
+    current, _ = fold_and_step(canvas, current, illumination, margin)
+    for sweep_index in range(1, ITERS):
+        extended, _ = exchange_halo(current, info, margin)
         canvas = gradient_canvas(
-            channels, ext_shape, spots, column_counts, extended, probe_field, own_amps, tables
+            2, ext_shape, spots, column_counts, extended, probe_field, own_amps, tables
         )
-        current, illumination = fold_and_step(canvas, current, illumination, margin)
+        current, _ = fold_and_step(canvas, current, illumination, margin)
     return current
 
 

time: 110 us -> 117 us (1.064)
  Pallas kernels: 107 us -> 110 us
  other arithmetic: 0 us -> 2.01 us
  local copies, waits for them, and re-layouts: 1.87 us -> 3.23 us
    pallas_call x4, Pallas kernels: 65.4 us -> 74 us  [the longest x2 45.9 us: exchange_halo(): pl.pallas_call(halo_kernel, out_shape=(jax.ShapeDtypeStruct((depth, rows...]
    pallas_call x2, Pallas kernels: 41.9 us -> 36.5 us  [fold_and_step(): pl.pallas_call(fold_kernel, out_shape=(jax.ShapeDtypeStruct((fields, rows...]
    reduce_sum x0 -> x1, other arithmetic: none -> 1.29 us  [on_device(): jnp.sum(jnp.where(jnp.arange(column_counts.shape[0]) == lax.axis_index('s...]
where the time goes in v19:
time: 117 us; the launch traced here: 116 us
  Pallas kernels  110 us (94%)
  local copies, waits for them, and re-layouts  3.23 us (3%)
  other arithmetic  2.01 us (2%)
    pallas_call x2, Pallas kernels, exchange_halo(): pl.pallas_call(halo_kernel, out_shape=(jax.ShapeDtypeStruct((depth, rows...  45.9 us
    pallas_call x2, Pallas kernels, fold_and_step(): pl.pallas_call(fold_kernel, out_shape=(jax.ShapeDtypeStruct((fields, rows...  36.5 us
    pallas_call x2, Pallas kernels, gradient_canvas(): pl.pallas_call(gradient_kernel, out_shape=out_shape, in_specs=in_specs, o...  28 us

profile of v19, /device:TPU:25, one launch (start us, length us, event | category | flops | bytes accessed | tf_op | source)
XLA Modules:
  0.0 115.7 jit_solution(6937571646072782211)
XLA Ops:
  0.0 1.3 %fusion = s32[]{:T(128)} fusion(s32[]{:T(128)S(6)} %axis_index.15, s32[32,1]{0,1:T(1,128)} %param.12), kind=kLoop, calls=%fused_computation.1 | loop fusion | flops 95 | bytes 136 | tf_op jit(solution)/shard_map/reduce_sum | solution.py:610
  1.3 0.8 reshape_squeeze.3
  2.1 0.7 add_bitcast_fusion
  2.8 0.6 scatter.4.info_ref
  3.4 24.4 %shard_map.64 = (f32[2,384,768]{2,1,0:T(8,128)}, s32[9,8,128]{2,1,0:T(8,128)}) custom-call(f32[2,128,512]{2,1,0:T(8,128)} %cur_ref.3, s32[8,128]{1,0:T(8,128)} %scatter.4.info_ref), custom_call_target="tpu_custom_call" | custom-call | tf_op jit(solution)/shard_map/pallas_call | solution.py:552
  27.8 16.5 %shard_map.65 = (f32[2,384,768]{2,1,0:T(8,128)}, f32[128,512]{1,0:T(8,128)}) custom-call(s32[2,2]{1,0:T(2,128)} %bitcast.9, s32[32]{0:T(128)} %bitcast.11, f32[2,384,768]{2,1,0:T(8,128)} %get-tuple-element.24.ext_ref, f32[2,256,256]{2,1,0:T(8,128)} %probe_ref.3, f32[2,256,256]{2,1,0:T(8,128)} %bitcast.7, bf16[4,256,256]{2,1,0:T(8,128)(2,1)} %constant.36.clone.tables_ref, ...), custom_call_target="tpu_custom_call" | custom-call | tf_op jit(solution)/shard_map/pallas_call | solution.py:291
  44.3 21.1 %shard_map.66 = (f32[2,128,512]{2,1,0:T(8,128)}, f32[128,512]{1,0:T(8,128)}) custom-call(f32[2,384,768]{2,1,0:T(8,128)} %get-tuple-element.26.canvas_ref, f32[2,128,512]{2,1,0:T(8,128)} %cur_ref.3, f32[128,512]{1,0:T(8,128)} %get-tuple-element.27.refs_0_), custom_call_target="tpu_custom_call" | custom-call | tf_op jit(solution)/shard_map/pallas_call | solution.py:575
  65.3 21.5 %shard_map.67 = (f32[2,384,768]{2,1,0:T(8,128)}, s32[9,8,128]{2,1,0:T(8,128)}) custom-call(f32[2,128,512]{2,1,0:T(8,128)} %get-tuple-element.28.cur_ref, s32[8,128]{1,0:T(8,128)} %scatter.4.info_ref), custom_call_target="tpu_custom_call" | custom-call | tf_op jit(solution)/shard_map/pallas_call | solution.py:552
  86.8 11.6 %shard_map.68.canvas_ref = f32[2,384,768]{2,1,0:T(8,128)} custom-call(s32[2,2]{1,0:T(2,128)} %bitcast.10, s32[32]{0:T(128)} %bitcast.12, f32[2,384,768]{2,1,0:T(8,128)} %get-tuple-element.29.ext_ref, f32[2,256,256]{2,1,0:T(8,128)} %probe_ref.3, f32[2,256,256]{2,1,0:T(8,128)} %bitcast.8, bf16[4,256,256]{2,1,0:T(8,128)(2,1)} %constant.36.clone.tables_ref), custom_call_target="tpu_custom_call" | custom-call | tf_op jit(solution)/shard_map/pallas_call | solution.py:291
  98.4 15.4 %shard_map.69 = (f32[2,128,512]{2,1,0:T(8,128)}, f32[128,512]{1,0:T(8,128)}) custom-call(f32[2,384,768]{2,1,0:T(8,128)} %shard_map.68.canvas_ref, f32[2,128,512]{2,1,0:T(8,128)} %get-tuple-element.28.cur_ref, f32[128,512]{1,0:T(8,128)} %get-tuple-element.27.refs_0_), custom_call_target="tpu_custom_call" | custom-call | tf_op jit(solution)/shard_map/pallas_call | solution.py:575
  113.8 1.9 %copy.8 = f32[2,128,512]{2,1,0:T(8,128)} copy(f32[2,128,512]{2,1,0:T(8,128)} %get-tuple-element.30) | data formatting | bytes 1048576

commit v20 on v15

--- a/solution.py
+++ b/solution.py
@@ -374,6 +374,15 @@
     inner = slice(margin, margin + cols)
     left = slice(0, margin)
     right = slice(margin + cols, ext_cols)
+    strips = start_copies(
+        place,
+        [
+            ((0, -1), cur_ref.at[:, :, 0:margin], ext_ref.at[:, middle, right]),
+            ((0, 1), cur_ref.at[:, :, cols - margin : cols], ext_ref.at[:, middle, left]),
+        ],
+        send_sems.at[2:4],
+        recv_sems.at[2:4],
+    )
     bands = start_copies(
         place,
         [
@@ -383,15 +392,7 @@
         send_sems.at[0:2],
         recv_sems.at[0:2],
     )
-    swap(
-        place,
-        [
-            ((0, -1), cur_ref.at[:, :, 0:margin], ext_ref.at[:, middle, right]),
-            ((0, 1), cur_ref.at[:, :, cols - margin : cols], ext_ref.at[:, middle, left]),
-        ],
-        send_sems.at[2:4],
-        recv_sems.at[2:4],
-    )
+    wait_copies(place, strips)
     own.wait()
     for blank, missing in blanks:
 

time: 110 us -> 110 us (level)
    pallas_call x2, Pallas kernels: 41.9 us -> 50.2 us  [fold_and_step(): pl.pallas_call(fold_kernel, out_shape=(jax.ShapeDtypeStruct((fields, rows...]
    pallas_call x2, Pallas kernels: 24 us -> 16 us  [gradient_canvas(): pl.pallas_call(gradient_kernel, out_shape=jax.ShapeDtypeStruct((channels,...]
where the time goes in v20:
time: 110 us; the launch traced here: 109 us
  Pallas kernels  107 us (97%)
  local copies, waits for them, and re-layouts  1.87 us (2%)
    pallas_call x2, Pallas kernels, fold_and_step(): pl.pallas_call(fold_kernel, out_shape=(jax.ShapeDtypeStruct((fields, rows...  50.2 us
    pallas_call x2, Pallas kernels, exchange_halo(): pl.pallas_call(halo_kernel, out_shape=jax.ShapeDtypeStruct((depth, rows +...  41.3 us
    pallas_call x2, Pallas kernels, gradient_canvas(): pl.pallas_call(gradient_kernel, out_shape=jax.ShapeDtypeStruct((channels,...  16 us

profile of v20, /device:TPU:25, one launch (start us, length us, event | category | flops | bytes accessed | tf_op | source)
XLA Modules:
  0.0 109.4 jit_solution(3592524855162695038)
XLA Ops:
  0.0 23.7 %shard_map.64.ext_ref = f32[2,384,768]{2,1,0:T(8,128)} custom-call(f32[2,128,512]{2,1,0:T(8,128)} %cur_ref.3), custom_call_target="tpu_custom_call" | custom-call | tf_op jit(solution)/shard_map/pallas_call | solution.py:507
  23.8 8.2 %shard_map.65.canvas_ref = f32[3,384,768]{2,1,0:T(8,128)} custom-call(s32[2,2]{1,0:T(2,128)} %bitcast.5, s32[32]{0:T(128)} %bitcast.7, f32[2,384,768]{2,1,0:T(8,128)} %shard_map.64.ext_ref, f32[2,256,256]{2,1,0:T(8,128)} %probe_ref.3, f32[2,256,256]{2,1,0:T(8,128)} %bitcast.3, bf16[4,256,256]{2,1,0:T(8,128)(2,1)} %constant.2.clone.tables_ref), custom_call_target="tpu_custom_call" | custom-call | tf_op jit(solution)/shard_map/pallas_call | solution.py:252
  31.9 30.4 %shard_map.66 = (f32[2,128,512]{2,1,0:T(8,128)}, f32[128,512]{1,0:T(8,128)}) custom-call(f32[3,384,768]{2,1,0:T(8,128)} %shard_map.65.canvas_ref, f32[2,128,512]{2,1,0:T(8,128)} %cur_ref.3), custom_call_target="tpu_custom_call" | custom-call | tf_op jit(solution)/shard_map/pallas_call | solution.py:527
  62.4 17.6 %shard_map.67.ext_ref = f32[2,384,768]{2,1,0:T(8,128)} custom-call(f32[2,128,512]{2,1,0:T(8,128)} %get-tuple-element.8.cur_ref), custom_call_target="tpu_custom_call" | custom-call | tf_op jit(solution)/shard_map/pallas_call | solution.py:507
  79.9 7.8 %shard_map.68.canvas_ref = f32[2,384,768]{2,1,0:T(8,128)} custom-call(s32[2,2]{1,0:T(2,128)} %bitcast.6, s32[32]{0:T(128)} %bitcast.8, f32[2,384,768]{2,1,0:T(8,128)} %shard_map.67.ext_ref, f32[2,256,256]{2,1,0:T(8,128)} %probe_ref.3, f32[2,256,256]{2,1,0:T(8,128)} %bitcast.4, bf16[4,256,256]{2,1,0:T(8,128)(2,1)} %constant.2.clone.tables_ref), custom_call_target="tpu_custom_call" | custom-call | tf_op jit(solution)/shard_map/pallas_call | solution.py:252
  87.7 19.8 %shard_map.69 = (f32[2,128,512]{2,1,0:T(8,128)}, f32[128,512]{1,0:T(8,128)}) custom-call(f32[2,384,768]{2,1,0:T(8,128)} %shard_map.68.canvas_ref, f32[2,128,512]{2,1,0:T(8,128)} %get-tuple-element.8.cur_ref, f32[128,512]{1,0:T(8,128)} %get-tuple-element.9.refs_0_), custom_call_target="tpu_custom_call" | custom-call | tf_op jit(solution)/shard_map/pallas_call | solution.py:527
  107.5 1.9 %copy.8 = f32[2,128,512]{2,1,0:T(8,128)} copy(f32[2,128,512]{2,1,0:T(8,128)} %get-tuple-element.10) | data formatting | bytes 1048576

commit v21 on v15

--- a/solution.py
+++ b/solution.py
@@ -181,21 +181,29 @@
             take, put = window_tools(size, spots_ref[slot, 0], spots_ref[slot, 1])
             probe_real = probe_ref[0]
             probe_imag = probe_ref[1]
-            real_parts = (tables_ref[0], tables_ref[1])
-            imag_parts = (tables_ref[2], tables_ref[3])
+            real_high, real_low, imag_high, imag_low = (tables_ref[k] for k in range(4))
+            left_real = jnp.concatenate([real_high, real_high, real_low], axis=1)
+            left_imag = jnp.concatenate([imag_high, imag_high, imag_low], axis=1)
+            right_real = jnp.concatenate([real_high, real_low, real_high], axis=0)
+            right_imag = jnp.concatenate([imag_high, imag_low, imag_high], axis=0)
+
+            def product(left_side, right_side):
+                return jnp.dot(left_side, right_side, preferred_element_type=jnp.float32)
 
             def left(field_real, field_imag, sign):
-                both = split_bf16(jnp.concatenate([field_real, field_imag], axis=1))
-                by_real = dot_split(real_parts, both)
-                by_imag = dot_split(imag_parts, both)
+                high, low = split_bf16(jnp.concatenate([field_real, field_imag], axis=1))
+                both = jnp.concatenate([high, low, high], axis=0)
+                by_real = product(left_real, both)
+                by_imag = product(left_imag, both)
                 out_real = by_real[:, :size] - sign * by_imag[:, size:]
                 out_imag = by_real[:, size:] + sign * by_imag[:, :size]
                 return out_real, out_imag
 
             def right(field_real, field_imag, sign):
-                both = split_bf16(jnp.concatenate([field_real, field_imag], axis=0))
-                by_real = dot_split(both, real_parts)
-                by_imag = dot_split(both, imag_parts)
+                high, low = split_bf16(jnp.concatenate([field_real, field_imag], axis=0))
+                both = jnp.concatenate([high, high, low], axis=1)
+                by_real = product(both, right_real)
+                by_imag = product(both, right_imag)
                 out_real = by_real[:size] - sign * by_imag[size:]
                 out_imag = by_imag[:size] * sign + by_real[size:]
                 return out_real, out_imag

time: 110 us -> 110 us (level)
  no operation moved by 1% of the time
where the time goes in v21:
time: 110 us; the launch traced here: 109 us
  Pallas kernels  107 us (97%)
  local copies, waits for them, and re-layouts  1.87 us (2%)
    pallas_call x2, Pallas kernels, fold_and_step(): pl.pallas_call(fold_kernel, out_shape=(jax.ShapeDtypeStruct((fields, rows...  41.9 us
    pallas_call x2, Pallas kernels, exchange_halo(): pl.pallas_call(halo_kernel, out_shape=jax.ShapeDtypeStruct((depth, rows +...  41.3 us
    pallas_call x2, Pallas kernels, gradient_canvas(): pl.pallas_call(gradient_kernel, out_shape=jax.ShapeDtypeStruct((channels,...  24.1 us

profile of v21, /device:TPU:25, one launch (start us, length us, event | category | flops | bytes accessed | tf_op | source)
XLA Modules:
  0.0 109.2 jit_solution(188624713728775855)
XLA Ops:
  0.0 23.7 %shard_map.64.ext_ref = f32[2,384,768]{2,1,0:T(8,128)} custom-call(f32[2,128,512]{2,1,0:T(8,128)} %cur_ref.3), custom_call_target="tpu_custom_call" | custom-call | tf_op jit(solution)/shard_map/pallas_call | solution.py:514
  23.8 12.3 %shard_map.65.canvas_ref = f32[3,384,768]{2,1,0:T(8,128)} custom-call(s32[2,2]{1,0:T(2,128)} %bitcast.5, s32[32]{0:T(128)} %bitcast.7, f32[2,384,768]{2,1,0:T(8,128)} %shard_map.64.ext_ref, f32[2,256,256]{2,1,0:T(8,128)} %probe_ref.3, f32[2,256,256]{2,1,0:T(8,128)} %bitcast.3, bf16[4,256,256]{2,1,0:T(8,128)(2,1)} %constant.2.clone.tables_ref), custom_call_target="tpu_custom_call" | custom-call | tf_op jit(solution)/shard_map/pallas_call | solution.py:260
  36.1 26.4 %shard_map.66 = (f32[2,128,512]{2,1,0:T(8,128)}, f32[128,512]{1,0:T(8,128)}) custom-call(f32[3,384,768]{2,1,0:T(8,128)} %shard_map.65.canvas_ref, f32[2,128,512]{2,1,0:T(8,128)} %cur_ref.3), custom_call_target="tpu_custom_call" | custom-call | tf_op jit(solution)/shard_map/pallas_call | solution.py:534
  62.4 17.6 %shard_map.67.ext_ref = f32[2,384,768]{2,1,0:T(8,128)} custom-call(f32[2,128,512]{2,1,0:T(8,128)} %get-tuple-element.8.cur_ref), custom_call_target="tpu_custom_call" | custom-call | tf_op jit(solution)/shard_map/pallas_call | solution.py:514
  80.0 11.8 %shard_map.68.canvas_ref = f32[2,384,768]{2,1,0:T(8,128)} custom-call(s32[2,2]{1,0:T(2,128)} %bitcast.6, s32[32]{0:T(128)} %bitcast.8, f32[2,384,768]{2,1,0:T(8,128)} %shard_map.67.ext_ref, f32[2,256,256]{2,1,0:T(8,128)} %probe_ref.3, f32[2,256,256]{2,1,0:T(8,128)} %bitcast.4, bf16[4,256,256]{2,1,0:T(8,128)(2,1)} %constant.2.clone.tables_ref), custom_call_target="tpu_custom_call" | custom-call | tf_op jit(solution)/shard_map/pallas_call | solution.py:260
  91.8 15.5 %shard_map.69 = (f32[2,128,512]{2,1,0:T(8,128)}, f32[128,512]{1,0:T(8,128)}) custom-call(f32[2,384,768]{2,1,0:T(8,128)} %shard_map.68.canvas_ref, f32[2,128,512]{2,1,0:T(8,128)} %get-tuple-element.8.cur_ref, f32[128,512]{1,0:T(8,128)} %get-tuple-element.9.refs_0_), custom_call_target="tpu_custom_call" | custom-call | tf_op jit(solution)/shard_map/pallas_call | solution.py:534
  107.4 1.9 %copy.8 = f32[2,128,512]{2,1,0:T(8,128)} copy(f32[2,128,512]{2,1,0:T(8,128)} %get-tuple-element.10) | data formatting | bytes 1048576

commit v22 on v15

--- a/solution.py
+++ b/solution.py
@@ -349,7 +349,17 @@
     middle = slice(margin, margin + rows)
     own = pltpu.make_async_copy(cur_ref, ext_ref.at[:, middle, margin : margin + cols], local_sems.at[0])
     own.start()
-    zeros_ref[...] = jnp.zeros(zeros_ref.shape, jnp.float32)
+    edge_device = jnp.logical_not(
+        exists(me_r - 1, me_c, n_r, n_c)
+        & exists(me_r + 1, me_c, n_r, n_c)
+        & exists(me_r, me_c - 1, n_r, n_c)
+        & exists(me_r, me_c + 1, n_r, n_c)
+    )
+
+    @pl.when(edge_device)
+    def _():
+        zeros_ref[...] = jnp.zeros(zeros_ref.shape, jnp.float32)
+
     unreached = [
         ((0, 1), ext_ref.at[:, middle, 0:margin], zeros_ref.at[:, :, 0:margin]),
         ((0, -1), ext_ref.at[:, middle, margin + cols : ext_cols], zeros_ref.at[:, :, 0:margin]),
@@ -430,7 +440,6 @@
     place = mesh_place()
     me_r, me_c, n_r, n_c = place
     own_band = pltpu.make_async_copy(canvas_ref.at[:, margin : margin + rows, :], band_ref, band_sem)
-    own_band.start()
     neighbour_barrier(me_r, me_c, n_r, n_c)
     top = slice(0, margin)
     bottom = slice(margin + rows, 2 * margin + rows)
@@ -457,6 +466,7 @@
         send_sems.at[4:6],
         recv_sems.at[4:6],
     )
+    own_band.start()
     wait_copies(place, corners)
     own_band.wait()
     for slot, source_r in ((0, me_r + 1), (1, me_r - 1)):

time: 110 us -> 110 us (level)
    pallas_call x2, Pallas kernels: 24 us -> 16 us  [gradient_canvas(): pl.pallas_call(gradient_kernel, out_shape=jax.ShapeDtypeStruct((channels,...]
    pallas_call x2, Pallas kernels: 41.9 us -> 47.6 us  [fold_and_step(): pl.pallas_call(fold_kernel, out_shape=(jax.ShapeDtypeStruct((fields, rows...]
    pallas_call x2, Pallas kernels: 41.5 us -> 43.1 us  [exchange_halo(): pl.pallas_call(halo_kernel, out_shape=jax.ShapeDtypeStruct((depth, rows +...]
where the time goes in v22:
time: 110 us; the launch traced here: 109 us
  Pallas kernels  107 us (97%)
  local copies, waits for them, and re-layouts  1.87 us (2%)
    pallas_call x2, Pallas kernels, fold_and_step(): pl.pallas_call(fold_kernel, out_shape=(jax.ShapeDtypeStruct((fields, rows...  47.6 us
    pallas_call x2, Pallas kernels, exchange_halo(): pl.pallas_call(halo_kernel, out_shape=jax.ShapeDtypeStruct((depth, rows +...  43.1 us
    pallas_call x2, Pallas kernels, gradient_canvas(): pl.pallas_call(gradient_kernel, out_shape=jax.ShapeDtypeStruct((channels,...  16 us

profile of v22, /device:TPU:25, one launch (start us, length us, event | category | flops | bytes accessed | tf_op | source)
XLA Modules:
  0.0 108.6 jit_solution(6552688476509211080)
XLA Ops:
  0.0 23.8 %shard_map.64.ext_ref = f32[2,384,768]{2,1,0:T(8,128)} custom-call(f32[2,128,512]{2,1,0:T(8,128)} %cur_ref.3), custom_call_target="tpu_custom_call" | custom-call | tf_op jit(solution)/shard_map/pallas_call | solution.py:516
  23.8 8.2 %shard_map.65.canvas_ref = f32[3,384,768]{2,1,0:T(8,128)} custom-call(s32[2,2]{1,0:T(2,128)} %bitcast.5, s32[32]{0:T(128)} %bitcast.7, f32[2,384,768]{2,1,0:T(8,128)} %shard_map.64.ext_ref, f32[2,256,256]{2,1,0:T(8,128)} %probe_ref.3, f32[2,256,256]{2,1,0:T(8,128)} %bitcast.3, bf16[4,256,256]{2,1,0:T(8,128)(2,1)} %constant.2.clone.tables_ref), custom_call_target="tpu_custom_call" | custom-call | tf_op jit(solution)/shard_map/pallas_call | solution.py:252
  32.0 28.7 %shard_map.66 = (f32[2,128,512]{2,1,0:T(8,128)}, f32[128,512]{1,0:T(8,128)}) custom-call(f32[3,384,768]{2,1,0:T(8,128)} %shard_map.65.canvas_ref, f32[2,128,512]{2,1,0:T(8,128)} %cur_ref.3), custom_call_target="tpu_custom_call" | custom-call | tf_op jit(solution)/shard_map/pallas_call | solution.py:536
  60.7 19.3 %shard_map.67.ext_ref = f32[2,384,768]{2,1,0:T(8,128)} custom-call(f32[2,128,512]{2,1,0:T(8,128)} %get-tuple-element.8.cur_ref), custom_call_target="tpu_custom_call" | custom-call | tf_op jit(solution)/shard_map/pallas_call | solution.py:516
  80.0 7.8 %shard_map.68.canvas_ref = f32[2,384,768]{2,1,0:T(8,128)} custom-call(s32[2,2]{1,0:T(2,128)} %bitcast.6, s32[32]{0:T(128)} %bitcast.8, f32[2,384,768]{2,1,0:T(8,128)} %shard_map.67.ext_ref, f32[2,256,256]{2,1,0:T(8,128)} %probe_ref.3, f32[2,256,256]{2,1,0:T(8,128)} %bitcast.4, bf16[4,256,256]{2,1,0:T(8,128)(2,1)} %constant.2.clone.tables_ref), custom_call_target="tpu_custom_call" | custom-call | tf_op jit(solution)/shard_map/pallas_call | solution.py:252
  87.8 18.9 %shard_map.69 = (f32[2,128,512]{2,1,0:T(8,128)}, f32[128,512]{1,0:T(8,128)}) custom-call(f32[2,384,768]{2,1,0:T(8,128)} %shard_map.68.canvas_ref, f32[2,128,512]{2,1,0:T(8,128)} %get-tuple-element.8.cur_ref, f32[128,512]{1,0:T(8,128)} %get-tuple-element.9.refs_0_), custom_call_target="tpu_custom_call" | custom-call | tf_op jit(solution)/shard_map/pallas_call | solution.py:536
  106.7 1.9 %copy.8 = f32[2,128,512]{2,1,0:T(8,128)} copy(f32[2,128,512]{2,1,0:T(8,128)} %get-tuple-element.10) | data formatting | bytes 1048576

commit v23 on v15

--- a/solution.py
+++ b/solution.py
@@ -457,24 +457,19 @@
         send_sems.at[4:6],
         recv_sems.at[4:6],
     )
-    wait_copies(place, corners)
     own_band.wait()
-    for slot, source_r in ((0, me_r + 1), (1, me_r - 1)):
-
-        @pl.when(exists(source_r, me_c, n_r, n_c))
-        def _():
-            band_ref[:, :, left] += corner_bufs[slot, 0]
-            band_ref[:, :, right] += corner_bufs[slot, 1]
-
-    strips = start_copies(
-        place,
-        [
-            ((0, -1), band_ref.at[:, :, left], col_bufs.at[0]),
-            ((0, 1), band_ref.at[:, :, right], col_bufs.at[1]),
-        ],
-        send_sems.at[6:8],
-        recv_sems.at[6:8],
-    )
+    strips = []
+    for side, columns, (dr, dc), buffer in ((0, left, (0, -1), col_bufs.at[0]), (1, right, (0, 1), col_bufs.at[1])):
+        wait_copies(place, [corners[side], corners[side + 2]])
+        for slot, source_r in ((0, me_r + 1), (1, me_r - 1)):
+
+            @pl.when(exists(source_r, me_c, n_r, n_c))
+            def _():
+                band_ref[:, :, columns] += corner_bufs[slot, side]
+
+        strips += start_copies(
+            place, [((dr, dc), band_ref.at[:, :, columns], buffer)], send_sems.at[6 + side : 7 + side], recv_sems.at[6 + side : 7 + side]
+        )
     wait_copies(place, mids)
     total_ref[...] = band_ref[:, :, inner]
     for slot, source_r in ((0, me_r + 1), (1, me_r - 1)):

time: 110 us -> 110 us (level)
  no operation moved by 1% of the time
where the time goes in v23:
time: 110 us; the launch traced here: 109 us
  Pallas kernels  107 us (97%)
  local copies, waits for them, and re-layouts  1.87 us (2%)
    pallas_call x2, Pallas kernels, fold_and_step(): pl.pallas_call(fold_kernel, out_shape=(jax.ShapeDtypeStruct((fields, rows...  42.1 us
    pallas_call x2, Pallas kernels, exchange_halo(): pl.pallas_call(halo_kernel, out_shape=jax.ShapeDtypeStruct((depth, rows +...  41.3 us
    pallas_call x2, Pallas kernels, gradient_canvas(): pl.pallas_call(gradient_kernel, out_shape=jax.ShapeDtypeStruct((channels,...  24 us

profile of v23, /device:TPU:25, one launch (start us, length us, event | category | flops | bytes accessed | tf_op | source)
XLA Modules:
  0.0 109.3 jit_solution(17854474989413392668)
XLA Ops:
  0.0 23.7 %shard_map.64.ext_ref = f32[2,384,768]{2,1,0:T(8,128)} custom-call(f32[2,128,512]{2,1,0:T(8,128)} %cur_ref.3), custom_call_target="tpu_custom_call" | custom-call | tf_op jit(solution)/shard_map/pallas_call | solution.py:501
  23.8 12.2 %shard_map.65.canvas_ref = f32[3,384,768]{2,1,0:T(8,128)} custom-call(s32[2,2]{1,0:T(2,128)} %bitcast.5, s32[32]{0:T(128)} %bitcast.7, f32[2,384,768]{2,1,0:T(8,128)} %shard_map.64.ext_ref, f32[2,256,256]{2,1,0:T(8,128)} %probe_ref.3, f32[2,256,256]{2,1,0:T(8,128)} %bitcast.3, bf16[4,256,256]{2,1,0:T(8,128)(2,1)} %constant.2.clone.tables_ref), custom_call_target="tpu_custom_call" | custom-call | tf_op jit(solution)/shard_map/pallas_call | solution.py:252
  36.0 26.0 %shard_map.66 = (f32[2,128,512]{2,1,0:T(8,128)}, f32[128,512]{1,0:T(8,128)}) custom-call(f32[3,384,768]{2,1,0:T(8,128)} %shard_map.65.canvas_ref, f32[2,128,512]{2,1,0:T(8,128)} %cur_ref.3), custom_call_target="tpu_custom_call" | custom-call | tf_op jit(solution)/shard_map/pallas_call | solution.py:521
  62.0 17.5 %shard_map.67.ext_ref = f32[2,384,768]{2,1,0:T(8,128)} custom-call(f32[2,128,512]{2,1,0:T(8,128)} %get-tuple-element.8.cur_ref), custom_call_target="tpu_custom_call" | custom-call | tf_op jit(solution)/shard_map/pallas_call | solution.py:501
  79.5 11.8 %shard_map.68.canvas_ref = f32[2,384,768]{2,1,0:T(8,128)} custom-call(s32[2,2]{1,0:T(2,128)} %bitcast.6, s32[32]{0:T(128)} %bitcast.8, f32[2,384,768]{2,1,0:T(8,128)} %shard_map.67.ext_ref, f32[2,256,256]{2,1,0:T(8,128)} %probe_ref.3, f32[2,256,256]{2,1,0:T(8,128)} %bitcast.4, bf16[4,256,256]{2,1,0:T(8,128)(2,1)} %constant.2.clone.tables_ref), custom_call_target="tpu_custom_call" | custom-call | tf_op jit(solution)/shard_map/pallas_call | solution.py:252
  91.3 16.1 %shard_map.69 = (f32[2,128,512]{2,1,0:T(8,128)}, f32[128,512]{1,0:T(8,128)}) custom-call(f32[2,384,768]{2,1,0:T(8,128)} %shard_map.68.canvas_ref, f32[2,128,512]{2,1,0:T(8,128)} %get-tuple-element.8.cur_ref, f32[128,512]{1,0:T(8,128)} %get-tuple-element.9.refs_0_), custom_call_target="tpu_custom_call" | custom-call | tf_op jit(solution)/shard_map/pallas_call | solution.py:521
  107.4 1.9 %copy.8 = f32[2,128,512]{2,1,0:T(8,128)} copy(f32[2,128,512]{2,1,0:T(8,128)} %get-tuple-element.10) | data formatting | bytes 1048576

commit v24 on v15

--- a/solution.py
+++ b/solution.py
@@ -1,3 +1,4 @@
+import functools
 import math
 
 import jax
@@ -414,12 +415,12 @@
     wait_copies(place, corners)
 
 
-def fold_kernel(canvas_ref, cur_ref, *refs):
-    if len(refs) == 10:
-        light_in_ref, refs = None, refs
+def fold_kernel(light_given, canvas_ref, cur_ref, *refs):
+    if light_given:
+        light_in_ref, out_ref, refs = refs[0], refs[1], refs[2:]
+        fold_body(canvas_ref, cur_ref, light_in_ref, out_ref, None, *refs)
     else:
-        light_in_ref, refs = refs[0], refs[1:]
-    fold_body(canvas_ref, cur_ref, light_in_ref, *refs)
+        fold_body(canvas_ref, cur_ref, None, *refs)
 
 
 def fold_body(canvas_ref, cur_ref, light_in_ref, out_ref, light_ref, mid_bufs, corner_bufs, col_bufs, band_ref, total_ref, send_sems, recv_sems, band_sem):
@@ -494,11 +495,12 @@
         total_ref[:, :, 0:margin] += col_bufs[1]
 
     fields = cur_ref.shape[0]
-    if total_ref.shape[0] > fields:
+    if light_in_ref is None:
         light_ref[...] = total_ref[fields]
+        light = light_ref[...]
     else:
-        light_ref[...] = light_in_ref[...]
-    out_ref[...] = cur_ref[...] - total_ref[0:fields] / (light_ref[...] + DAMPING)
+        light = light_in_ref[...]
+    out_ref[...] = cur_ref[...] - total_ref[0:fields] / (light + DAMPING)
 
 
 def exchange_halo(current, margin):
@@ -523,14 +525,12 @@
 def fold_and_step(canvas, current, light, margin):
     depth, ext_rows, ext_cols = canvas.shape
     fields, rows, cols = current.shape
-    return pl.pallas_call(
-        fold_kernel,
-        out_shape=(
-            jax.ShapeDtypeStruct((fields, rows, cols), jnp.float32),
-            jax.ShapeDtypeStruct((rows, cols), jnp.float32),
-        ),
+    results = pl.pallas_call(
+        functools.partial(fold_kernel, light is not None),
+        out_shape=(jax.ShapeDtypeStruct((fields, rows, cols), jnp.float32),)
+        + (() if light is not None else (jax.ShapeDtypeStruct((rows, cols), jnp.float32),)),
         in_specs=[pl.BlockSpec(memory_space=pl.ANY), VMEM_SPEC] + ([] if light is None else [VMEM_SPEC]),
-        out_specs=(VMEM_SPEC, VMEM_SPEC),
+        out_specs=(VMEM_SPEC,) + (() if light is not None else (VMEM_SPEC,)),
         scratch_shapes=[
             pltpu.VMEM((2, depth, margin, cols), jnp.float32),
             pltpu.VMEM((2, 2, depth, margin, margin), jnp.float32),
@@ -545,6 +545,7 @@
             vmem_limit_bytes=60 * 1024 * 1024, has_side_effects=True, collective_id=depth
         ),
     )(canvas, current, *([] if light is None else [light]))
+    return (results[0], light) if light is not None else tuple(results)
 
 
 def on_device(object_field, probe_field, amplitudes, centres, counts):

time: 110 us -> 110 us (level)
  no operation moved by 1% of the time
where the time goes in v24:
time: 110 us; the launch traced here: 109 us
  Pallas kernels  107 us (97%)
  local copies, waits for them, and re-layouts  1.87 us (2%)
    pallas_call x2, Pallas kernels, fold_and_step(): pl.pallas_call(functools.partial(fold_kernel, light is not None), out_sha...  42.2 us
    pallas_call x2, Pallas kernels, exchange_halo(): pl.pallas_call(halo_kernel, out_shape=jax.ShapeDtypeStruct((depth, rows +...  41.3 us
    pallas_call x2, Pallas kernels, gradient_canvas(): pl.pallas_call(gradient_kernel, out_shape=jax.ShapeDtypeStruct((channels,...  24 us

profile of v24, /device:TPU:25, one launch (start us, length us, event | category | flops | bytes accessed | tf_op | source)
XLA Modules:
  0.0 109.4 jit_solution(2712527962978598288)
XLA Ops:
  0.0 23.7 %shard_map.64.ext_ref = f32[2,384,768]{2,1,0:T(8,128)} custom-call(f32[2,128,512]{2,1,0:T(8,128)} %cur_ref.3), custom_call_target="tpu_custom_call" | custom-call | tf_op jit(solution)/shard_map/pallas_call | solution.py:508
  23.8 12.2 %shard_map.65.canvas_ref = f32[3,384,768]{2,1,0:T(8,128)} custom-call(s32[2,2]{1,0:T(2,128)} %bitcast.5, s32[32]{0:T(128)} %bitcast.7, f32[2,384,768]{2,1,0:T(8,128)} %shard_map.64.ext_ref, f32[2,256,256]{2,1,0:T(8,128)} %probe_ref.3, f32[2,256,256]{2,1,0:T(8,128)} %bitcast.3, bf16[4,256,256]{2,1,0:T(8,128)(2,1)} %constant.2.clone.tables_ref), custom_call_target="tpu_custom_call" | custom-call | tf_op jit(solution)/shard_map/pallas_call | solution.py:253
  36.0 26.4 %shard_map.66 = (f32[2,128,512]{2,1,0:T(8,128)}, f32[128,512]{1,0:T(8,128)}) custom-call(f32[3,384,768]{2,1,0:T(8,128)} %shard_map.65.canvas_ref, f32[2,128,512]{2,1,0:T(8,128)} %cur_ref.3), custom_call_target="tpu_custom_call" | custom-call | tf_op jit(solution)/shard_map/pallas_call | solution.py:528
  62.4 17.6 %shard_map.67.ext_ref = f32[2,384,768]{2,1,0:T(8,128)} custom-call(f32[2,128,512]{2,1,0:T(8,128)} %get-tuple-element.7.cur_ref), custom_call_target="tpu_custom_call" | custom-call | tf_op jit(solution)/shard_map/pallas_call | solution.py:508
  80.0 11.7 %shard_map.68.canvas_ref = f32[2,384,768]{2,1,0:T(8,128)} custom-call(s32[2,2]{1,0:T(2,128)} %bitcast.6, s32[32]{0:T(128)} %bitcast.8, f32[2,384,768]{2,1,0:T(8,128)} %shard_map.67.ext_ref, f32[2,256,256]{2,1,0:T(8,128)} %probe_ref.3, f32[2,256,256]{2,1,0:T(8,128)} %bitcast.4, bf16[4,256,256]{2,1,0:T(8,128)(2,1)} %constant.2.clone.tables_ref), custom_call_target="tpu_custom_call" | custom-call | tf_op jit(solution)/shard_map/pallas_call | solution.py:253
  91.7 15.8 %shard_map.69 = f32[2,128,512]{2,1,0:T(8,128)} custom-call(f32[2,384,768]{2,1,0:T(8,128)} %shard_map.68.canvas_ref, f32[2,128,512]{2,1,0:T(8,128)} %get-tuple-element.7.cur_ref, f32[128,512]{1,0:T(8,128)} %get-tuple-element.8.refs_0_), custom_call_target="tpu_custom_call" | custom-call | tf_op jit(solution)/shard_map/pallas_call | solution.py:528
  107.5 1.9 %copy.8 = f32[2,128,512]{2,1,0:T(8,128)} copy(f32[2,128,512]{2,1,0:T(8,128)} %shard_map.69) | data formatting | bytes 1048576
